TPU v7x, 32 devices: a whole 2x2x4 slice. The times are simulated.
32 devices in a mesh: gx: 4 (over y, x), gy: 2 (over core), gz: 4 (over z).
Axes of the slice: x: 2, y: 2, z: 4, core: 2. Of those that a mesh axis runs over, the one named last changes fastest.
Arguments:
- field: bfloat16 [16, 64, 32, 512], P(None, 'gz', 'gy', 'gx'), may hold values from -6 to 6
- fine_taps: float32 [3, 9], replicated, may hold values from 0.1 to 0.6
- coarse_taps: float32 [3, 9], replicated, may hold values from 0.1 to 0.6
- top_kernel: bfloat16 [8, 4, 64, 2048], P('gz', 'gy', 'gx'), may hold values from -6 to 6
Outputs:
- applied: bfloat16 [16, 64, 32, 512], P(None, 'gz', 'gy', 'gx')
All inputs are finite; a program needn't handle non-finite values.
Results may differ from a plain program's by a relative error of at most 0.0047.
Values may be sent and summed in bfloat16 or wider, within the bound.
No kernel may reach another device: no remote copies, remote signals or barrier semaphores. Data moves between devices by JAX's collectives and lax.ppermute only.
A program may use at most 128 MiB of HBM per device.

v0:
```python
import jax
import jax.numpy as jnp
from jax import lax
from jax.sharding import PartitionSpec as P


def padded_2(cells, sides, width):
    for axis, dim in sides:
        count = lax.axis_size(axis)
        ends = count - 1
        head = lax.slice_in_dim(cells, 0, width, axis=dim)
        tail = lax.slice_in_dim(cells, cells.shape[dim] - width, cells.shape[dim], axis=dim)
        cells = jnp.concatenate(
            [
                lax.ppermute(tail, axis, [(i, (i + 1) % count) for i in range(ends)]),
                cells,
                lax.ppermute(head, axis, [((i + 1) % count, i) for i in range(ends)]),
            ],
            axis=dim,
        )
    return cells


def band_matrix(kernel_row, padded_length):
    length = padded_length - 8
    source = lax.broadcasted_iota(jnp.int32, (padded_length, length), 0)
    target = lax.broadcasted_iota(jnp.int32, (padded_length, length), 1)
    offset = source - target
    band = jnp.zeros((padded_length, length), jnp.float32)
    for tap in range(9):
        band = band + jnp.where(offset == tap, kernel_row[tap], 0.0)
    return band


def conv_padded(padded, kernel_row, along):
    length = padded.shape[along] - 8
    if along == padded.ndim - 1:
        band = band_matrix(kernel_row, padded.shape[along])
        return lax.dot_general(
            padded,
            band,
            (((along,), (0,)), ((), ())),
            precision=lax.Precision.HIGHEST,
            preferred_element_type=jnp.float32,
        )
    total = kernel_row[0] * lax.slice_in_dim(padded, 0, length, axis=along)
    for offset in range(1, 9):
        total = total + kernel_row[offset] * lax.slice_in_dim(
            padded, offset, offset + length, axis=along
        )
    return total


def separable_steps(values, kernel, rim_x, rim_y, rim_z):
    values = conv_padded(rim_x(values).astype(jnp.float32), kernel[2], 3)
    values = conv_padded(rim_y(values), kernel[1], 2)
    return conv_padded(rim_z(values), kernel[0], 1)


def restrict(values, factor):
    count, depth, rows, cols = values.shape
    shaped = values.reshape(
        count, depth // factor, factor, rows // factor, factor, cols // factor, factor
    )
    return shaped.mean(axis=(2, 4, 6))


def prolong(values, factor):
    values = jnp.repeat(values, factor, axis=1)
    values = jnp.repeat(values, factor, axis=2)
    return jnp.repeat(values, factor, axis=3)


def shards(field, fine_taps, coarse_taps, top_kernel):
    cells = field.astype(jnp.float32)
    coarse_cells = restrict(cells, 2)
    fine_part = separable_steps(
        field,
        fine_taps,
        lambda values: padded_2(values, (("gx", 3),), 4),
        lambda values: padded_2(values, (("gy", 2),), 4),
        lambda values: padded_2(values, (("gz", 1),), 4),
    )
    coarse_part = separable_steps(
        coarse_cells,
        coarse_taps,
        lambda values: padded_2(values.astype(jnp.bfloat16), (("gx", 3),), 4).astype(values.dtype),
        lambda values: padded_2(values.astype(jnp.bfloat16), (("gy", 2),), 4).astype(values.dtype),
        lambda values: padded_2(values.astype(jnp.bfloat16), (("gz", 1),), 4).astype(values.dtype),
    )
    top_in = restrict(coarse_cells, 4).astype(jnp.bfloat16)
    count, top_depth, top_rows, top_cols = top_in.shape
    along_x = lax.all_gather(top_in, "gx", axis=3, tiled=True)
    along_y = lax.all_gather(along_x, "gy", axis=2, tiled=True)
    along_z = lax.all_gather(along_y, "gz", axis=1, tiled=True)
    whole_top = along_z.reshape(count, -1)
    kernel_rows = top_kernel.reshape(-1, top_kernel.shape[3])
    top_part = lax.dot_general(
        whole_top, kernel_rows, (((1,), (1,)), ((), ())), preferred_element_type=jnp.float32
    )
    top_part = top_part.reshape(count, top_depth, top_rows, top_cols)
    coarse_total = coarse_part + prolong(top_part, 4)
    return (fine_part + prolong(coarse_total, 2)).astype(jnp.bfloat16)


def solution(mesh):
    return jax.shard_map(
        shards,
        mesh=mesh,
        in_specs=(P(None, "gz", "gy", "gx"), P(), P(), P("gz", "gy", "gx", None)),
        out_specs=P(None, "gz", "gy", "gx"),
        check_vma=False,
    )
```

profile of v0, /device:TPU:0, one launch (start us, length us, event | category | flops | bytes accessed | tf_op | source)
XLA Modules:
  0.0 185.4 jit_solution(7652606793168775549)
XLA Ops:
  0.0 9.9 %copy.23 = f32[16,16,16,128]{0,3,2,1:T(8,128)} copy(bf16[16,16,16,128]{3,2,1,0:T(8,128)(2,1)} %param.4) | data formatting | bytes 3145728 | tf_op jit(solution)/shard_map/reshape | solution.py:62
  9.9 11.7 %reduce_sum.18 = f32[16,8,8,64]{0,3,2,1:T(8,128)S(1)} reduce(f32[16,8,2,8,2,64,2]{0,6,5,4,3,2,1:T(2,128)} %bitcast.77, f32[]{:T(128)} %constant.13.clone.1), dimensions={2,4,6}, to_apply=%region_0.0 | reduce | flops 458752 | bytes 2359300 | tf_op jit(solution)/shard_map/reduce_sum | solution.py:65
  21.7 1.4 copy.24
  23.1 1.9 %fusion.209 = (bf16[16,8,8,64]{3,0,2,1:T(8,128)(2,1)S(1)}, f32[16,8,8,64]{3,0,2,1:T(8,128)}) fusion(f32[16,8,8,64]{3,0,2,1:T(8,128)} %copy.24), kind=kLoop, calls=%fused_computation.244 | loop fusion | flops 131072 | bytes 655360 | tf_op jit(solution)/shard_map/convert_element_type | solution.py:87
  25.0 0.7 copy-done.3
  25.7 0.9 fusion.215
  26.6 5.6 %collective-permute-start.6 = (bf16[16,8,8,4]{3,0,2,1:T(8,128)(2,1)}, bf16[16,8,8,4]{3,0,2,1:T(8,128)(2,1)}, u32[]{:S(2)}, u32[]{:S(2)}) collective-permute-start(bf16[16,8,8,4]{3,0,2,1:T(8,128)(2,1)} %get-tuple-element.17), channel_id=1, source_target_pairs={{0,8},{8,16},{16,24},{1,9},{9,17},{17,25},{2,10},{10,18},{18,26},{... | collective-permute-start | bytes 24584 | tf_op jit(solution)/shard_map/ppermute | solution.py:15
  32.1 1.3 collective-permute-start.7
  33.4 0.6 fusion.212
  34.0 2.5 %copy.37 = bf16[16,16,16,4]{2,1,3,0:T(8,128)(2,1)} copy(bf16[16,16,16,4]{3,2,1,0:T(8,128)(2,1)S(1)} %get-tuple-element.9) | data formatting | bytes 65536
  36.5 5.2 %collective-permute-start = (bf16[16,16,16,4]{2,1,3,0:T(8,128)(2,1)}, bf16[16,16,16,4]{2,1,3,0:T(8,128)(2,1)}, u32[]{:S(2)}, u32[]{:S(2)}) collective-permute-start(bf16[16,16,16,4]{2,1,3,0:T(8,128)(2,1)} %copy.37), channel_id=1, source_target_pairs={{0,8},{8,16},{16,24},{1,9},{9,17},{17,25},{2,10},{10,18},{18,26},{... | collective-permute-start | bytes 98312 | tf_op jit(solution)/shard_map/ppermute | solution.py:15
  41.7 2.5 %copy.38 = bf16[16,16,16,4]{2,1,3,0:T(8,128)(2,1)} copy(bf16[16,16,16,4]{3,2,1,0:T(8,128)(2,1)S(1)} %get-tuple-element.10) | data formatting | bytes 65536
  44.2 1.3 collective-permute-start.1
  45.5 0.7 fusion.218
  46.2 0.7 fusion.219
  46.9 0.7 fusion.216
  47.6 0.7 fusion.217
  48.3 1.7 copy.25
  49.9 0.5 reduce_sum.19
  50.5 9.9 %all_gather.9 = bf16[16,2,2,64]{0,2,1,3:T(2,128)(2,1)S(1)} all-gather(bf16[16,2,2,16]{0,2,1,3:T(2,128)(2,1)S(1)} %copy.26), channel_id=1, replica_groups=mesh['gx'=4,'gy'=2,'gz'=4] {'gx'}, dimensions={3}, use_global_device_ids=true | all-gather | bytes 10240 | tf_op jit(solution)/shard_map/all_gather | solution.py:93
  60.5 1.8 all_gather.10
  62.3 13.6 %all_gather.11 = bf16[16,8,4,64]{3,0,1,2:T(8,128)(2,1)S(1)} all-gather(bf16[16,2,4,64]{3,0,1,2:T(8,128)(2,1)S(1)} %all_gather.10), channel_id=1, replica_groups=mesh['gx'=4,'gy'=2,'gz'=4] {'gz'}, dimensions={1}, use_global_device_ids=true | all-gather | bytes 81920 | tf_op jit(solution)/shard_map/all_gather | solution.py:95
  76.2 7.2 %convolution_convert_fusion = bf16[16,8,8,64]{3,0,2,1:T(8,128)(2,1)S(1)} fusion(bf16[16,8,8,4]{3,0,2,1:T(8,128)(2,1)} %collective-permute-done.7, bf16[16,8,8,64]{3,0,2,1:T(8,128)(2,1)} %copy-done.3, bf16[16,8,8,4]{3,0,2,1:T(8,128)(2,1)} %collective-permute-done.6, f32[]{:T(128)} %bitcast.40, f32[]{:T(128)} %bitcast.39, f32[]{:T(128)} %bitcast.38, ...), kind=kOutput, calls=%fused_computation.80 | convolution fusion | flops 57255424 | bytes 278564 | tf_op jit(solution)/shard_map/dot_general | solution.py:39
  83.4 1.3 collective-permute-start.8
  84.7 1.3 collective-permute-start.9
  86.0 2.5 %copy.21 = bf16[16,16,16,4]{3,2,1,0:T(8,128)(2,1)S(1)} copy(bf16[16,16,16,4]{2,1,3,0:T(8,128)(2,1)} %collective-permute-done) | data formatting | bytes 65536 | tf_op jit(solution)/shard_map/ppermute | solution.py:15
  88.6 3.5 %copy.22 = bf16[16,16,16,4]{3,2,1,0:T(8,128)(2,1)} copy(bf16[16,16,16,4]{2,1,3,0:T(8,128)(2,1)} %collective-permute-done.1) | data formatting | bytes 65536 | tf_op jit(solution)/shard_map/ppermute | solution.py:17
  92.0 9.0 %fusion.46 = f32[16,16,16,128]{3,2,1,0:T(8,128)S(1)} fusion(bf16[16,16,16,4]{3,2,1,0:T(8,128)(2,1)} %copy.22, bf16[16,16,16,128]{3,2,1,0:T(8,128)(2,1)S(1)} %copy-done.2, bf16[16,16,16,4]{3,2,1,0:T(8,128)(2,1)S(1)} %copy.21, f32[]{:T(128)} %bitcast.10, f32[]{:T(128)} %bitcast.9, f32[]{:T(128)} %bitcast.8, f32[]{:T(128)} %bitcast.7, f32[]{:T(128)} %bitcast.6, ...), kind=kOutput, calls=%fused_computation.74 | convolution fusion | flops 859450368 | bytes 3211300 | tf_op jit(solution)/shard_map/dot_general | solution.py:39
  101.3 3.1 %collective-permute-start.2 = (f32[16,16,4,128]{3,2,1,0:T(4,128)S(1)}, f32[16,16,4,128]{3,2,1,0:T(4,128)S(1)}, u32[]{:S(2)}, u32[]{:S(2)}) collective-permute-start(f32[16,16,4,128]{3,2,1,0:T(4,128)S(1)} %get-tuple-element.7), channel_id=1, source_target_pairs={{0,4},{1,5},{2,6},{3,7},{8,12},{9,13},{10,14},{11,15},{16,20},{17,... | collective-permute-start | bytes 1572872 | tf_op jit(solution)/shard_map/ppermute | solution.py:15
  104.3 1.5 collective-permute-start.3
  106.0 5.7 %fusion.62 = bf16[16,8,8,64]{3,0,2,1:T(8,128)(2,1)S(1)} fusion(f32[16,8,16,64]{3,0,2,1:T(8,128)S(1)} %maximum_convert_fusion, f32[]{:T(128)} %bitcast.50, f32[]{:T(128)} %bitcast.49, f32[]{:T(128)} %bitcast.48, f32[]{:T(128)} %bitcast.47, f32[]{:T(128)} %bitcast.46, f32[]{:T(128)} %bitcast.45, f32[]{:T(128)} %bitcast.44, f32[]{:T(128)} %bitcast.43, f32[]{:T(128)} %bitcast.30), kind=kLoop, calls=%fused_computation.101 | loop fusion | flops 1179648 | bytes 2490404 | tf_op jit(solution)/shard_map/convert_element_type | solution.py:89
  111.7 0.7 fusion.213
  112.4 3.5 %collective-permute-start.10 = (bf16[16,4,8,64]{3,0,2,1:T(8,128)(2,1)}, bf16[16,4,8,64]{3,0,2,1:T(8,128)(2,1)S(1)}, u32[]{:S(2)}, u32[]{:S(2)}) collective-permute-start(bf16[16,4,8,64]{3,0,2,1:T(8,128)(2,1)} %get-tuple-element.13), channel_id=1, source_target_pairs={{0,1},{1,2},{2,3},{4,5},{5,6},{6,7},{8,9},{9,10},{10,11},{12,13},{... | collective-permute-start | bytes 196616 | tf_op jit(solution)/shard_map/ppermute | solution.py:15
  115.9 1.3 collective-permute-start.11
  117.3 8.9 %fusion.25 = f32[16,16,16,128]{3,2,1,0:T(8,128)S(1)} fusion(f32[16,16,16,128]{3,2,1,0:T(8,128)S(1)} %fusion.46, f32[16,16,4,128]{3,2,1,0:T(4,128)S(1)} %collective-permute-done.3, f32[16,16,4,128]{3,2,1,0:T(4,128)S(1)} %collective-permute-done.2, f32[]{:T(128)} %bitcast.20, f32[]{:T(128)} %bitcast.19, f32[]{:T(128)} %bitcast.18, f32[]{:T(128)} %bitcast.17, ...), kind=kLoop, calls=%fused_computation.49 | loop fusion | flops 13107200 | bytes 5242916 | tf_op jit(solution)/shard_map/add | solution.py:48
  126.2 1.0 fusion.210
  127.2 5.3 %collective-permute-start.4 = (f32[16,4,16,128]{3,2,1,0:T(8,128)}, f32[16,4,16,128]{3,2,1,0:T(8,128)}, u32[]{:S(2)}, u32[]{:S(2)}) collective-permute-start(f32[16,4,16,128]{3,2,1,0:T(8,128)} %get-tuple-element.5), channel_id=1, source_target_pairs={{0,1},{1,2},{2,3},{4,5},{5,6},{6,7},{8,9},{9,10},{10,11},{12,13},{... | collective-permute-start | bytes 1572872 | tf_op jit(solution)/shard_map/ppermute | solution.py:15
  132.6 1.3 collective-permute-start.5
  133.9 0.4 fusion.111
  134.5 1.5 broadcast_in_dim.120
  136.0 2.2 %copy.30 = f32[16,8,8,64]{3,0,2,1:T(8,128)S(1)} copy(f32[16,8,8,64]{0,2,3,1:T(8,128)} %bitcast.79) | data formatting | bytes 524288 | tf_op jit(solution)/shard_map/reshape | solution.py:71
  138.4 5.9 %fusion.53 = f32[16,8,8,64]{3,0,2,1:T(8,128)S(1)} fusion(f32[16,8,8,64]{3,0,2,1:T(8,128)S(1)} %copy.30, f32[16,16,8,64]{3,0,2,1:T(8,128)S(1)} %maximum_convert_fusion.1, f32[]{:T(128)} %bitcast.58, f32[]{:T(128)} %bitcast.57, f32[]{:T(128)} %bitcast.56, f32[]{:T(128)} %bitcast.55, f32[]{:T(128)} %bitcast.54, f32[]{:T(128)} %bitcast.53, f32[]{:T(128)} %bitcast.52, ...), kind=kLoop, calls=%fused_computation.83 | loop fusion | flops 1179648 | bytes 2883620 | tf_op jit(solution)/shard_map/add | solution.py:102
  144.5 0.4 broadcast_in_dim.121
  144.9 1.5 broadcast_in_dim.122
  146.4 6.7 %copy.32 = f32[16,16,16,64]{2,1,3,0:T(8,128)} copy(f32[16,16,16,64]{3,1,2,0:T(8,128)} %bitcast.80) | data formatting | bytes 2097152 | tf_op jit(solution)/shard_map/reshape | solution.py:70
  153.1 10.7 %broadcast_in_dim.123 = f32[16,16,16,64,2]{2,1,4,3,0:T(8,128)} broadcast(f32[16,16,16,64]{2,1,3,0:T(8,128)} %copy.32), dimensions={0,1,2,3} | broadcast | bytes 3145728 | tf_op jit(solution)/shard_map/broadcast_in_dim | solution.py:71
  163.8 11.4 %copy.33 = f32[16,16,16,128]{3,2,1,0:T(8,128)} copy(f32[16,16,16,128]{2,1,3,0:T(8,128)} %bitcast.76) | data formatting | bytes 4194304 | tf_op jit(solution)/shard_map/reshape | solution.py:71
  175.2 10.1 %fusion.5 = bf16[16,16,16,128]{3,2,1,0:T(8,128)(2,1)} fusion(f32[16,16,16,128]{3,2,1,0:T(8,128)} %copy.33, f32[16,16,16,128]{3,2,1,0:T(8,128)S(1)} %fusion.25, f32[16,4,16,128]{3,2,1,0:T(8,128)} %collective-permute-done.5, f32[16,4,16,128]{3,2,1,0:T(8,128)} %collective-permute-done.4, f32[]{:T(128)} %bitcast.28, f32[]{:T(128)} %bitcast.27, f32[]{:T(128)} %bitcast.26, ...), kind=kLoop, calls=%fused_computation.29 | loop fusion | flops 14155776 | bytes 6291492 | tf_op jit(solution)/shard_map/convert_element_type | solution.py:103
  (36 shorter events, 1.5 us)
Async XLA Ops:
  0.0 133.9 %copy-start = (bf16[2,2,16,2048]{3,2,1,0:T(8,128)(2,1)S(1)}, bf16[2,2,16,2048]{3,2,1,0:T(8,128)(2,1)}, u32[]{:S(2)}) copy-start(bf16[2,2,16,2048]{3,2,1,0:T(8,128)(2,1)} %param.7) | copy-start | bytes 786436
  21.7 11.8 %copy-start.2 = (bf16[16,16,16,128]{3,2,1,0:T(8,128)(2,1)S(1)}, bf16[16,16,16,128]{3,2,1,0:T(8,128)(2,1)}, u32[]{:S(2)}) copy-start(bf16[16,16,16,128]{3,2,1,0:T(8,128)(2,1)} %param.4) | copy-start | bytes 3145732
  25.0 0.7 copy-start.3
  26.6 49.6 %collective-permute-start.6 = (bf16[16,8,8,4]{3,0,2,1:T(8,128)(2,1)}, bf16[16,8,8,4]{3,0,2,1:T(8,128)(2,1)}, u32[]{:S(2)}, u32[]{:S(2)}) collective-permute-start(bf16[16,8,8,4]{3,0,2,1:T(8,128)(2,1)} %get-tuple-element.17), channel_id=1, source_target_pairs={{0,8},{8,16},{16,24},{1,9},{9,17},{17,25},{2,10},{10,18},{18,26},{... | collective-permute-start | bytes 24584 | tf_op jit(solution)/shard_map/ppermute | solution.py:15
  32.1 44.1 %collective-permute-start.7 = (bf16[16,8,8,4]{3,0,2,1:T(8,128)(2,1)}, bf16[16,8,8,4]{3,0,2,1:T(8,128)(2,1)}, u32[]{:S(2)}, u32[]{:S(2)}) collective-permute-start(bf16[16,8,8,4]{3,0,2,1:T(8,128)(2,1)} %get-tuple-element.18), channel_id=1, source_target_pairs={{8,0},{16,8},{24,16},{9,1},{17,9},{25,17},{10,2},{18,10},{26,18},{... | collective-permute-start | bytes 24584 | tf_op jit(solution)/shard_map/ppermute | solution.py:17
  34.0 11.5 %copy-start.4 = (f32[3,9]{1,0:T(4,128)S(1)}, f32[3,9]{1,0:T(4,128)}, u32[]{:S(2)}) copy-start(f32[3,9]{1,0:T(4,128)} %param.6) | copy-start | bytes 328
  34.0 12.9 %copy-start.5 = (f32[3,9]{1,0:T(4,128)S(1)}, f32[3,9]{1,0:T(4,128)}, u32[]{:S(2)}) copy-start(f32[3,9]{1,0:T(4,128)} %param.5) | copy-start | bytes 328
  36.5 49.5 %collective-permute-start = (bf16[16,16,16,4]{2,1,3,0:T(8,128)(2,1)}, bf16[16,16,16,4]{2,1,3,0:T(8,128)(2,1)}, u32[]{:S(2)}, u32[]{:S(2)}) collective-permute-start(bf16[16,16,16,4]{2,1,3,0:T(8,128)(2,1)} %copy.37), channel_id=1, source_target_pairs={{0,8},{8,16},{16,24},{1,9},{9,17},{17,25},{2,10},{10,18},{18,26},{... | collective-permute-start | bytes 98312 | tf_op jit(solution)/shard_map/ppermute | solution.py:15
  44.2 44.4 %collective-permute-start.1 = (bf16[16,16,16,4]{2,1,3,0:T(8,128)(2,1)}, bf16[16,16,16,4]{2,1,3,0:T(8,128)(2,1)}, u32[]{:S(2)}, u32[]{:S(2)}) collective-permute-start(bf16[16,16,16,4]{2,1,3,0:T(8,128)(2,1)} %copy.38), channel_id=1, source_target_pairs={{8,0},{16,8},{24,16},{9,1},{17,9},{25,17},{10,2},{18,10},{26,18},{... | collective-permute-start | bytes 98312 | tf_op jit(solution)/shard_map/ppermute | solution.py:17
  83.4 22.4 %collective-permute-start.8 = (bf16[16,8,4,64]{3,0,2,1:T(8,128)(2,1)S(1)}, bf16[16,8,4,64]{3,0,2,1:T(8,128)(2,1)S(1)}, u32[]{:S(2)}, u32[]{:S(2)}) collective-permute-start(bf16[16,8,4,64]{3,0,2,1:T(8,128)(2,1)S(1)} %get-tuple-element.15), channel_id=1, source_target_pairs={{0,4},{1,5},{2,6},{3,7},{8,12},{9,13},{10,14},{11,15},{16,20},{17,... | collective-permute-start | bytes 196616 | tf_op jit(solution)/shard_map/ppermute | solution.py:15
  84.7 21.1 %collective-permute-start.9 = (bf16[16,8,4,64]{3,0,2,1:T(8,128)(2,1)S(1)}, bf16[16,8,4,64]{3,0,2,1:T(8,128)(2,1)S(1)}, u32[]{:S(2)}, u32[]{:S(2)}) collective-permute-start(bf16[16,8,4,64]{3,0,2,1:T(8,128)(2,1)S(1)} %get-tuple-element.16), channel_id=1, source_target_pairs={{4,0},{5,1},{6,2},{7,3},{12,8},{13,9},{14,10},{15,11},{20,16},{21,... | collective-permute-start | bytes 196616 | tf_op jit(solution)/shard_map/ppermute | solution.py:17
  101.3 16.0 %collective-permute-start.2 = (f32[16,16,4,128]{3,2,1,0:T(4,128)S(1)}, f32[16,16,4,128]{3,2,1,0:T(4,128)S(1)}, u32[]{:S(2)}, u32[]{:S(2)}) collective-permute-start(f32[16,16,4,128]{3,2,1,0:T(4,128)S(1)} %get-tuple-element.7), channel_id=1, source_target_pairs={{0,4},{1,5},{2,6},{3,7},{8,12},{9,13},{10,14},{11,15},{16,20},{17,... | collective-permute-start | bytes 1572872 | tf_op jit(solution)/shard_map/ppermute | solution.py:15
  104.3 12.9 %collective-permute-start.3 = (f32[16,16,4,128]{3,2,1,0:T(4,128)S(1)}, f32[16,16,4,128]{3,2,1,0:T(4,128)S(1)}, u32[]{:S(2)}, u32[]{:S(2)}) collective-permute-start(f32[16,16,4,128]{3,2,1,0:T(4,128)S(1)} %get-tuple-element.8), channel_id=1, source_target_pairs={{4,0},{5,1},{6,2},{7,3},{12,8},{13,9},{14,10},{15,11},{20,16},{21,... | collective-permute-start | bytes 1572872 | tf_op jit(solution)/shard_map/ppermute | solution.py:17
  112.4 25.8 %collective-permute-start.10 = (bf16[16,4,8,64]{3,0,2,1:T(8,128)(2,1)}, bf16[16,4,8,64]{3,0,2,1:T(8,128)(2,1)S(1)}, u32[]{:S(2)}, u32[]{:S(2)}) collective-permute-start(bf16[16,4,8,64]{3,0,2,1:T(8,128)(2,1)} %get-tuple-element.13), channel_id=1, source_target_pairs={{0,1},{1,2},{2,3},{4,5},{5,6},{6,7},{8,9},{9,10},{10,11},{12,13},{... | collective-permute-start | bytes 196616 | tf_op jit(solution)/shard_map/ppermute | solution.py:15
  115.9 22.3 %collective-permute-start.11 = (bf16[16,4,8,64]{3,0,2,1:T(8,128)(2,1)S(1)}, bf16[16,4,8,64]{3,0,2,1:T(8,128)(2,1)S(1)}, u32[]{:S(2)}, u32[]{:S(2)}) collective-permute-start(bf16[16,4,8,64]{3,0,2,1:T(8,128)(2,1)S(1)} %get-tuple-element.14), channel_id=1, source_target_pairs={{1,0},{2,1},{3,2},{5,4},{6,5},{7,6},{9,8},{10,9},{11,10},{13,12},{... | collective-permute-start | bytes 196616 | tf_op jit(solution)/shard_map/ppermute | solution.py:17
  127.2 47.9 %collective-permute-start.4 = (f32[16,4,16,128]{3,2,1,0:T(8,128)}, f32[16,4,16,128]{3,2,1,0:T(8,128)}, u32[]{:S(2)}, u32[]{:S(2)}) collective-permute-start(f32[16,4,16,128]{3,2,1,0:T(8,128)} %get-tuple-element.5), channel_id=1, source_target_pairs={{0,1},{1,2},{2,3},{4,5},{5,6},{6,7},{8,9},{9,10},{10,11},{12,13},{... | collective-permute-start | bytes 1572872 | tf_op jit(solution)/shard_map/ppermute | solution.py:15
  132.6 42.6 %collective-permute-start.5 = (f32[16,4,16,128]{3,2,1,0:T(8,128)}, f32[16,4,16,128]{3,2,1,0:T(8,128)}, u32[]{:S(2)}, u32[]{:S(2)}) collective-permute-start(f32[16,4,16,128]{3,2,1,0:T(8,128)} %get-tuple-element.6), channel_id=1, source_target_pairs={{1,0},{2,1},{3,2},{5,4},{6,5},{7,6},{9,8},{10,9},{11,10},{13,12},{... | collective-permute-start | bytes 1572872 | tf_op jit(solution)/shard_map/ppermute | solution.py:17
  175.2 10.1 %copy-start.1 = (bf16[2,2,16,2048]{3,2,1,0:T(8,128)(2,1)S(1)}, bf16[2,2,16,2048]{3,2,1,0:T(8,128)(2,1)}, u32[]{:S(2)}) copy-start(bf16[2,2,16,2048]{3,2,1,0:T(8,128)(2,1)} %param.7) | copy-start | bytes 786436
where the time goes:
time: 187 us; the launch traced here: 185 us
  local copies, waits for them, and re-layouts  66 us (35%)
  other arithmetic  45.1 us (24%)
  starting transfers between devices  31.9 us (17%)
  blocking collectives  25.3 us (14%)
  matrix products  16.6 us (9%)
    ppermute x6, starting transfers between devices, padded_2(): lax.ppermute(tail, axis, [(i, (i + 1) % count) for i in range(ends)])  24 us
    dot_general x2, matrix products, conv_padded(): lax.dot_general(padded, band, (((along,), (0,)), ((), ())), precision=lax...  16.2 us
    all_gather x1, blocking collectives, shards(): along_z = lax.all_gather(along_y, 'gz', axis=1, tiled=True)  13.6 us
    reshape x2, local copies, waits for them, and re-layouts, prolong(): return jnp.repeat(values, factor, axis=3)  13.6 us
    reduce_sum x2, other arithmetic, restrict(): return shaped.mean(axis=(2, 4, 6))  12.3 us
    broadcast_in_dim x2, local copies, waits for them, and re-layouts, prolong(): return jnp.repeat(values, factor, axis=3)  12.1 us
    convert_element_type x1, other arithmetic, shards(): return (fine_part + prolong(coarse_total, 2)).astype(jnp.bfloat16)  10.1 us
    reshape x1, local copies, waits for them, and re-layouts, restrict(): values.reshape(count, depth // factor, factor, rows // factor, factor, co...  9.92 us
  transfers between devices with their start and end apart: 12, of which 0 were waited for; matrix products, arithmetic and copies ran while one was open for 49% of the time, Pallas kernels for 0%

commit v1 on v0

v1 whole, which is shorter than its diff:
```python
import jax
import jax.numpy as jnp
from jax import lax
from jax.experimental import pallas as pl
from jax.experimental.pallas import tpu as pltpu
from jax.sharding import PartitionSpec as P

F32 = jnp.float32
BF16 = jnp.bfloat16
R = 4
E = 2 * R


def swaps(count, kind):
    pairs = []
    for i in range(kind, count - 1, 2):
        pairs += [(i, i + 1), (i + 1, i)]
    return pairs


def kinds(count):
    return [k for k in (0, 1) if swaps(count, k)]


def upper(index, kind):
    return lax.rem(index + kind, 2) == 0


def iota(shape, dim):
    return lax.broadcasted_iota(jnp.int32, shape, dim)


def dot(a, b, dims=((1,), (0,)), precision=None):
    return lax.dot_general(a, b, (dims, ((), ())), precision=precision, preferred_element_type=F32)


def lookup(offset, taps, row):
    total = jnp.zeros(offset.shape, F32)
    for k in range(2 * R + 1):
        total = jnp.where(offset == k, taps[row, k], total)
    return total


def one(condition, value=1.0):
    return jnp.where(condition, value, 0.0).astype(BF16)


def wide(parts):
    return jnp.concatenate(parts, axis=1)


class Sizes:
    def __init__(self, shape, top_shape, mesh_sizes):
        self.V, self.Z, self.Y, self.X = shape
        self.nx, self.ny, self.nz = mesh_sizes
        self.rows = self.Z * self.Y
        self.lanes = self.V * self.X
        self.raw = R * self.Y
        self.avg = (R // 2) * (self.Y // 2)
        self.face = self.raw + self.avg
        self.kx, self.ky, self.kz = kinds(self.nx), kinds(self.ny), kinds(self.nz)
        self.yf, self.yc = self.Z * R, (self.Z // 2) * R
        self.zyf, self.zyc = R * R, R * R
        self.ypack = self.yf + self.yc + len(self.kz) * (self.zyf + self.zyc)
        self.tz, self.ty, self.tx = top_shape
        self.top = self.tz * self.ty * self.tx
        self.gz = self.raw + self.face
        self.tile = self.ty * self.tx * self.nx


def call(body, outs, cost=0, bytes_=0):
    return pl.pallas_call(
        body,
        out_shape=outs,
        cost_estimate=pl.CostEstimate(flops=cost, bytes_accessed=bytes_, transcendentals=0),
    )


def smem():
    return pl.BlockSpec(memory_space=pltpu.SMEM)


def vmem():
    return pl.BlockSpec(memory_space=pltpu.VMEM)


def faces_kernel(s, field, *outs):
    me = lax.axis_index("gz")
    row = iota((s.avg, s.raw), 0)
    col = iota((s.avg, s.raw), 1)
    half = s.Y // 2
    mean = one((col // s.Y // 2 == row // half) & (col % s.Y // 2 == row % half), 0.25)
    for kind, out in zip(s.kz, outs):
        up = upper(me, kind)
        start = jnp.where(up, s.Z - R, 0)
        further = jnp.where(up, s.Z - E, R)
        for v in range(s.V):
            out[v, : s.raw, :] = field[v, pl.ds(start, R)].reshape(s.raw, s.X)
        data = wide([field[v, pl.ds(further, R)].reshape(s.raw, s.X) for v in range(s.V)])
        means = dot(mean, data).astype(BF16)
        for v in range(s.V):
            out[v, s.raw :, :] = means[:, v * s.X : (v + 1) * s.X]


def edges_kernel(s, field, *outs):
    gx = lax.axis_index("gx")
    *edges, piece = outs
    data = wide([field[v].reshape(s.rows, s.X) for v in range(s.V)])
    row = iota((s.lanes, s.V * E), 0)
    lane = iota((s.lanes, s.V * E), 1)
    half = s.Y // 2
    for kind, out in zip(s.kx, edges):
        first = jnp.where(upper(gx, kind), s.X - E, 0)
        pick = one((row // s.X == lane // E) & (row % s.X - first == lane % E))
        packed = dot(data, pick).astype(BF16)
        out[: s.rows, :] = packed
        r = iota((2 * s.avg, s.rows), 0)
        c = iota((2 * s.avg, s.rows), 1)
        layer = r // half * 2 + jnp.where(r < s.avg, R, s.Z - E - R)
        mean = one((c // s.Y // 2 * 2 == layer) & (c % s.Y // 2 == r % half), 0.25)
        out[s.rows :, :] = dot(mean, packed).astype(BF16)
    deep, tall, long = s.Z // s.tz, s.Y // s.ty, s.X // s.tx
    r = iota((8, s.rows), 0)
    c = iota((8, s.rows), 1)
    pool = one(c // s.Y // deep * s.ty + c % s.Y // tall == r, 1.0 / (deep * tall))
    sums = dot(pool, data)
    sub = iota((s.V, s.X), 0)
    x = iota((s.X, s.tile), 0)
    lane = iota((s.X, s.tile), 1)
    for i in range(s.tz):
        total = jnp.zeros((s.V, s.tile), F32)
        for j in range(s.ty):
            p = i * s.ty + j
            by_vector = jnp.zeros((s.V, s.X), F32)
            for v in range(s.V):
                line = jnp.broadcast_to(sums[p : p + 1, v * s.X : (v + 1) * s.X], (s.V, s.X))
                by_vector = jnp.where(sub == v, line, by_vector)
            spread = jnp.where(lane == (j * s.nx + gx) * s.tx + x // long, 1.0 / long, 0.0)
            total = total + dot(by_vector, spread, precision=lax.Precision.HIGHEST)
        piece[i * s.V : (i + 1) * s.V, :] = total.astype(BF16)


def corners_kernel(s, *refs):
    me = lax.axis_index("gz")
    halos, outs = refs[: len(s.kx)], refs[len(s.kx) :]
    for kind, out in zip(s.kz, outs):
        up = upper(me, kind)
        start = pl.multiple_of(jnp.where(up, s.rows - s.raw, 0), 16)
        mean = pl.multiple_of(jnp.where(up, s.rows + s.avg, s.rows), 16)
        for i, halo in enumerate(halos):
            out[i * s.face : i * s.face + s.raw, :] = halo[pl.ds(start, s.raw), :]
            out[i * s.face + s.raw : (i + 1) * s.face, :] = halo[pl.ds(mean, s.avg), :]


def x_weights(s, fine, coarse):
    gx = lax.axis_index("gx")
    blocks = []

    def block(place, count):
        col = iota((count, s.X), 1)
        a = lookup(place - col + R, fine, 2)
        b = 0.5 * lookup((place + E) // 2 - R - col // 2 + R, coarse, 2)
        blocks.append(wide([a, b]).astype(BF16))

    block(iota((s.X, s.X), 0), s.X)
    for kind in s.kx:
        c = iota((s.V * E, s.X), 0) % E
        block(jnp.where(upper(gx, kind), s.X + c, c - E), s.V * E)
    return jnp.concatenate(blocks, axis=0)


def xpass_kernel(s, *refs):
    fine, coarse, field, *refs = refs
    n, m = len(s.kx), len(s.kz)
    halos, refs = refs[:n], refs[n:]
    faces, refs = refs[:m], refs[m:]
    corners, refs = refs[:m], refs[m:]
    own, refs = refs[0], refs[1:]
    sides, packs = refs[:m], refs[m:]
    weights = x_weights(s, fine, coarse)
    lane_v = iota((1, s.V * E), 1) // E
    halo_all = [
        jnp.concatenate([h[: s.rows, :]] + [c[i * s.face : (i + 1) * s.face, :] for c in corners], axis=0)
        for i, h in enumerate(halos)
    ]
    for v in range(s.V):
        at = slice(v * s.X, (v + 1) * s.X)
        data = jnp.concatenate([field[v].reshape(s.rows, s.X)] + [f[v] for f in faces], axis=0)
        masked = [jnp.where(lane_v == v, h, jnp.zeros_like(h)) for h in halo_all]
        passed = dot(wide([data] + masked), weights).astype(BF16)
        own[: s.rows, at] = passed[: s.rows, : s.X]
        own[s.rows :, at] = passed[: s.rows, s.X :]
        for i, side in enumerate(sides):
            base = s.rows + i * s.face
            side[: s.raw, at] = passed[base : base + s.raw, : s.X]
            side[s.raw :, at] = passed[base : base + s.face, s.X :]
    gy = lax.axis_index("gy")
    half = s.Y // 2
    for kind, pack in zip(s.ky, packs):
        up = upper(gy, kind)
        y0 = jnp.where(up, s.Y - R, 0)
        c0 = jnp.where(up, half - R, 0)
        r, c = iota((s.yf, s.rows), 0), iota((s.yf, s.rows), 1)
        pick = one((c // s.Y == r // R) & (c % s.Y == y0 + r % R))
        pack[: s.yf, :] = dot(pick, own[: s.rows, :]).astype(BF16)
        r, c = iota((s.yc, s.rows), 0), iota((s.yc, s.rows), 1)
        pick = one((c // s.Y // 2 == r // R) & (c % s.Y // 2 == c0 + r % R), 0.25)
        at = s.yf
        pack[at : at + s.yc, :] = dot(pick, own[s.rows :, :]).astype(BF16)
        at += s.yc
        for side in sides:
            r, c = iota((s.zyf, s.raw), 0), iota((s.zyf, s.raw), 1)
            pick = one((c // s.Y == r // R) & (c % s.Y == y0 + r % R))
            pack[at : at + s.zyf, :] = dot(pick, side[: s.raw, :]).astype(BF16)
            at += s.zyf
            r, c = iota((s.zyc, s.face), 0), iota((s.zyc, s.face), 1)
            q, j = r // R, r % R
            near = (c < s.raw) & (c // s.Y // 2 == q) & (c % s.Y // 2 == c0 + j)
            b = c - s.raw
            far = (c >= s.raw) & (b // half + R // 2 == q) & (b % half == c0 + j)
            pick = jnp.where(near, 0.25, jnp.where(far, 1.0, 0.0)).astype(BF16)
            pack[at : at + s.zyc, :] = dot(pick, side[s.raw :, :]).astype(BF16)
            at += s.zyc


def yz_weights(s, fine, coarse):
    gy, gz = lax.axis_index("gy"), lax.axis_index("gz")
    half, deep = s.Y // 2, s.Z // 2
    blocks = []

    def block(taps, z, y, div, scale=None):
        count = z.shape[1]
        a = lookup(z - iota((s.Z, count), 0) // div + R, taps, 0)
        b = lookup(y - iota((s.Y, count), 0) // div + R, taps, 1)
        if scale is not None:
            b = b * scale
        both = a.reshape(s.Z, 1, count) * b.reshape(1, s.Y, count)
        blocks.append(both.reshape(s.rows, count).astype(BF16))

    c = iota((1, s.rows), 1)
    block(fine, c // s.Y, c % s.Y, 1)
    block(coarse, c // s.Y // 2, c % s.Y // 2, 2, 0.25)
    for kind in s.kz:
        up = upper(gz, kind)
        c = iota((1, s.raw), 1)
        block(fine, c // s.Y + jnp.where(up, s.Z, -R), c % s.Y, 1)
        c = iota((1, s.face), 1)
        b = c - s.raw
        near = c // s.Y // 2 + jnp.where(up, deep, -R // 2)
        far = b // half + jnp.where(up, deep + R // 2, -R)
        z = jnp.where(c < s.raw, near, far)
        y = jnp.where(c < s.raw, c % s.Y // 2, b % half)
        block(coarse, z, y, 2, jnp.where(c < s.raw, 0.25, 1.0))
    for kind in s.ky:
        up = upper(gy, kind)
        fy, cy = jnp.where(up, s.Y, -R), jnp.where(up, half, -R)
        c = iota((1, s.yf), 1)
        block(fine, c // R, c % R + fy, 1)
        c = iota((1, s.yc), 1)
        block(coarse, c // R, c % R + cy, 2)
        for zkind in s.kz:
            zup = upper(gz, zkind)
            c = iota((1, s.zyf), 1)
            block(fine, c // R + jnp.where(zup, s.Z, -R), c % R + fy, 1)
            q = iota((1, s.zyc), 1) // R
            j = iota((1, s.zyc), 1) % R
            near = q + jnp.where(zup, deep, -R // 2)
            far = q - R // 2 + jnp.where(zup, deep + R // 2, -R)
            block(coarse, jnp.where(q < R // 2, near, far), j + cy, 2)
    r, c = iota((s.rows, s.top), 0), iota((s.rows, s.top), 1)
    z, y = r // s.Y // (s.Z // s.tz), r % s.Y // (s.Y // s.ty)
    blocks.append(one((c // s.tx == z * s.ty + y)))
    return blocks


def final_kernel(s, *refs):
    fine, coarse, own, *refs = refs
    m, k = len(s.kz), len(s.ky)
    sides, refs = refs[:m], refs[m:]
    packs, refs = refs[:k], refs[k:]
    gathered, kernel, out, weights = refs
    at = 0
    for block in yz_weights(s, fine, coarse):
        weights[:, at : at + block.shape[1]] = block
        at += block.shape[1]
    total = jnp.zeros((s.top, s.V), F32)
    for z in range(s.nz):
        for i in range(s.tz):
            for y in range(s.ny):
                part = jnp.zeros((s.V, s.tile), F32)
                for x in range(s.nx):
                    device = (x * s.ny + y) * s.nz + z
                    part = part + gathered[device, i * s.V : (i + 1) * s.V, :].astype(F32)
                q = ((z * s.tz + i) * s.ny + y) * s.tile
                total = total + dot(kernel[:, q : q + s.tile], part.astype(BF16), ((1,), (1,)))
    r, c = iota((s.top, s.X), 0), iota((s.top, s.X), 1)
    spread = c // (s.X // s.tx) == r % s.tx
    for v in range(s.V):
        cols = slice(v * s.X, (v + 1) * s.X)
        line = jnp.broadcast_to(total[:, v : v + 1], (s.top, s.X))
        top = jnp.where(spread, line, 0.0).astype(BF16)
        parts = [own[:, cols]] + [x[:, cols] for x in sides] + [x[:, cols] for x in packs] + [top]
        result = dot(weights[...], jnp.concatenate(parts, axis=0))
        out[v] = result.astype(BF16).reshape(s.Z, s.Y, s.X)


def shape(*dims):
    return jax.ShapeDtypeStruct(dims, BF16)


def bind(body, s):
    def kernel(*refs):
        body(s, *refs)

    kernel.__name__ = body.__name__
    return kernel


def shards(sizes, field, fine_taps, coarse_taps, top_kernel):
    s = Sizes(field.shape, top_kernel.shape[:3], sizes)
    n, m, k = len(s.kx), len(s.kz), len(s.ky)

    def run(body, arrays, outs, scalars=0, scratch=(), flops=0, nbytes=2 << 20):
        return pl.pallas_call(
            bind(body, s),
            name=body.__name__,
            out_shape=outs,
            in_specs=[smem()] * scalars + [vmem()] * (len(arrays) - scalars),
            out_specs=[vmem()] * len(outs),
            scratch_shapes=scratch,
            cost_estimate=pl.CostEstimate(flops=flops, bytes_accessed=nbytes, transcendentals=0),
        )(*arrays)

    faces = run(faces_kernel, [field], [shape(s.V, s.face, s.X)] * m)
    faces = [lax.ppermute(a, "gz", swaps(s.nz, kind)) for a, kind in zip(faces, s.kz)]
    *edges, piece = run(
        edges_kernel, [field], [shape(s.rows + 2 * s.avg, s.V * E)] * n + [shape(s.tz * s.V, s.tile)]
    )
    halos = [lax.ppermute(a, "gx", swaps(s.nx, kind)) for a, kind in zip(edges, s.kx)]
    corners = run(corners_kernel, halos, [shape(n * s.face, s.V * E)] * m)
    corners = [lax.ppermute(a, "gz", swaps(s.nz, kind)) for a, kind in zip(corners, s.kz)]
    devices = s.nx * s.ny * s.nz
    gathered = lax.all_to_all(
        jnp.broadcast_to(piece, (devices,) + piece.shape), ("gx", "gy", "gz"), 0, 0
    )
    own, *rest = run(
        xpass_kernel,
        [fine_taps, coarse_taps, field] + halos + faces + corners,
        [shape(2 * s.rows, s.lanes)] + [shape(s.gz, s.lanes)] * m + [shape(s.ypack, s.lanes)] * k,
        scalars=2,
    )
    sides, packs = rest[:m], rest[m:]
    packs = [lax.ppermute(a, "gy", swaps(s.ny, kind)) for a, kind in zip(packs, s.ky)]
    depth = 2 * s.rows + m * s.gz + k * s.ypack + s.top
    kernel_rows = top_kernel.reshape(s.top, top_kernel.shape[3])
    return run(
        final_kernel,
        [fine_taps, coarse_taps, own] + sides + packs + [gathered, kernel_rows],
        [shape(*field.shape)],
        scalars=2,
        scratch=[pltpu.VMEM((s.rows, depth), BF16)],
    )[0]


def solution(mesh):
    sizes = tuple(mesh.shape[name] for name in ("gx", "gy", "gz"))

    def body(*args):
        return shards(sizes, *args)

    return jax.shard_map(
        body,
        mesh=mesh,
        in_specs=(P(None, "gz", "gy", "gx"), P(), P(), P("gz", "gy", "gx", None)),
        out_specs=P(None, "gz", "gy", "gx"),
        check_vma=False,
    )
```

time: 187 us -> 56.7 us (0.30)
  local copies, waits for them, and re-layouts: 66 us -> 3.57 us
  other arithmetic: 45.1 us -> 0 us
  starting transfers between devices: 31.9 us -> 10.9 us
  Pallas kernels: 0 us -> 18.7 us
  matrix products: 16.6 us -> 0 us
  blocking collectives: 25.3 us -> 19.1 us
  waiting for transfers between devices: 0.04 us -> 3.95 us
    reshape x5 -> x0, local copies, waits for them, and re-layouts: 30.4 us -> none  [the longest x2 13.6 us: prolong(): return jnp.repeat(values, factor, axis=3)]
    all_gather x3 -> x0, blocking collectives: 25.3 us -> none  [the longest x1 13.6 us: shards(): along_z = lax.all_gather(along_y, 'gz', axis=1, tiled=True)]
    ppermute x12 -> x7, starting transfers between devices: 31.9 us -> 10.9 us  [the longest x4 8.75 us: shards(): lax.ppermute(a, 'gz', swaps(s.nz, kind))]
    all_to_all x0 -> x1, blocking collectives: none -> 19.1 us  [shards(): lax.all_to_all(jnp.broadcast_to(piece, (devices,) + piece.shape), ('gx',...]
    pallas_call x0 -> x5, Pallas kernels: none -> 18.7 us  [run(): pl.pallas_call(bind(body, s), name=body.__name__, out_shape=outs, in_spec...]
    convert_element_type x6 -> x0, other arithmetic: 18.1 us -> none  [the longest x1 10.1 us: shards(): return (fine_part + prolong(coarse_total, 2)).astype(jnp.bfloat16)]
    dot_general x3 -> x0, matrix products: 16.6 us -> none  [the longest x2 16.2 us: conv_padded(): lax.dot_general(padded, band, (((along,), (0,)), ((), ())), precision=lax...]
    add x2 -> x0, other arithmetic: 14.8 us -> none  [the longest x1 8.94 us: conv_padded(): total + kernel_row[offset] * lax.slice_in_dim(padded, offset, offset + le...]
  transfers between devices with their start and end apart: 12 -> 7, of which waited for: 0 -> 2; matrix products, arithmetic and copies ran while one was open for 49% -> 0% of each run, Pallas kernels for 0% -> 9%
where the time goes in v1:
time: 56.7 us; the launch traced here: 56.3 us
  blocking collectives  19.1 us (34%)
  Pallas kernels  18.7 us (33%)
  starting transfers between devices  10.9 us (19%)
  waiting for transfers between devices  3.95 us (7%)
  local copies, waits for them, and re-layouts  3.57 us (6%)
    all_to_all x1, blocking collectives, shards(): lax.all_to_all(jnp.broadcast_to(piece, (devices,) + piece.shape), ('gx',...  19.1 us
    pallas_call x5, Pallas kernels, run(): pl.pallas_call(bind(body, s), name=body.__name__, out_shape=outs, in_spec...  18.7 us
    ppermute x4, starting transfers between devices, shards(): lax.ppermute(a, 'gz', swaps(s.nz, kind))  8.75 us
    unnamed x16, local copies, waits for them, and re-layouts  3.53 us
    ppermute x2, waiting for transfers between devices, shards(): lax.ppermute(a, 'gx', swaps(s.nx, kind))  2.41 us
    ppermute x2, starting transfers between devices, shards(): lax.ppermute(a, 'gx', swaps(s.nx, kind))  2.15 us
    ppermute x4, waiting for transfers between devices, shards(): lax.ppermute(a, 'gz', swaps(s.nz, kind))  1.54 us
  transfers between devices with their start and end apart: 7, of which 2 were waited for; matrix products, arithmetic and copies ran while one was open for 0% of the time, Pallas kernels for 9%

profile of v1, /device:TPU:0, one launch (start us, length us, event | category | flops | bytes accessed | tf_op | source)
XLA Modules:
  0.0 56.3 jit_solution(247735749783946337)
XLA Ops:
  0.0 2.2 %faces_kernel.1 = (bf16[16,80,128]{2,1,0:T(8,128)(2,1)}, bf16[16,80,128]{2,1,0:T(8,128)(2,1)}) custom-call(bf16[16,16,16,128]{3,2,1,0:T(8,128)(2,1)} %refs_2_.1), custom_call_target="tpu_custom_call" | custom-call | bytes 2097152 | tf_op jit(solution)/shard_map/faces_kernel/pallas_call | solution.py:324
  2.2 3.1 %collective-permute-start.2 = (bf16[16,80,128]{2,1,0:T(8,128)(2,1)}, bf16[16,80,128]{2,1,0:T(8,128)(2,1)S(1)}, u32[]{:S(2)}, u32[]{:S(2)}) collective-permute-start(bf16[16,80,128]{2,1,0:T(8,128)(2,1)} %get-tuple-element.18), channel_id=1, source_target_pairs={{0,1},{1,0},{2,3},{3,2},{4,5},{5,4},{6,7},{7,6},{8,9},{9,8},{10,11... | collective-permute-start | bytes 983048 | tf_op jit(solution)/shard_map/ppermute | solution.py:335
  5.3 0.7 %collective-permute-start.3 = (bf16[16,80,128]{2,1,0:T(8,128)(2,1)}, bf16[16,80,128]{2,1,0:T(8,128)(2,1)S(1)}, u32[]{:S(2)}, u32[]{:S(2)}) collective-permute-start(bf16[16,80,128]{2,1,0:T(8,128)(2,1)} %get-tuple-element.19), channel_id=1, source_target_pairs={{1,2},{2,1},{5,6},{6,5},{9,10},{10,9},{13,14},{14,13},{17,18},{18,... | collective-permute-start | bytes 983048 | tf_op jit(solution)/shard_map/ppermute | solution.py:335
  6.0 3.4 %edges_kernel.1 = (bf16[288,128]{1,0:T(8,128)(2,1)}, bf16[288,128]{1,0:T(8,128)(2,1)}, bf16[32,128]{1,0:T(8,128)(2,1)}) custom-call(bf16[16,16,16,128]{3,2,1,0:T(8,128)(2,1)} %refs_2_.1), custom_call_target="tpu_custom_call" | custom-call | bytes 2097152 | tf_op jit(solution)/shard_map/edges_kernel/pallas_call | solution.py:324
  9.3 0.0 copy-start.7
  9.3 1.5 %collective-permute-start = (bf16[288,128]{1,0:T(8,128)(2,1)}, bf16[288,128]{1,0:T(8,128)(2,1)S(1)}, u32[]{:S(2)}, u32[]{:S(2)}) collective-permute-start(bf16[288,128]{1,0:T(8,128)(2,1)} %get-tuple-element.16), channel_id=1, source_target_pairs={{0,8},{8,0},{16,24},{24,16},{1,9},{9,1},{17,25},{25,17},{2,10},{10... | collective-permute-start | bytes 221192 | tf_op jit(solution)/shard_map/ppermute | solution.py:339
  10.8 0.7 %collective-permute-start.1 = (bf16[288,128]{1,0:T(8,128)(2,1)}, bf16[288,128]{1,0:T(8,128)(2,1)S(1)}, u32[]{:S(2)}, u32[]{:S(2)}) collective-permute-start(bf16[288,128]{1,0:T(8,128)(2,1)} %get-tuple-element.17), channel_id=1, source_target_pairs={{8,16},{16,8},{9,17},{17,9},{10,18},{18,10},{11,19},{19,11},{12,20... | collective-permute-start | bytes 221192 | tf_op jit(solution)/shard_map/ppermute | solution.py:339
  11.5 2.4 %collective-permute-done.refs_0_.refs_3_ = bf16[288,128]{1,0:T(8,128)(2,1)S(1)} collective-permute-done((bf16[288,128]{1,0:T(8,128)(2,1)}, bf16[288,128]{1,0:T(8,128)(2,1)S(1)}, u32[]{:S(2)}, u32[]{:S(2)}) %collective-permute-start) | collective-permute-done | bytes 73760 | tf_op jit(solution)/shard_map/ppermute | solution.py:339
  13.9 0.0 copy-start.3
  13.9 0.0 collective-permute-done.1.refs_1_.refs_4_
  13.9 0.6 %copy-done.3 = bf16[288,128]{1,0:T(8,128)(2,1)} copy-done((bf16[288,128]{1,0:T(8,128)(2,1)}, bf16[288,128]{1,0:T(8,128)(2,1)S(1)}, u32[]{:S(2)}) %copy-start.3) | copy-done | bytes 73752
  14.5 0.0 copy-start.4
  14.5 0.6 %copy-done.4 = bf16[288,128]{1,0:T(8,128)(2,1)} copy-done((bf16[288,128]{1,0:T(8,128)(2,1)}, bf16[288,128]{1,0:T(8,128)(2,1)S(1)}, u32[]{:S(2)}) %copy-start.4) | copy-done | bytes 73752
  15.1 1.6 %corners_kernel.1 = (bf16[160,128]{1,0:T(8,128)(2,1)}, bf16[160,128]{1,0:T(8,128)(2,1)}) custom-call(bf16[288,128]{1,0:T(8,128)(2,1)} %copy-done.3, bf16[288,128]{1,0:T(8,128)(2,1)} %copy-done.4), custom_call_target="tpu_custom_call" | custom-call | bytes 2097152 | tf_op jit(solution)/shard_map/corners_kernel/pallas_call | solution.py:324
  16.7 4.4 %collective-permute-start.4 = (bf16[160,128]{1,0:T(8,128)(2,1)}, bf16[160,128]{1,0:T(8,128)(2,1)S(1)}, u32[]{:S(2)}, u32[]{:S(2)}) collective-permute-start(bf16[160,128]{1,0:T(8,128)(2,1)} %get-tuple-element.20), channel_id=1, source_target_pairs={{0,1},{1,0},{2,3},{3,2},{4,5},{5,4},{6,7},{7,6},{8,9},{9,8},{10,11... | collective-permute-start | bytes 122888 | tf_op jit(solution)/shard_map/ppermute | solution.py:341
  21.1 0.7 %collective-permute-start.5 = (bf16[160,128]{1,0:T(8,128)(2,1)}, bf16[160,128]{1,0:T(8,128)(2,1)S(1)}, u32[]{:S(2)}, u32[]{:S(2)}) collective-permute-start(bf16[160,128]{1,0:T(8,128)(2,1)} %get-tuple-element.21), channel_id=1, source_target_pairs={{1,2},{2,1},{5,6},{6,5},{9,10},{10,9},{13,14},{14,13},{17,18},{18,... | collective-permute-start | bytes 122888 | tf_op jit(solution)/shard_map/ppermute | solution.py:341
  21.7 1.5 %collective-permute-done.4.refs_7_ = bf16[160,128]{1,0:T(8,128)(2,1)S(1)} collective-permute-done((bf16[160,128]{1,0:T(8,128)(2,1)}, bf16[160,128]{1,0:T(8,128)(2,1)S(1)}, u32[]{:S(2)}, u32[]{:S(2)}) %collective-permute-start.4) | collective-permute-done | bytes 40992 | tf_op jit(solution)/shard_map/ppermute | solution.py:341
  23.2 0.0 copy-start.5
  23.2 0.0 collective-permute-done.5.refs_8_
  23.2 0.0 copy-start.6
  23.2 0.0 collective-permute-done.2.refs_5_
  23.3 0.0 copy-start.1
  23.3 0.0 collective-permute-done.3.refs_6_
  23.3 0.6 %copy-done.5 = bf16[160,128]{1,0:T(8,128)(2,1)} copy-done((bf16[160,128]{1,0:T(8,128)(2,1)}, bf16[160,128]{1,0:T(8,128)(2,1)S(1)}, u32[]{:S(2)}) %copy-start.5) | copy-done | bytes 40984
  23.9 0.0 copy-done.6
  23.9 0.1 copy-done.1
  24.0 0.0 copy-start.2
  24.0 0.7 %copy-done.2 = bf16[16,80,128]{2,1,0:T(8,128)(2,1)} copy-done((bf16[16,80,128]{2,1,0:T(8,128)(2,1)}, bf16[16,80,128]{2,1,0:T(8,128)(2,1)S(1)}, u32[]{:S(2)}) %copy-start.2) | copy-done | bytes 327704
  24.7 5.6 %xpass_kernel.1 = (bf16[512,2048]{1,0:T(8,128)(2,1)}, bf16[144,2048]{1,0:T(8,128)(2,1)}, bf16[144,2048]{1,0:T(8,128)(2,1)}, bf16[160,2048]{1,0:T(8,128)(2,1)}) custom-call(f32[3,9]{1,0:T(4,128)} %refs_0_.7, f32[3,9]{1,0:T(4,128)} %refs_1_.3, bf16[16,16,16,128]{3,2,1,0:T(8,128)(2,1)} %refs_2_.1, bf16[288,128]{1,0:T(8,128)(2,1)} %copy-done.3, ...), custom_call_target="tpu_custom_call" | custom-call | bytes 2097152 | tf_op jit(solution)/shard_map/xpass_kernel/pallas_call | solution.py:324
  30.3 0.0 collective-permute-start.6
  30.3 0.0 copy-done.7
  30.4 19.1 %all_to_all.5.refs_6_ = bf16[32,32,128]{2,1,0:T(8,128)(2,1)} all-to-all(bf16[32,32,128]{2,1,0:T(8,128)(2,1)S(1)} %broadcast_in_dim.3), channel_id=1, replica_groups=mesh['gx'=4,'gy'=2,'gz'=4] {'gx','gy','gz'}, dimensions={0} | all-to-all | bytes 524288 | tf_op jit(solution)/shard_map/all_to_all | solution.py:343
  49.5 0.0 collective-permute-done.6.refs_5_
  49.5 0.0 copy-start
  49.5 0.8 %copy-done = bf16[160,2048]{1,0:T(8,128)(2,1)} copy-done((bf16[160,2048]{1,0:T(8,128)(2,1)}, bf16[160,2048]{1,0:T(8,128)(2,1)S(1)}, u32[]{:S(2)}) %copy-start) | copy-done | bytes 655384
  50.3 6.0 %final_kernel.1 = bf16[16,16,16,128]{3,2,1,0:T(8,128)(2,1)} custom-call(f32[3,9]{1,0:T(4,128)} %refs_0_.7, f32[3,9]{1,0:T(4,128)} %refs_1_.3, bf16[512,2048]{1,0:T(8,128)(2,1)} %get-tuple-element.22.refs_2_, bf16[144,2048]{1,0:T(8,128)(2,1)} %get-tuple-element.23.refs_3_, bf16[144,2048]{1,0:T(8,128)(2,1)} %get-tuple-element.24.refs_4_, ...), custom_call_target="tpu_custom_call" | custom-call | bytes 2097152 | tf_op jit(solution)/shard_map/final_kernel/pallas_call | solution.py:324
  (1 shorter events, 0.0 us)
Async XLA Ops:
  2.2 21.0 %collective-permute-start.2 = (bf16[16,80,128]{2,1,0:T(8,128)(2,1)}, bf16[16,80,128]{2,1,0:T(8,128)(2,1)S(1)}, u32[]{:S(2)}, u32[]{:S(2)}) collective-permute-start(bf16[16,80,128]{2,1,0:T(8,128)(2,1)} %get-tuple-element.18), channel_id=1, source_target_pairs={{0,1},{1,0},{2,3},{3,2},{4,5},{5,4},{6,7},{7,6},{8,9},{9,8},{10,11... | collective-permute-start | bytes 983048 | tf_op jit(solution)/shard_map/ppermute | solution.py:335
  5.3 18.0 %collective-permute-start.3 = (bf16[16,80,128]{2,1,0:T(8,128)(2,1)}, bf16[16,80,128]{2,1,0:T(8,128)(2,1)S(1)}, u32[]{:S(2)}, u32[]{:S(2)}) collective-permute-start(bf16[16,80,128]{2,1,0:T(8,128)(2,1)} %get-tuple-element.19), channel_id=1, source_target_pairs={{1,2},{2,1},{5,6},{6,5},{9,10},{10,9},{13,14},{14,13},{17,18},{18,... | collective-permute-start | bytes 983048 | tf_op jit(solution)/shard_map/ppermute | solution.py:335
  9.3 21.0 %copy-start.7 = (bf16[32,128]{1,0:T(8,128)(2,1)S(1)}, bf16[32,128]{1,0:T(8,128)(2,1)}, u32[]{:S(2)}) copy-start(bf16[32,128]{1,0:T(8,128)(2,1)} %get-tuple-element.26) | copy-start | bytes 24580
  9.3 4.6 %collective-permute-start = (bf16[288,128]{1,0:T(8,128)(2,1)}, bf16[288,128]{1,0:T(8,128)(2,1)S(1)}, u32[]{:S(2)}, u32[]{:S(2)}) collective-permute-start(bf16[288,128]{1,0:T(8,128)(2,1)} %get-tuple-element.16), channel_id=1, source_target_pairs={{0,8},{8,0},{16,24},{24,16},{1,9},{9,1},{17,25},{25,17},{2,10},{10... | collective-permute-start | bytes 221192 | tf_op jit(solution)/shard_map/ppermute | solution.py:339
  10.8 3.1 %collective-permute-start.1 = (bf16[288,128]{1,0:T(8,128)(2,1)}, bf16[288,128]{1,0:T(8,128)(2,1)S(1)}, u32[]{:S(2)}, u32[]{:S(2)}) collective-permute-start(bf16[288,128]{1,0:T(8,128)(2,1)} %get-tuple-element.17), channel_id=1, source_target_pairs={{8,16},{16,8},{9,17},{17,9},{10,18},{18,10},{11,19},{19,11},{12,20... | collective-permute-start | bytes 221192 | tf_op jit(solution)/shard_map/ppermute | solution.py:339
  13.9 0.6 %copy-start.3 = (bf16[288,128]{1,0:T(8,128)(2,1)}, bf16[288,128]{1,0:T(8,128)(2,1)S(1)}, u32[]{:S(2)}) copy-start(bf16[288,128]{1,0:T(8,128)(2,1)S(1)} %collective-permute-done.refs_0_.refs_3_) | copy-start | bytes 221188
  14.5 0.6 %copy-start.4 = (bf16[288,128]{1,0:T(8,128)(2,1)}, bf16[288,128]{1,0:T(8,128)(2,1)S(1)}, u32[]{:S(2)}) copy-start(bf16[288,128]{1,0:T(8,128)(2,1)S(1)} %collective-permute-done.1.refs_1_.refs_4_) | copy-start | bytes 221188
  16.7 6.6 %collective-permute-start.4 = (bf16[160,128]{1,0:T(8,128)(2,1)}, bf16[160,128]{1,0:T(8,128)(2,1)S(1)}, u32[]{:S(2)}, u32[]{:S(2)}) collective-permute-start(bf16[160,128]{1,0:T(8,128)(2,1)} %get-tuple-element.20), channel_id=1, source_target_pairs={{0,1},{1,0},{2,3},{3,2},{4,5},{5,4},{6,7},{7,6},{8,9},{9,8},{10,11... | collective-permute-start | bytes 122888 | tf_op jit(solution)/shard_map/ppermute | solution.py:341
  21.1 2.2 %collective-permute-start.5 = (bf16[160,128]{1,0:T(8,128)(2,1)}, bf16[160,128]{1,0:T(8,128)(2,1)S(1)}, u32[]{:S(2)}, u32[]{:S(2)}) collective-permute-start(bf16[160,128]{1,0:T(8,128)(2,1)} %get-tuple-element.21), channel_id=1, source_target_pairs={{1,2},{2,1},{5,6},{6,5},{9,10},{10,9},{13,14},{14,13},{17,18},{18,... | collective-permute-start | bytes 122888 | tf_op jit(solution)/shard_map/ppermute | solution.py:341
  23.2 0.6 %copy-start.5 = (bf16[160,128]{1,0:T(8,128)(2,1)}, bf16[160,128]{1,0:T(8,128)(2,1)S(1)}, u32[]{:S(2)}) copy-start(bf16[160,128]{1,0:T(8,128)(2,1)S(1)} %collective-permute-done.4.refs_7_) | copy-start | bytes 122884
  23.2 0.6 %copy-start.6 = (bf16[160,128]{1,0:T(8,128)(2,1)}, bf16[160,128]{1,0:T(8,128)(2,1)S(1)}, u32[]{:S(2)}) copy-start(bf16[160,128]{1,0:T(8,128)(2,1)S(1)} %collective-permute-done.5.refs_8_) | copy-start | bytes 122884
  23.3 0.7 %copy-start.1 = (bf16[16,80,128]{2,1,0:T(8,128)(2,1)}, bf16[16,80,128]{2,1,0:T(8,128)(2,1)S(1)}, u32[]{:S(2)}) copy-start(bf16[16,80,128]{2,1,0:T(8,128)(2,1)S(1)} %collective-permute-done.2.refs_5_) | copy-start | bytes 983044
  24.0 0.7 %copy-start.2 = (bf16[16,80,128]{2,1,0:T(8,128)(2,1)}, bf16[16,80,128]{2,1,0:T(8,128)(2,1)S(1)}, u32[]{:S(2)}) copy-start(bf16[16,80,128]{2,1,0:T(8,128)(2,1)S(1)} %collective-permute-done.3.refs_6_) | copy-start | bytes 983044
  30.3 19.2 %collective-permute-start.6 = (bf16[160,2048]{1,0:T(8,128)(2,1)}, bf16[160,2048]{1,0:T(8,128)(2,1)S(1)}, u32[]{:S(2)}, u32[]{:S(2)}) collective-permute-start(bf16[160,2048]{1,0:T(8,128)(2,1)} %get-tuple-element.25), channel_id=1, source_target_pairs={{0,4},{4,0},{1,5},{5,1},{2,6},{6,2},{3,7},{7,3},{8,12},{12,8},{9,1... | collective-permute-start | bytes 1966088 | tf_op jit(solution)/shard_map/ppermute | solution.py:353
  49.5 0.8 %copy-start = (bf16[160,2048]{1,0:T(8,128)(2,1)}, bf16[160,2048]{1,0:T(8,128)(2,1)S(1)}, u32[]{:S(2)}) copy-start(bf16[160,2048]{1,0:T(8,128)(2,1)S(1)} %collective-permute-done.6.refs_5_) | copy-start | bytes 1966084

commit v2 on v1

v2 whole, which is shorter than its diff:
```python
import jax
import jax.numpy as jnp
from jax import lax
from jax.experimental import pallas as pl
from jax.experimental.pallas import tpu as pltpu
from jax.sharding import PartitionSpec as P

F32 = jnp.float32
BF16 = jnp.bfloat16
R = 4
E = 2 * R


def swaps(count, kind):
    pairs = []
    for i in range(kind, count - 1, 2):
        pairs += [(i, i + 1), (i + 1, i)]
    return pairs


def kinds(count):
    return [k for k in (0, 1) if swaps(count, k)]


def upper(index, kind):
    return lax.rem(index + kind, 2) == 0


def iota(shape, dim):
    return lax.broadcasted_iota(jnp.int32, shape, dim)


def dot(a, b, dims=((1,), (0,)), precision=None):
    return lax.dot_general(a, b, (dims, ((), ())), precision=precision, preferred_element_type=F32)


def lookup(offset, taps, row):
    total = jnp.zeros(offset.shape, F32)
    for k in range(2 * R + 1):
        total = jnp.where(offset == k, taps[row, k], total)
    return total


def one(condition, value=1.0):
    return jnp.where(condition, value, 0.0).astype(BF16)


def wide(parts):
    return jnp.concatenate(parts, axis=1)


class Sizes:
    def __init__(self, shape, top_shape, mesh_sizes):
        self.V, self.Z, self.Y, self.X = shape
        self.nx, self.ny, self.nz = mesh_sizes
        self.rows = self.Z * self.Y
        self.lanes = self.V * self.X
        self.raw = R * self.Y
        self.avg = (R // 2) * (self.Y // 2)
        self.face = self.raw + self.avg
        self.kx, self.ky, self.kz = kinds(self.nx), kinds(self.ny), kinds(self.nz)
        self.yf, self.yc = self.Z * R, (self.Z // 2) * R
        self.zyf, self.zyc = R * R, R * R
        self.tz, self.ty, self.tx = top_shape
        self.top = self.tz * self.ty * self.tx
        self.gz = self.raw + self.face
        self.tile = self.ty * self.tx * self.nx


def smem():
    return pl.BlockSpec(memory_space=pltpu.SMEM)


def vmem():
    return pl.BlockSpec(memory_space=pltpu.VMEM)


def faces_kernel(s, field, *refs):
    me = lax.axis_index("gz")
    halos, outs = refs[: len(s.kx)], refs[len(s.kx) :]
    row = iota((s.avg, s.raw), 0)
    col = iota((s.avg, s.raw), 1)
    half = s.Y // 2
    mean = one((col // s.Y // 2 == row // half) & (col % s.Y // 2 == row % half), 0.25)
    for kind, out in zip(s.kz, outs):
        up = upper(me, kind)
        start = jnp.where(up, s.Z - R, 0)
        further = jnp.where(up, s.Z - E, R)
        for v in range(s.V):
            out[v * s.face : v * s.face + s.raw, :] = field[v, pl.ds(start, R)].reshape(s.raw, s.X)
        data = wide([field[v, pl.ds(further, R)].reshape(s.raw, s.X) for v in range(s.V)])
        means = dot(mean, data).astype(BF16)
        for v in range(s.V):
            out[v * s.face + s.raw : (v + 1) * s.face, :] = means[:, v * s.X : (v + 1) * s.X]
        row0 = pl.multiple_of(jnp.where(up, s.rows - s.raw, 0), 16)
        mean0 = pl.multiple_of(jnp.where(up, s.rows + s.avg, s.rows), 16)
        at = s.V * s.face
        for halo in halos:
            out[at : at + s.raw, :] = halo[pl.ds(row0, s.raw), :]
            out[at + s.raw : at + s.face, :] = halo[pl.ds(mean0, s.avg), :]
            at += s.face


def edges_kernel(s, field, *outs):
    gx = lax.axis_index("gx")
    *edges, piece = outs
    data = wide([field[v].reshape(s.rows, s.X) for v in range(s.V)])
    row = iota((s.lanes, s.V * E), 0)
    lane = iota((s.lanes, s.V * E), 1)
    half = s.Y // 2
    for kind, out in zip(s.kx, edges):
        first = jnp.where(upper(gx, kind), s.X - E, 0)
        pick = one((row // s.X == lane // E) & (row % s.X - first == lane % E))
        packed = dot(data, pick).astype(BF16)
        out[: s.rows, :] = packed
        r = iota((2 * s.avg, s.rows), 0)
        c = iota((2 * s.avg, s.rows), 1)
        layer = r // half * 2 + jnp.where(r < s.avg, R, s.Z - E - R)
        mean = one((c // s.Y // 2 * 2 == layer) & (c % s.Y // 2 == r % half), 0.25)
        out[s.rows :, :] = dot(mean, packed).astype(BF16)
    deep, tall, long = s.Z // s.tz, s.Y // s.ty, s.X // s.tx
    r = iota((8, s.rows), 0)
    c = iota((8, s.rows), 1)
    pool = one(c // s.Y // deep * s.ty + c % s.Y // tall == r, 1.0 / (deep * tall))
    sums = dot(pool, data)
    sub = iota((s.V, s.X), 0)
    x = iota((s.X, s.tile), 0)
    lane = iota((s.X, s.tile), 1)
    for i in range(s.tz):
        total = jnp.zeros((s.V, s.tile), F32)
        for j in range(s.ty):
            p = i * s.ty + j
            by_vector = jnp.zeros((s.V, s.X), F32)
            for v in range(s.V):
                line = jnp.broadcast_to(sums[p : p + 1, v * s.X : (v + 1) * s.X], (s.V, s.X))
                by_vector = jnp.where(sub == v, line, by_vector)
            spread = jnp.where(lane == (j * s.nx + gx) * s.tx + x // long, 1.0 / long, 0.0)
            total = total + dot(by_vector, spread, precision=lax.Precision.HIGHEST)
        piece[i * s.V : (i + 1) * s.V, :] = total.astype(BF16)


def x_weights(s, fine, coarse):
    gx = lax.axis_index("gx")
    blocks = []

    def block(place, count):
        col = iota((count, s.X), 1)
        a = lookup(place - col + R, fine, 2)
        b = 0.5 * lookup((place + E) // 2 - R - col // 2 + R, coarse, 2)
        blocks.append(wide([a, b]).astype(BF16))

    block(iota((s.X, s.X), 0), s.X)
    for kind in s.kx:
        c = iota((s.V * E, s.X), 0) % E
        block(jnp.where(upper(gx, kind), s.X + c, c - E), s.V * E)
    return jnp.concatenate(blocks, axis=0)


def pick_y(s, up, fine):
    if fine:
        r, c = iota((s.yf, s.rows), 0), iota((s.yf, s.rows), 1)
        y0 = jnp.where(up, s.Y - R, 0)
        return one((c // s.Y == r // R) & (c % s.Y == y0 + r % R))
    r, c = iota((s.yc, s.rows), 0), iota((s.yc, s.rows), 1)
    c0 = jnp.where(up, s.Y // 2 - R, 0)
    return one((c // s.Y // 2 == r // R) & (c % s.Y // 2 == c0 + r % R), 0.25)


def pick_zy(s, up, fine):
    half = s.Y // 2
    if fine:
        r, c = iota((s.zyf, s.raw), 0), iota((s.zyf, s.raw), 1)
        y0 = jnp.where(up, s.Y - R, 0)
        return one((c // s.Y == r // R) & (c % s.Y == y0 + r % R))
    r, c = iota((s.zyc, s.face), 0), iota((s.zyc, s.face), 1)
    q, y = r // R, r % R + jnp.where(up, half - R, 0)
    near = (c < s.raw) & (c // s.Y // 2 == q) & (c % s.Y // 2 == y)
    b = c - s.raw
    far = (c >= s.raw) & (b // half + R // 2 == q) & (b % half == y)
    return jnp.where(near, 0.25, jnp.where(far, 1.0, 0.0)).astype(BF16)


def xpass(s, weights, data, halos, v):
    lane_v = iota((1, s.V * E), 1) // E
    masked = [jnp.where(lane_v == v, h, jnp.zeros_like(h)) for h in halos]
    return dot(wide([data] + masked), weights).astype(BF16)


def own_kernel(s, *refs):
    fine, coarse, field, *refs = refs
    n = len(s.kx)
    halos, (weights, own, *packs) = [h[: s.rows, :] for h in refs[:n]], refs[n:]
    weights[...] = x_weights(s, fine, coarse)
    for v in range(s.V):
        at = slice(v * s.X, (v + 1) * s.X)
        passed = xpass(s, weights[...], field[v].reshape(s.rows, s.X), halos, v)
        own[: s.rows, at] = passed[:, : s.X]
        own[s.rows :, at] = passed[:, s.X :]
    gy = lax.axis_index("gy")
    for kind, pack in zip(s.ky, packs):
        up = upper(gy, kind)
        pack[: s.yf, :] = dot(pick_y(s, up, True), own[: s.rows, :]).astype(BF16)
        pack[s.yf :, :] = dot(pick_y(s, up, False), own[s.rows :, :]).astype(BF16)


def sides_kernel(s, weights, *refs):
    m = len(s.kz)
    faces, sides, packs = refs[:m], refs[m : 2 * m], refs[2 * m :]
    base = s.V * s.face
    halos = [
        jnp.concatenate([f[base + i * s.face : base + (i + 1) * s.face, :] for f in faces], axis=0)
        for i in range(len(s.kx))
    ]
    for v in range(s.V):
        at = slice(v * s.X, (v + 1) * s.X)
        data = jnp.concatenate([f[v * s.face : (v + 1) * s.face, :] for f in faces], axis=0)
        passed = xpass(s, weights[...], data, halos, v)
        for i, side in enumerate(sides):
            base = i * s.face
            side[: s.raw, at] = passed[base : base + s.raw, : s.X]
            side[s.raw :, at] = passed[base : base + s.face, s.X :]
    gy = lax.axis_index("gy")
    for kind, pack in zip(s.ky, packs):
        up = upper(gy, kind)
        at = 0
        for side in sides:
            pack[at : at + s.zyf, :] = dot(pick_zy(s, up, True), side[: s.raw, :]).astype(BF16)
            at += s.zyf
            pack[at : at + s.zyc, :] = dot(pick_zy(s, up, False), side[s.raw :, :]).astype(BF16)
            at += s.zyc


def yz_weights(s, fine, coarse):
    gy, gz = lax.axis_index("gy"), lax.axis_index("gz")
    half, deep = s.Y // 2, s.Z // 2

    def block(taps, z, y, div, scale=None):
        count = z.shape[1]
        a = lookup(z - iota((s.Z, count), 0) // div + R, taps, 0)
        b = lookup(y - iota((s.Y, count), 0) // div + R, taps, 1)
        if scale is not None:
            b = b * scale
        both = a.reshape(s.Z, 1, count) * b.reshape(1, s.Y, count)
        return both.reshape(s.rows, count).astype(BF16)

    c = iota((1, s.rows), 1)
    first = [
        block(fine, c // s.Y, c % s.Y, 1),
        block(coarse, c // s.Y // 2, c % s.Y // 2, 2, 0.25),
    ]
    second = []
    for kind in s.ky:
        up = upper(gy, kind)
        c = iota((1, s.yf), 1)
        first.append(block(fine, c // R, c % R + jnp.where(up, s.Y, -R), 1))
        c = iota((1, s.yc), 1)
        first.append(block(coarse, c // R, c % R + jnp.where(up, half, -R), 2))
    for kind in s.kz:
        up = upper(gz, kind)
        c = iota((1, s.raw), 1)
        second.append(block(fine, c // s.Y + jnp.where(up, s.Z, -R), c % s.Y, 1))
        c = iota((1, s.face), 1)
        b = c - s.raw
        near = c // s.Y // 2 + jnp.where(up, deep, -R // 2)
        far = b // half + jnp.where(up, deep + R // 2, -R)
        z = jnp.where(c < s.raw, near, far)
        y = jnp.where(c < s.raw, c % s.Y // 2, b % half)
        second.append(block(coarse, z, y, 2, jnp.where(c < s.raw, 0.25, 1.0)))
    for kind in s.ky:
        up = upper(gy, kind)
        for zkind in s.kz:
            zup = upper(gz, zkind)
            c = iota((1, s.zyf), 1)
            z, y = c // R + jnp.where(zup, s.Z, -R), c % R + jnp.where(up, s.Y, -R)
            second.append(block(fine, z, y, 1))
            c = iota((1, s.zyc), 1)
            q = c // R
            near = q + jnp.where(zup, deep, -R // 2)
            far = q - R // 2 + jnp.where(zup, deep + R // 2, -R)
            z, y = jnp.where(q < R // 2, near, far), c % R + jnp.where(up, half, -R)
            second.append(block(coarse, z, y, 2))
    r, c = iota((s.rows, s.top), 0), iota((s.rows, s.top), 1)
    z, y = r // s.Y // (s.Z // s.tz), r % s.Y // (s.Y // s.ty)
    second.append(one(c // s.tx == z * s.ty + y))
    return first, second


def partial_kernel(s, *refs):
    fine, coarse, own, *refs = refs
    k = len(s.ky)
    packs, (total, later, now) = refs[:k], refs[k:]
    first, second = yz_weights(s, fine, coarse)
    for ref, blocks in ((now, first), (later, second)):
        at = 0
        for block in blocks:
            ref[:, at : at + block.shape[1]] = block
            at += block.shape[1]
    step = min(s.lanes, 4 * s.X)
    for at in range(0, s.lanes, step):
        cols = slice(at, at + step)
        parts = [own[:, cols]] + [x[:, cols] for x in packs]
        total[:, cols] = dot(now[...], jnp.concatenate(parts, axis=0))


def final_kernel(s, *refs):
    m, k = len(s.kz), len(s.ky)
    partial, later, *refs = refs
    sides, refs = refs[:m], refs[m:]
    packs, refs = refs[:k], refs[k:]
    gathered, kernel, out = refs
    gy, gz = lax.axis_index("gy"), lax.axis_index("gz")
    total = jnp.zeros((s.top, s.V), F32)
    for z in range(s.nz):
        for y in range(s.ny):
            for i in range(s.tz):
                part = gathered[slot(z, gz, s.nz), slot(y, gy, s.ny), i * s.V : (i + 1) * s.V, :]
                q = ((z * s.tz + i) * s.ny + y) * s.tile
                total = total + dot(kernel[:, q : q + s.tile], part, ((1,), (1,)))
    r, c = iota((s.top, s.X), 0), iota((s.top, s.X), 1)
    spread = c // (s.X // s.tx) == r % s.tx
    for v in range(s.V):
        cols = slice(v * s.X, (v + 1) * s.X)
        line = jnp.broadcast_to(total[:, v : v + 1], (s.top, s.X))
        top = jnp.where(spread, line, 0.0).astype(BF16)
        parts = [x[:, cols] for x in sides] + [x[:, cols] for x in packs] + [top]
        result = dot(later[...], jnp.concatenate(parts, axis=0)) + partial[:, cols]
        out[v] = result.astype(BF16).reshape(s.Z, s.Y, s.X)


def doubling(count):
    return count & (count - 1) == 0


def slot(index, me, count):
    return index ^ me if doubling(count) else index


def gather(a, axis, count, join):
    if not doubling(count):
        return join(list(lax.all_gather(a, axis)))
    step = 1
    while step < count:
        a = join([a, lax.ppermute(a, axis, [(i, i ^ step) for i in range(count)])])
        step *= 2
    return a


def shape(*dims):
    return jax.ShapeDtypeStruct(dims, BF16)


def bind(body, s):
    def kernel(*refs):
        body(s, *refs)

    kernel.__name__ = body.__name__
    return kernel


def shards(sizes, field, fine_taps, coarse_taps, top_kernel):
    s = Sizes(field.shape, top_kernel.shape[:3], sizes)
    n, m, k = len(s.kx), len(s.kz), len(s.ky)
    taps = [fine_taps, coarse_taps]

    def run(body, arrays, outs, scalars=0, scratch=(), flops=0, nbytes=1 << 20):
        call = pl.pallas_call(
            bind(body, s),
            name=body.__name__,
            out_shape=outs,
            in_specs=[smem()] * scalars + [vmem()] * (len(arrays) - scalars),
            out_specs=[vmem()] * len(outs),
            scratch_shapes=scratch,
            compiler_params=pltpu.CompilerParams(vmem_limit_bytes=24 << 20),
            cost_estimate=pl.CostEstimate(flops=flops, bytes_accessed=nbytes, transcendentals=0),
        )
        return list(call(*arrays))

    def swap(arrays, axis, count, which):
        return [lax.ppermute(a, axis, swaps(count, kind)) for a, kind in zip(arrays, which)]

    *edges, piece = run(
        edges_kernel, [field], [shape(s.rows + 2 * s.avg, s.V * E)] * n + [shape(s.tz * s.V, s.tile)]
    )
    stack = lambda parts: jnp.concatenate(parts, axis=0)
    known = gather(piece[None], "gy", s.ny, stack)
    halos = swap(edges, "gx", s.nx, s.kx)
    faces = run(faces_kernel, [field] + halos, [shape((s.V + n) * s.face, s.X)] * m)
    faces = swap(faces, "gz", s.nz, s.kz)
    known = gather(known, "gx", s.nx, sum)
    known = gather(known[None], "gz", s.nz, stack)
    x_depth = s.X + n * s.V * E
    weights, own, *packs = run(
        own_kernel,
        taps + [field] + halos,
        [shape(x_depth, 2 * s.X), shape(2 * s.rows, s.lanes)] + [shape(s.yf + s.yc, s.lanes)] * k,
        scalars=2,
    )
    packs = swap(packs, "gy", s.ny, s.ky)
    now = 2 * s.rows + k * (s.yf + s.yc)
    later = m * s.gz + k * m * (s.zyf + s.zyc) + s.top
    partial, w_later = run(
        partial_kernel,
        taps + [own] + packs,
        [jax.ShapeDtypeStruct((s.rows, s.lanes), F32), shape(s.rows, later)],
        scalars=2,
        scratch=[pltpu.VMEM((s.rows, now), BF16)],
    )
    rest = run(
        sides_kernel,
        [weights] + faces,
        [shape(s.gz, s.lanes)] * m + [shape(m * (s.zyf + s.zyc), s.lanes)] * k,
    )
    sides, packs = rest[:m], swap(rest[m:], "gy", s.ny, s.ky)
    kernel_rows = top_kernel.reshape(s.top, top_kernel.shape[3])
    return run(
        final_kernel,
        [partial, w_later] + sides + packs + [known, kernel_rows],
        [shape(*field.shape)],
    )[0]


def solution(mesh):
    sizes = tuple(mesh.shape[name] for name in ("gx", "gy", "gz"))

    def body(*args):
        return shards(sizes, *args)

    return jax.shard_map(
        body,
        mesh=mesh,
        in_specs=(P(None, "gz", "gy", "gx"), P(), P(), P("gz", "gy", "gx", None)),
        out_specs=P(None, "gz", "gy", "gx"),
        check_vma=False,
    )
```

time: 56.7 us -> 35.6 us (0.63)
  blocking collectives: 19.1 us -> 0 us
  starting transfers between devices: 10.9 us -> 21.1 us
  Pallas kernels: 18.7 us -> 9.52 us
  local copies, waits for them, and re-layouts: 3.57 us -> 1.24 us
  waiting for transfers between devices: 3.95 us -> 3.36 us
    all_to_all x1 -> x0, blocking collectives: 19.1 us -> none  [shards(): lax.all_to_all(jnp.broadcast_to(piece, (devices,) + piece.shape), ('gx',...]
    ppermute x7 -> x11, starting transfers between devices: 10.9 us -> 21.1 us  [the longest x5 15.3 us: gather(): a = join([a, lax.ppermute(a, axis, [(i, i ^ step) for i in range(count)])])]
    pallas_call x5 -> x6, Pallas kernels: 18.7 us -> 9.52 us  [run(): return list(call(*arrays))]
    unnamed x16 -> x8, local copies, waits for them, and re-layouts: 3.53 us -> 1.24 us
    ppermute x7 -> x11, waiting for transfers between devices: 3.95 us -> 3.36 us  [the longest x5 3.35 us: gather(): a = join([a, lax.ppermute(a, axis, [(i, i ^ step) for i in range(count)])])]
  transfers between devices with their start and end apart: 7 -> 11, of which waited for: 2 -> 2; matrix products, arithmetic and copies ran while one was open for 0% -> 0% of each run, Pallas kernels for 9% -> 15%
where the time goes in v2:
time: 35.6 us; the launch traced here: 35.4 us
  starting transfers between devices  21.1 us (59%)
  Pallas kernels  9.52 us (27%)
  waiting for transfers between devices  3.36 us (9%)
  local copies, waits for them, and re-layouts  1.24 us (3%)
    ppermute x5, starting transfers between devices, gather(): a = join([a, lax.ppermute(a, axis, [(i, i ^ step) for i in range(count)])])  15.3 us
    pallas_call x6, Pallas kernels, run(): return list(call(*arrays))  9.52 us
    ppermute x6, starting transfers between devices, swap(): lax.ppermute(a, axis, swaps(count, kind))  5.81 us
    ppermute x5, waiting for transfers between devices, gather(): a = join([a, lax.ppermute(a, axis, [(i, i ^ step) for i in range(count)])])  3.35 us
    unnamed x8, local copies, waits for them, and re-layouts  1.24 us
  transfers between devices with their start and end apart: 11, of which 2 were waited for; matrix products, arithmetic and copies ran while one was open for 0% of the time, Pallas kernels for 15%

profile of v2, /device:TPU:0, one launch (start us, length us, event | category | flops | bytes accessed | tf_op | source)
XLA Modules:
  0.0 35.4 jit_solution(18130420010262955569)
XLA Ops:
  0.0 0.0 copy-start
  0.0 1.2 %copy-done = bf16[16,16,16,128]{3,2,1,0:T(8,128)(2,1)S(1)} copy-done((bf16[16,16,16,128]{3,2,1,0:T(8,128)(2,1)S(1)}, bf16[16,16,16,128]{3,2,1,0:T(8,128)(2,1)}, u32[]{:S(2)}) %copy-start) | copy-done | bytes 1048600
  1.2 0.0 copy-start.2
  1.2 0.0 copy-start.3
  1.2 1.5 %edges_kernel.1 = (bf16[288,128]{1,0:T(8,128)(2,1)S(1)}, bf16[288,128]{1,0:T(8,128)(2,1)S(1)}, bf16[32,128]{1,0:T(8,128)(2,1)S(1)}) custom-call(bf16[16,16,16,128]{3,2,1,0:T(8,128)(2,1)S(1)} %copy-done), custom_call_target="tpu_custom_call" | custom-call | bytes 1048576 | tf_op jit(solution)/shard_map/edges_kernel/pallas_call | solution.py:376
  2.8 0.5 %collective-permute-start.6 = (bf16[1,32,128]{2,1,0:T(8,128)(2,1)S(1)}, bf16[1,32,128]{2,1,0:T(8,128)(2,1)S(1)}, u32[]{:S(2)}, u32[]{:S(2)}) collective-permute-start(bf16[1,32,128]{2,1,0:T(8,128)(2,1)S(1)} %bitcast.5), channel_id=1, source_target_pairs={{0,4},{4,0},{1,5},{5,1},{2,6},{6,2},{3,7},{7,3},{8,12},{12,8},{9,1... | collective-permute-start | bytes 24584 | tf_op jit(solution)/shard_map/ppermute | solution.py:343
  3.3 2.5 %collective-permute-start = (bf16[288,128]{1,0:T(8,128)(2,1)S(1)}, bf16[288,128]{1,0:T(8,128)(2,1)S(1)}, u32[]{:S(2)}, u32[]{:S(2)}) collective-permute-start(bf16[288,128]{1,0:T(8,128)(2,1)S(1)} %get-tuple-element.18), channel_id=1, source_target_pairs={{0,8},{8,0},{16,24},{24,16},{1,9},{9,1},{17,25},{25,17},{2,10},{10... | collective-permute-start | bytes 221192 | tf_op jit(solution)/shard_map/ppermute | solution.py:379
  5.8 0.7 %collective-permute-start.1 = (bf16[288,128]{1,0:T(8,128)(2,1)S(1)}, bf16[288,128]{1,0:T(8,128)(2,1)S(1)}, u32[]{:S(2)}, u32[]{:S(2)}) collective-permute-start(bf16[288,128]{1,0:T(8,128)(2,1)S(1)} %get-tuple-element.19), channel_id=1, source_target_pairs={{8,16},{16,8},{9,17},{17,9},{10,18},{18,10},{11,19},{19,11},{12,20... | collective-permute-start | bytes 221192 | tf_op jit(solution)/shard_map/ppermute | solution.py:379
  6.4 0.0 collective-permute-done.6
  6.5 4.3 %collective-permute-start.7 = (bf16[2,32,128]{2,1,0:T(8,128)(2,1)S(1)}, bf16[2,32,128]{2,1,0:T(8,128)(2,1)S(1)}, u32[]{:S(2)}, u32[]{:S(2)}) collective-permute-start(bf16[2,32,128]{2,1,0:T(8,128)(2,1)S(1)} %pad_maximum_fusion.2), channel_id=1, source_target_pairs={{0,8},{8,0},{16,24},{24,16},{1,9},{9,1},{17,25},{25,17},{2,10},{10... | collective-permute-start | bytes 49160 | tf_op jit(solution)/shard_map/ppermute | solution.py:343
  10.8 0.0 collective-permute-done.refs_3_.refs_1_
  10.8 0.0 collective-permute-done.1.refs_4_.refs_2_
  10.8 0.2 faces_kernel.1
  11.0 1.6 %collective-permute-start.3 = (bf16[1440,128]{1,0:T(8,128)(2,1)S(1)}, bf16[1440,128]{1,0:T(8,128)(2,1)S(1)}, u32[]{:S(2)}, u32[]{:S(2)}) collective-permute-start(bf16[1440,128]{1,0:T(8,128)(2,1)S(1)} %get-tuple-element.25), channel_id=1, source_target_pairs={{0,1},{1,0},{2,3},{3,2},{4,5},{5,4},{6,7},{7,6},{8,9},{9,8},{10,11... | collective-permute-start | bytes 1105928 | tf_op jit(solution)/shard_map/ppermute | solution.py:379
  12.6 0.7 %collective-permute-start.4 = (bf16[1440,128]{1,0:T(8,128)(2,1)S(1)}, bf16[1440,128]{1,0:T(8,128)(2,1)S(1)}, u32[]{:S(2)}, u32[]{:S(2)}) collective-permute-start(bf16[1440,128]{1,0:T(8,128)(2,1)S(1)} %get-tuple-element.26), channel_id=1, source_target_pairs={{1,2},{2,1},{5,6},{6,5},{9,10},{10,9},{13,14},{14,13},{17,18},{18,... | collective-permute-start | bytes 1105928 | tf_op jit(solution)/shard_map/ppermute | solution.py:379
  13.3 0.0 collective-permute-done.7
  13.3 3.9 %collective-permute-start.8 = (bf16[2,32,128]{2,1,0:T(8,128)(2,1)S(1)}, bf16[2,32,128]{2,1,0:T(8,128)(2,1)S(1)}, u32[]{:S(2)}, u32[]{:S(2)}) collective-permute-start(bf16[2,32,128]{2,1,0:T(8,128)(2,1)S(1)} %fusion), channel_id=1, source_target_pairs={{0,16},{8,24},{16,0},{24,8},{1,17},{9,25},{17,1},{25,9},{2,18},{10... | collective-permute-start | bytes 49160 | tf_op jit(solution)/shard_map/ppermute | solution.py:343
  17.3 0.0 copy-done.2
  17.3 0.0 copy-done.3
  17.3 2.5 %own_kernel.1 = (bf16[384,256]{1,0:T(8,128)(2,1)S(1)}, bf16[512,2048]{1,0:T(8,128)(2,1)S(1)}, bf16[96,2048]{1,0:T(8,128)(2,1)S(1)}) custom-call(f32[3,9]{1,0:T(4,128)S(1)} %copy-done.2, f32[3,9]{1,0:T(4,128)S(1)} %copy-done.3, bf16[16,16,16,128]{3,2,1,0:T(8,128)(2,1)S(1)} %copy-done, bf16[288,128]{1,0:T(8,128)(2,1)S(1)} %collective-permute-done.refs_3_.refs_1_, ...), custom_call_target="tpu_custom_call" | custom-call | bytes 1048576 | tf_op jit(solution)/shard_map/own_kernel/pallas_call | solution.py:376
  19.7 0.0 copy-start.1
  19.8 0.1 collective-permute-start.2
  19.8 0.0 collective-permute-done.8
  19.9 4.4 %collective-permute-start.9 = (bf16[1,2,32,128]{3,2,1,0:T(8,128)(2,1)S(1)}, bf16[1,2,32,128]{3,2,1,0:T(8,128)(2,1)S(1)}, u32[]{:S(2)}, u32[]{:S(2)}) collective-permute-start(bf16[1,2,32,128]{3,2,1,0:T(8,128)(2,1)S(1)} %add_bitcast_fusion), channel_id=1, source_target_pairs={{0,1},{1,0},{2,3},{3,2},{4,5},{5,4},{6,7},{7,6},{8,9},{9,8},{10,11... | collective-permute-start | bytes 49160 | tf_op jit(solution)/shard_map/ppermute | solution.py:343
  24.3 0.0 collective-permute-done.3.refs_1_
  24.3 0.0 collective-permute-done.4.refs_2_
  24.3 1.1 %sides_kernel.1 = (bf16[144,2048]{1,0:T(8,128)(2,1)S(1)}, bf16[144,2048]{1,0:T(8,128)(2,1)S(1)}, bf16[64,2048]{1,0:T(8,128)(2,1)S(1)}) custom-call(bf16[384,256]{1,0:T(8,128)(2,1)S(1)} %get-tuple-element.24.refs_0_, bf16[1440,128]{1,0:T(8,128)(2,1)S(1)} %collective-permute-done.3.refs_1_, bf16[1440,128]{1,0:T(8,128)(2,1)S(1)} %collective-permute-done.4.refs_2_), custom_call_target="tpu_custom_call" | custom-call | bytes 1048576 | tf_op jit(solution)/shard_map/sides_kernel/pallas_call | solution.py:376
  25.4 0.3 collective-permute-start.5
  25.6 0.4 %collective-permute-done.9 = bf16[1,2,32,128]{3,2,1,0:T(8,128)(2,1)S(1)} collective-permute-done((bf16[1,2,32,128]{3,2,1,0:T(8,128)(2,1)S(1)}, bf16[1,2,32,128]{3,2,1,0:T(8,128)(2,1)S(1)}, u32[]{:S(2)}, u32[]{:S(2)}) %collective-permute-start.9) | collective-permute-done | bytes 16416 | tf_op jit(solution)/shard_map/ppermute | solution.py:343
  26.0 2.2 %collective-permute-start.10 = (bf16[2,2,32,128]{3,2,1,0:T(8,128)(2,1)S(1)}, bf16[2,2,32,128]{3,2,1,0:T(8,128)(2,1)S(1)}, u32[]{:S(2)}, u32[]{:S(2)}) collective-permute-start(bf16[2,2,32,128]{3,2,1,0:T(8,128)(2,1)S(1)} %pad_maximum_fusion.1), channel_id=1, source_target_pairs={{0,2},{1,3},{2,0},{3,1},{4,6},{5,7},{6,4},{7,5},{8,10},{9,11},{10,... | collective-permute-start | bytes 98312 | tf_op jit(solution)/shard_map/ppermute | solution.py:343
  28.2 2.9 %collective-permute-done.10 = bf16[2,2,32,128]{3,2,1,0:T(8,128)(2,1)S(1)} collective-permute-done((bf16[2,2,32,128]{3,2,1,0:T(8,128)(2,1)S(1)}, bf16[2,2,32,128]{3,2,1,0:T(8,128)(2,1)S(1)}, u32[]{:S(2)}, u32[]{:S(2)}) %collective-permute-start.10) | collective-permute-done | bytes 32800 | tf_op jit(solution)/shard_map/ppermute | solution.py:343
  31.1 0.0 collective-permute-done.2.refs_3_
  31.1 1.7 %partial_kernel.1 = (f32[256,2048]{1,0:T(8,128)S(1)}, bf16[256,416]{1,0:T(8,128)(2,1)S(1)}) custom-call(f32[3,9]{1,0:T(4,128)S(1)} %copy-done.2, f32[3,9]{1,0:T(4,128)S(1)} %copy-done.3, bf16[512,2048]{1,0:T(8,128)(2,1)S(1)} %get-tuple-element.20.refs_2_, bf16[96,2048]{1,0:T(8,128)(2,1)S(1)} %collective-permute-done.2.refs_3_), custom_call_target="tpu_custom_call" | custom-call | bytes 1048576 | tf_op jit(solution)/shard_map/partial_kernel/pallas_call | solution.py:376
  32.8 0.0 collective-permute-done.5.refs_4_
  32.8 0.0 copy-done.1
  32.8 2.6 %final_kernel.1 = bf16[16,16,16,128]{3,2,1,0:T(8,128)(2,1)} custom-call(f32[256,2048]{1,0:T(8,128)S(1)} %get-tuple-element.22.refs_0_, bf16[256,416]{1,0:T(8,128)(2,1)S(1)} %get-tuple-element.23.refs_1_, bf16[144,2048]{1,0:T(8,128)(2,1)S(1)} %get-tuple-element.27.refs_2_, bf16[144,2048]{1,0:T(8,128)(2,1)S(1)} %get-tuple-element.28.refs_3_, ...), custom_call_target="tpu_custom_call" | custom-call | bytes 1048576 | tf_op jit(solution)/shard_map/final_kernel/pallas_call | solution.py:376
  (5 shorter events, 0.0 us)
Async XLA Ops:
  0.0 1.2 %copy-start = (bf16[16,16,16,128]{3,2,1,0:T(8,128)(2,1)S(1)}, bf16[16,16,16,128]{3,2,1,0:T(8,128)(2,1)}, u32[]{:S(2)}) copy-start(bf16[16,16,16,128]{3,2,1,0:T(8,128)(2,1)} %refs_0_.7) | copy-start | bytes 3145732
  1.2 16.0 %copy-start.2 = (f32[3,9]{1,0:T(4,128)S(1)}, f32[3,9]{1,0:T(4,128)}, u32[]{:S(2)}) copy-start(f32[3,9]{1,0:T(4,128)} %refs_0_.6) | copy-start | bytes 328
  1.2 16.0 %copy-start.3 = (f32[3,9]{1,0:T(4,128)S(1)}, f32[3,9]{1,0:T(4,128)}, u32[]{:S(2)}) copy-start(f32[3,9]{1,0:T(4,128)} %refs_1_.3) | copy-start | bytes 328
  2.8 3.7 %collective-permute-start.6 = (bf16[1,32,128]{2,1,0:T(8,128)(2,1)S(1)}, bf16[1,32,128]{2,1,0:T(8,128)(2,1)S(1)}, u32[]{:S(2)}, u32[]{:S(2)}) collective-permute-start(bf16[1,32,128]{2,1,0:T(8,128)(2,1)S(1)} %bitcast.5), channel_id=1, source_target_pairs={{0,4},{4,0},{1,5},{5,1},{2,6},{6,2},{3,7},{7,3},{8,12},{12,8},{9,1... | collective-permute-start | bytes 24584 | tf_op jit(solution)/shard_map/ppermute | solution.py:343
  3.3 7.5 %collective-permute-start = (bf16[288,128]{1,0:T(8,128)(2,1)S(1)}, bf16[288,128]{1,0:T(8,128)(2,1)S(1)}, u32[]{:S(2)}, u32[]{:S(2)}) collective-permute-start(bf16[288,128]{1,0:T(8,128)(2,1)S(1)} %get-tuple-element.18), channel_id=1, source_target_pairs={{0,8},{8,0},{16,24},{24,16},{1,9},{9,1},{17,25},{25,17},{2,10},{10... | collective-permute-start | bytes 221192 | tf_op jit(solution)/shard_map/ppermute | solution.py:379
  5.8 5.0 %collective-permute-start.1 = (bf16[288,128]{1,0:T(8,128)(2,1)S(1)}, bf16[288,128]{1,0:T(8,128)(2,1)S(1)}, u32[]{:S(2)}, u32[]{:S(2)}) collective-permute-start(bf16[288,128]{1,0:T(8,128)(2,1)S(1)} %get-tuple-element.19), channel_id=1, source_target_pairs={{8,16},{16,8},{9,17},{17,9},{10,18},{18,10},{11,19},{19,11},{12,20... | collective-permute-start | bytes 221192 | tf_op jit(solution)/shard_map/ppermute | solution.py:379
  6.5 6.9 %collective-permute-start.7 = (bf16[2,32,128]{2,1,0:T(8,128)(2,1)S(1)}, bf16[2,32,128]{2,1,0:T(8,128)(2,1)S(1)}, u32[]{:S(2)}, u32[]{:S(2)}) collective-permute-start(bf16[2,32,128]{2,1,0:T(8,128)(2,1)S(1)} %pad_maximum_fusion.2), channel_id=1, source_target_pairs={{0,8},{8,0},{16,24},{24,16},{1,9},{9,1},{17,25},{25,17},{2,10},{10... | collective-permute-start | bytes 49160 | tf_op jit(solution)/shard_map/ppermute | solution.py:343
  11.0 13.3 %collective-permute-start.3 = (bf16[1440,128]{1,0:T(8,128)(2,1)S(1)}, bf16[1440,128]{1,0:T(8,128)(2,1)S(1)}, u32[]{:S(2)}, u32[]{:S(2)}) collective-permute-start(bf16[1440,128]{1,0:T(8,128)(2,1)S(1)} %get-tuple-element.25), channel_id=1, source_target_pairs={{0,1},{1,0},{2,3},{3,2},{4,5},{5,4},{6,7},{7,6},{8,9},{9,8},{10,11... | collective-permute-start | bytes 1105928 | tf_op jit(solution)/shard_map/ppermute | solution.py:379
  12.6 11.7 %collective-permute-start.4 = (bf16[1440,128]{1,0:T(8,128)(2,1)S(1)}, bf16[1440,128]{1,0:T(8,128)(2,1)S(1)}, u32[]{:S(2)}, u32[]{:S(2)}) collective-permute-start(bf16[1440,128]{1,0:T(8,128)(2,1)S(1)} %get-tuple-element.26), channel_id=1, source_target_pairs={{1,2},{2,1},{5,6},{6,5},{9,10},{10,9},{13,14},{14,13},{17,18},{18,... | collective-permute-start | bytes 1105928 | tf_op jit(solution)/shard_map/ppermute | solution.py:379
  13.3 6.5 %collective-permute-start.8 = (bf16[2,32,128]{2,1,0:T(8,128)(2,1)S(1)}, bf16[2,32,128]{2,1,0:T(8,128)(2,1)S(1)}, u32[]{:S(2)}, u32[]{:S(2)}) collective-permute-start(bf16[2,32,128]{2,1,0:T(8,128)(2,1)S(1)} %fusion), channel_id=1, source_target_pairs={{0,16},{8,24},{16,0},{24,8},{1,17},{9,25},{17,1},{25,9},{2,18},{10... | collective-permute-start | bytes 49160 | tf_op jit(solution)/shard_map/ppermute | solution.py:343
  19.7 13.1 %copy-start.1 = (bf16[2,2,16,2048]{3,2,1,0:T(8,128)(2,1)S(1)}, bf16[2,2,16,2048]{3,2,1,0:T(8,128)(2,1)}, u32[]{:S(2)}) copy-start(bf16[2,2,16,2048]{3,2,1,0:T(8,128)(2,1)} %param.7) | copy-start | bytes 786436
  19.8 11.4 %collective-permute-start.2 = (bf16[96,2048]{1,0:T(8,128)(2,1)S(1)}, bf16[96,2048]{1,0:T(8,128)(2,1)S(1)}, u32[]{:S(2)}, u32[]{:S(2)}) collective-permute-start(bf16[96,2048]{1,0:T(8,128)(2,1)S(1)} %get-tuple-element.21), channel_id=1, source_target_pairs={{0,4},{4,0},{1,5},{5,1},{2,6},{6,2},{3,7},{7,3},{8,12},{12,8},{9,1... | collective-permute-start | bytes 1179656 | tf_op jit(solution)/shard_map/ppermute | solution.py:379
  19.9 6.2 %collective-permute-start.9 = (bf16[1,2,32,128]{3,2,1,0:T(8,128)(2,1)S(1)}, bf16[1,2,32,128]{3,2,1,0:T(8,128)(2,1)S(1)}, u32[]{:S(2)}, u32[]{:S(2)}) collective-permute-start(bf16[1,2,32,128]{3,2,1,0:T(8,128)(2,1)S(1)} %add_bitcast_fusion), channel_id=1, source_target_pairs={{0,1},{1,0},{2,3},{3,2},{4,5},{5,4},{6,7},{7,6},{8,9},{9,8},{10,11... | collective-permute-start | bytes 49160 | tf_op jit(solution)/shard_map/ppermute | solution.py:343
  25.4 7.4 %collective-permute-start.5 = (bf16[64,2048]{1,0:T(8,128)(2,1)S(1)}, bf16[64,2048]{1,0:T(8,128)(2,1)S(1)}, u32[]{:S(2)}, u32[]{:S(2)}) collective-permute-start(bf16[64,2048]{1,0:T(8,128)(2,1)S(1)} %get-tuple-element.29), channel_id=1, source_target_pairs={{0,4},{4,0},{1,5},{5,1},{2,6},{6,2},{3,7},{7,3},{8,12},{12,8},{9,1... | collective-permute-start | bytes 786440 | tf_op jit(solution)/shard_map/ppermute | solution.py:379
  26.0 5.1 %collective-permute-start.10 = (bf16[2,2,32,128]{3,2,1,0:T(8,128)(2,1)S(1)}, bf16[2,2,32,128]{3,2,1,0:T(8,128)(2,1)S(1)}, u32[]{:S(2)}, u32[]{:S(2)}) collective-permute-start(bf16[2,2,32,128]{3,2,1,0:T(8,128)(2,1)S(1)} %pad_maximum_fusion.1), channel_id=1, source_target_pairs={{0,2},{1,3},{2,0},{3,1},{4,6},{5,7},{6,4},{7,5},{8,10},{9,11},{10,... | collective-permute-start | bytes 98312 | tf_op jit(solution)/shard_map/ppermute | solution.py:343

commit v3 on v2

--- a/solution.py
+++ b/solution.py
@@ -11,11 +11,18 @@
 E = 2 * R
 
 
-def swaps(count, kind):
+def swaps(count, kind, ring=False):
     pairs = []
     for i in range(kind, count - 1, 2):
         pairs += [(i, i + 1), (i + 1, i)]
+    if ring and kind == 1 and pairs and count % 2 == 0:
+        pairs += [(0, count - 1), (count - 1, 0)]
     return pairs
+
+
+def partner_missing(index, count, kind):
+    at = index + jnp.where(upper(index, kind), 1, -1)
+    return (at < 0) | (at >= count)
 
 
 def kinds(count):
@@ -65,6 +72,10 @@
         self.top = self.tz * self.ty * self.tx
         self.gz = self.raw + self.face
         self.tile = self.ty * self.tx * self.nx
+        self.ride = self.nx == 4 and self.nz == 4 and self.tile == self.V * E
+        self.edge = self.rows + 2 * self.avg + (self.tz * self.V if self.ride else 0)
+        self.chunks = 4 if self.V % 4 == 0 else 1
+        self.corner = len(self.kx) * self.face + (self.tz * self.V if self.ride else 0)
 
 
 def smem():
@@ -75,9 +86,8 @@
     return pl.BlockSpec(memory_space=pltpu.VMEM)
 
 
-def faces_kernel(s, field, *refs):
+def faces_kernel(s, field, *outs):
     me = lax.axis_index("gz")
-    halos, outs = refs[: len(s.kx)], refs[len(s.kx) :]
     row = iota((s.avg, s.raw), 0)
     col = iota((s.avg, s.raw), 1)
     half = s.Y // 2
@@ -87,56 +97,82 @@
         start = jnp.where(up, s.Z - R, 0)
         further = jnp.where(up, s.Z - E, R)
         for v in range(s.V):
-            out[v * s.face : v * s.face + s.raw, :] = field[v, pl.ds(start, R)].reshape(s.raw, s.X)
+            out[v, : s.raw, :] = field[v, pl.ds(start, R)].reshape(s.raw, s.X)
         data = wide([field[v, pl.ds(further, R)].reshape(s.raw, s.X) for v in range(s.V)])
         means = dot(mean, data).astype(BF16)
         for v in range(s.V):
-            out[v * s.face + s.raw : (v + 1) * s.face, :] = means[:, v * s.X : (v + 1) * s.X]
-        row0 = pl.multiple_of(jnp.where(up, s.rows - s.raw, 0), 16)
-        mean0 = pl.multiple_of(jnp.where(up, s.rows + s.avg, s.rows), 16)
-        at = s.V * s.face
+            out[v, s.raw :, :] = means[:, v * s.X : (v + 1) * s.X]
+
+
+def corners_kernel(s, *refs):
+    me = lax.axis_index("gz")
+    n = len(s.kx)
+    halos, refs = refs[:n], refs[n:]
+    if s.ride:
+        piece, across, *outs, known = refs
+        total = piece[...].astype(F32) + across[...].astype(F32)
         for halo in halos:
-            out[at : at + s.raw, :] = halo[pl.ds(row0, s.raw), :]
-            out[at + s.raw : at + s.face, :] = halo[pl.ds(mean0, s.avg), :]
-            at += s.face
-
-
-def edges_kernel(s, field, *outs):
+            total = total + halo[s.rows + 2 * s.avg :, :].astype(F32)
+        known[...] = total.astype(BF16)
+    else:
+        outs = refs
+    for kind, out in zip(s.kz, outs):
+        up = upper(me, kind)
+        start = pl.multiple_of(jnp.where(up, s.rows - s.raw, 0), 16)
+        mean = pl.multiple_of(jnp.where(up, s.rows + s.avg, s.rows), 16)
+        for i, halo in enumerate(halos):
+            at = i * s.face
+            out[at : at + s.raw, :] = halo[pl.ds(start, s.raw), :]
+            out[at + s.raw : at + s.face, :] = halo[pl.ds(mean, s.avg), :]
+        if s.ride:
+            out[n * s.face :, :] = total.astype(BF16)
+
+
+def edges_kernel(s, field, *refs):
     gx = lax.axis_index("gx")
-    *edges, piece = outs
-    data = wide([field[v].reshape(s.rows, s.X) for v in range(s.V)])
-    row = iota((s.lanes, s.V * E), 0)
-    lane = iota((s.lanes, s.V * E), 1)
+    n = len(s.kx)
+    edges, piece = refs[:n], refs[n]
+    chunk = s.V // s.chunks
     half = s.Y // 2
-    for kind, out in zip(s.kx, edges):
-        first = jnp.where(upper(gx, kind), s.X - E, 0)
-        pick = one((row // s.X == lane // E) & (row % s.X - first == lane % E))
-        packed = dot(data, pick).astype(BF16)
-        out[: s.rows, :] = packed
-        r = iota((2 * s.avg, s.rows), 0)
-        c = iota((2 * s.avg, s.rows), 1)
-        layer = r // half * 2 + jnp.where(r < s.avg, R, s.Z - E - R)
-        mean = one((c // s.Y // 2 * 2 == layer) & (c % s.Y // 2 == r % half), 0.25)
-        out[s.rows :, :] = dot(mean, packed).astype(BF16)
     deep, tall, long = s.Z // s.tz, s.Y // s.ty, s.X // s.tx
-    r = iota((8, s.rows), 0)
-    c = iota((8, s.rows), 1)
+    row = iota((chunk * s.X, s.V * E), 0)
+    lane = iota((chunk * s.X, s.V * E), 1)
+    own_v, own_x = row // s.X, row % s.X
+    r, c = iota((8, s.rows), 0), iota((8, s.rows), 1)
     pool = one(c // s.Y // deep * s.ty + c % s.Y // tall == r, 1.0 / (deep * tall))
-    sums = dot(pool, data)
     sub = iota((s.V, s.X), 0)
-    x = iota((s.X, s.tile), 0)
-    lane = iota((s.X, s.tile), 1)
+    first = [jnp.where(upper(gx, kind), s.X - E, 0) for kind in s.kx]
+    packed = [jnp.zeros((s.rows, s.V * E), F32) for kind in s.kx]
+    by_vector = [jnp.zeros((s.V, s.X), F32) for _ in range(s.tz * s.ty)]
+    for i in range(s.chunks):
+        data = wide([field[v].reshape(s.rows, s.X) for v in range(i * chunk, (i + 1) * chunk)])
+        for j in range(n):
+            pick = one((own_v + i * chunk == lane // E) & (own_x - first[j] == lane % E))
+            packed[j] = packed[j] + dot(data, pick)
+        sums = dot(pool, data)
+        for p in range(s.tz * s.ty):
+            for v in range(chunk):
+                line = jnp.broadcast_to(sums[p : p + 1, v * s.X : (v + 1) * s.X], (s.V, s.X))
+                by_vector[p] = jnp.where(sub == v + i * chunk, line, by_vector[p])
+    r, c = iota((2 * s.avg, s.rows), 0), iota((2 * s.avg, s.rows), 1)
+    layer = r // half * 2 + jnp.where(r < s.avg, R, s.Z - E - R)
+    mean = one((c // s.Y // 2 * 2 == layer) & (c % s.Y // 2 == r % half), 0.25)
+    for j in range(n):
+        edge = packed[j].astype(BF16)
+        edges[j][: s.rows, :] = edge
+        edges[j][s.rows : s.rows + 2 * s.avg, :] = dot(mean, edge).astype(BF16)
+    x, lane = iota((s.X, s.tile), 0), iota((s.X, s.tile), 1)
     for i in range(s.tz):
         total = jnp.zeros((s.V, s.tile), F32)
         for j in range(s.ty):
-            p = i * s.ty + j
-            by_vector = jnp.zeros((s.V, s.X), F32)
-            for v in range(s.V):
-                line = jnp.broadcast_to(sums[p : p + 1, v * s.X : (v + 1) * s.X], (s.V, s.X))
-                by_vector = jnp.where(sub == v, line, by_vector)
             spread = jnp.where(lane == (j * s.nx + gx) * s.tx + x // long, 1.0 / long, 0.0)
-            total = total + dot(by_vector, spread, precision=lax.Precision.HIGHEST)
-        piece[i * s.V : (i + 1) * s.V, :] = total.astype(BF16)
+            total = total + dot(by_vector[i * s.ty + j], spread, precision=lax.Precision.HIGHEST)
+        total = total.astype(BF16)
+        piece[i * s.V : (i + 1) * s.V, :] = total
+        if s.ride:
+            for edge in edges:
+                at = s.rows + 2 * s.avg + i * s.V
+                edge[at : at + s.V, :] = total
 
 
 def x_weights(s, fine, coarse):
@@ -152,7 +188,8 @@
     block(iota((s.X, s.X), 0), s.X)
     for kind in s.kx:
         c = iota((s.V * E, s.X), 0) % E
-        block(jnp.where(upper(gx, kind), s.X + c, c - E), s.V * E)
+        place = jnp.where(upper(gx, kind), s.X + c, c - E)
+        block(jnp.where(partner_missing(gx, s.nx, kind), -4 * s.X, place), s.V * E)
     return jnp.concatenate(blocks, axis=0)
 
 
@@ -205,15 +242,14 @@
 
 def sides_kernel(s, weights, *refs):
     m = len(s.kz)
-    faces, sides, packs = refs[:m], refs[m : 2 * m], refs[2 * m :]
-    base = s.V * s.face
+    faces, corners, sides, packs = refs[:m], refs[m : 2 * m], refs[2 * m : 3 * m], refs[3 * m :]
     halos = [
-        jnp.concatenate([f[base + i * s.face : base + (i + 1) * s.face, :] for f in faces], axis=0)
+        jnp.concatenate([c[i * s.face : (i + 1) * s.face, :] for c in corners], axis=0)
         for i in range(len(s.kx))
     ]
     for v in range(s.V):
         at = slice(v * s.X, (v + 1) * s.X)
-        data = jnp.concatenate([f[v * s.face : (v + 1) * s.face, :] for f in faces], axis=0)
+        data = jnp.concatenate([f[v] for f in faces], axis=0)
         passed = xpass(s, weights[...], data, halos, v)
         for i, side in enumerate(sides):
             base = i * s.face
@@ -249,21 +285,25 @@
         block(coarse, c // s.Y // 2, c % s.Y // 2, 2, 0.25),
     ]
     second = []
+
+    def zplace(kind, z):
+        return jnp.where(partner_missing(gz, s.nz, kind), -4 * s.Z, z)
+
     for kind in s.ky:
         up = upper(gy, kind)
         c = iota((1, s.yf), 1)
-        first.append(block(fine, c // R, c % R + jnp.where(up, s.Y, -R), 1))
+        second.append(block(fine, c // R, c % R + jnp.where(up, s.Y, -R), 1))
         c = iota((1, s.yc), 1)
-        first.append(block(coarse, c // R, c % R + jnp.where(up, half, -R), 2))
+        second.append(block(coarse, c // R, c % R + jnp.where(up, half, -R), 2))
     for kind in s.kz:
         up = upper(gz, kind)
         c = iota((1, s.raw), 1)
-        second.append(block(fine, c // s.Y + jnp.where(up, s.Z, -R), c % s.Y, 1))
+        second.append(block(fine, zplace(kind, c // s.Y + jnp.where(up, s.Z, -R)), c % s.Y, 1))
         c = iota((1, s.face), 1)
         b = c - s.raw
         near = c // s.Y // 2 + jnp.where(up, deep, -R // 2)
         far = b // half + jnp.where(up, deep + R // 2, -R)
-        z = jnp.where(c < s.raw, near, far)
+        z = zplace(kind, jnp.where(c < s.raw, near, far))
         y = jnp.where(c < s.raw, c % s.Y // 2, b % half)
         second.append(block(coarse, z, y, 2, jnp.where(c < s.raw, 0.25, 1.0)))
     for kind in s.ky:
@@ -272,23 +312,20 @@
             zup = upper(gz, zkind)
             c = iota((1, s.zyf), 1)
             z, y = c // R + jnp.where(zup, s.Z, -R), c % R + jnp.where(up, s.Y, -R)
-            second.append(block(fine, z, y, 1))
+            second.append(block(fine, zplace(zkind, z), y, 1))
             c = iota((1, s.zyc), 1)
             q = c // R
             near = q + jnp.where(zup, deep, -R // 2)
             far = q - R // 2 + jnp.where(zup, deep + R // 2, -R)
             z, y = jnp.where(q < R // 2, near, far), c % R + jnp.where(up, half, -R)
-            second.append(block(coarse, z, y, 2))
+            second.append(block(coarse, zplace(zkind, z), y, 2))
     r, c = iota((s.rows, s.top), 0), iota((s.rows, s.top), 1)
     z, y = r // s.Y // (s.Z // s.tz), r % s.Y // (s.Y // s.ty)
     second.append(one(c // s.tx == z * s.ty + y))
     return first, second
 
 
-def partial_kernel(s, *refs):
-    fine, coarse, own, *refs = refs
-    k = len(s.ky)
-    packs, (total, later, now) = refs[:k], refs[k:]
+def partial_kernel(s, fine, coarse, own, total, later, now):
     first, second = yz_weights(s, fine, coarse)
     for ref, blocks in ((now, first), (later, second)):
         at = 0
@@ -298,33 +335,41 @@
     step = min(s.lanes, 4 * s.X)
     for at in range(0, s.lanes, step):
         cols = slice(at, at + step)
-        parts = [own[:, cols]] + [x[:, cols] for x in packs]
-        total[:, cols] = dot(now[...], jnp.concatenate(parts, axis=0))
+        total[:, cols] = dot(now[...], own[:, cols])
 
 
 def final_kernel(s, *refs):
     m, k = len(s.kz), len(s.ky)
     partial, later, *refs = refs
+    ends, refs = refs[:k], refs[k:]
     sides, refs = refs[:m], refs[m:]
     packs, refs = refs[:k], refs[k:]
-    gathered, kernel, out = refs
+    gathered, kernel, out, held, sems = refs
     gy, gz = lax.axis_index("gy"), lax.axis_index("gz")
     total = jnp.zeros((s.top, s.V), F32)
     for z in range(s.nz):
         for y in range(s.ny):
             for i in range(s.tz):
-                part = gathered[slot(z, gz, s.nz), slot(y, gy, s.ny), i * s.V : (i + 1) * s.V, :]
+                part = gathered[slot(y, gy, s.ny), slot(z, gz, s.nz), i * s.V : (i + 1) * s.V, :]
                 q = ((z * s.tz + i) * s.ny + y) * s.tile
                 total = total + dot(kernel[:, q : q + s.tile], part, ((1,), (1,)))
     r, c = iota((s.top, s.X), 0), iota((s.top, s.X), 1)
     spread = c // (s.X // s.tx) == r % s.tx
+    chunk = s.V // s.chunks
+    copies = []
     for v in range(s.V):
         cols = slice(v * s.X, (v + 1) * s.X)
         line = jnp.broadcast_to(total[:, v : v + 1], (s.top, s.X))
         top = jnp.where(spread, line, 0.0).astype(BF16)
-        parts = [x[:, cols] for x in sides] + [x[:, cols] for x in packs] + [top]
+        parts = [x[:, cols] for x in (*ends, *sides, *packs)] + [top]
         result = dot(later[...], jnp.concatenate(parts, axis=0)) + partial[:, cols]
-        out[v] = result.astype(BF16).reshape(s.Z, s.Y, s.X)
+        held[v] = result.astype(BF16).reshape(s.Z, s.Y, s.X)
+        if v % chunk == chunk - 1:
+            at = pl.ds(v + 1 - chunk, chunk)
+            copies.append(pltpu.make_async_copy(held.at[at], out.at[at], sems.at[v // chunk]))
+            copies[-1].start()
+    for copy in copies:
+        copy.wait()
 
 
 def doubling(count):
@@ -360,63 +405,99 @@
 def shards(sizes, field, fine_taps, coarse_taps, top_kernel):
     s = Sizes(field.shape, top_kernel.shape[:3], sizes)
     n, m, k = len(s.kx), len(s.kz), len(s.ky)
-    taps = [fine_taps, coarse_taps]
-
-    def run(body, arrays, outs, scalars=0, scratch=(), flops=0, nbytes=1 << 20):
+
+    def run(body, arrays, outs, scalars=0, scratch=(), flops=0, far=(), far_out=False):
+        specs = [vmem()] * len(arrays)
+        for i in range(scalars):
+            specs[i] = smem()
+        for i in far:
+            specs[i] = pl.BlockSpec(memory_space=pltpu.HBM)
         call = pl.pallas_call(
             bind(body, s),
             name=body.__name__,
             out_shape=outs,
-            in_specs=[smem()] * scalars + [vmem()] * (len(arrays) - scalars),
-            out_specs=[vmem()] * len(outs),
+            in_specs=specs,
+            out_specs=[pl.BlockSpec(memory_space=pltpu.HBM) if far_out else vmem()] * len(outs),
             scratch_shapes=scratch,
             compiler_params=pltpu.CompilerParams(vmem_limit_bytes=24 << 20),
-            cost_estimate=pl.CostEstimate(flops=flops, bytes_accessed=nbytes, transcendentals=0),
+            cost_estimate=pl.CostEstimate(flops=flops, bytes_accessed=1 << 20, transcendentals=0),
         )
         return list(call(*arrays))
 
-    def swap(arrays, axis, count, which):
-        return [lax.ppermute(a, axis, swaps(count, kind)) for a, kind in zip(arrays, which)]
-
-    *edges, piece = run(
-        edges_kernel, [field], [shape(s.rows + 2 * s.avg, s.V * E)] * n + [shape(s.tz * s.V, s.tile)]
-    )
+    def swap(arrays, axis, count, which, ring=False):
+        return [lax.ppermute(a, axis, swaps(count, kind, ring)) for a, kind in zip(arrays, which)]
+
+    taps = [fine_taps, coarse_taps]
+    buffers = [pltpu.VMEM(field.shape, BF16), pltpu.SemaphoreType.DMA((s.chunks,))]
+    top = shape(s.tz * s.V, s.tile)
+    with jax.named_scope("faces"):
+        faces = run(faces_kernel, [field], [shape(s.V, s.face, s.X)] * m)
+    with jax.named_scope("zface"):
+        faces = swap(faces, "gz", s.nz, s.kz)
+    with jax.named_scope("edges"):
+        *edges, piece = run(edges_kernel, [field], [shape(s.edge, s.V * E)] * n + [top])
+    with jax.named_scope("xedge"):
+        halos = swap(edges, "gx", s.nx, s.kx, s.ride)
+    corner = [shape(s.corner, s.V * E)] * m
     stack = lambda parts: jnp.concatenate(parts, axis=0)
-    known = gather(piece[None], "gy", s.ny, stack)
-    halos = swap(edges, "gx", s.nx, s.kx)
-    faces = run(faces_kernel, [field] + halos, [shape((s.V + n) * s.face, s.X)] * m)
-    faces = swap(faces, "gz", s.nz, s.kz)
-    known = gather(known, "gx", s.nx, sum)
-    known = gather(known[None], "gz", s.nz, stack)
+    if s.ride:
+        with jax.named_scope("across"):
+            across = lax.ppermute(piece, "gx", [(i, i ^ 2) for i in range(s.nx)])
+        with jax.named_scope("corners"):
+            *corners, known = run(corners_kernel, halos + [piece, across], corner + [top])
+    else:
+        with jax.named_scope("corners"):
+            corners = run(corners_kernel, halos, corner)
+    with jax.named_scope("zcorner"):
+        corners = swap(corners, "gz", s.nz, s.kz, s.ride)
+    if s.ride:
+        with jax.named_scope("zacross"):
+            across = lax.ppermute(known, "gz", [(i, i ^ 2) for i in range(s.nz)])
+        near, far = [c[n * s.face :] for c in corners]
+        known = jnp.stack([known, near, across, far])
+    else:
+        known = gather(gather(piece, "gx", s.nx, sum)[None], "gz", s.nz, stack)
+    with jax.named_scope("known"):
+        known = gather(known[None], "gy", s.ny, stack)
     x_depth = s.X + n * s.V * E
-    weights, own, *packs = run(
-        own_kernel,
-        taps + [field] + halos,
-        [shape(x_depth, 2 * s.X), shape(2 * s.rows, s.lanes)] + [shape(s.yf + s.yc, s.lanes)] * k,
-        scalars=2,
-    )
-    packs = swap(packs, "gy", s.ny, s.ky)
-    now = 2 * s.rows + k * (s.yf + s.yc)
-    later = m * s.gz + k * m * (s.zyf + s.zyc) + s.top
-    partial, w_later = run(
-        partial_kernel,
-        taps + [own] + packs,
-        [jax.ShapeDtypeStruct((s.rows, s.lanes), F32), shape(s.rows, later)],
-        scalars=2,
-        scratch=[pltpu.VMEM((s.rows, now), BF16)],
-    )
-    rest = run(
-        sides_kernel,
-        [weights] + faces,
-        [shape(s.gz, s.lanes)] * m + [shape(m * (s.zyf + s.zyc), s.lanes)] * k,
-    )
-    sides, packs = rest[:m], swap(rest[m:], "gy", s.ny, s.ky)
+    with jax.named_scope("own"):
+        weights, own, *ends = run(
+            own_kernel,
+            taps + [field] + halos,
+            [shape(x_depth, 2 * s.X), shape(2 * s.rows, s.lanes)]
+            + [shape(s.yf + s.yc, s.lanes)] * k,
+            scalars=2,
+            flops=4 * s.rows * s.V * x_depth * s.X,
+        )
+    with jax.named_scope("yown"):
+        ends = swap(ends, "gy", s.ny, s.ky)
+    later = k * (s.yf + s.yc) + m * s.gz + k * m * (s.zyf + s.zyc) + s.top
+    with jax.named_scope("partial"):
+        partial, w_later = run(
+            partial_kernel,
+            taps + [own],
+            [jax.ShapeDtypeStruct((s.rows, s.lanes), F32), shape(s.rows, later)],
+            scalars=2,
+            scratch=[pltpu.VMEM((s.rows, 2 * s.rows), BF16)],
+            flops=4 * s.rows * s.rows * s.lanes,
+        )
+    with jax.named_scope("sides"):
+        rest = run(
+            sides_kernel,
+            [weights] + faces + corners,
+            [shape(s.gz, s.lanes)] * m + [shape(m * (s.zyf + s.zyc), s.lanes)] * k,
+        )
+    with jax.named_scope("yside"):
+        sides, packs = rest[:m], swap(rest[m:], "gy", s.ny, s.ky)
     kernel_rows = top_kernel.reshape(s.top, top_kernel.shape[3])
-    return run(
-        final_kernel,
-        [partial, w_later] + sides + packs + [known, kernel_rows],
-        [shape(*field.shape)],
-    )[0]
+    with jax.named_scope("final"):
+        return run(
+            final_kernel,
+            [partial, w_later] + ends + sides + packs + [known, kernel_rows],
+            [shape(*field.shape)],
+            scratch=buffers,
+            far_out=True,
+        )[0]
 
 
 def solution(mesh):

time: 35.6 us -> 29.9 us (0.84)
  starting transfers between devices: 21.1 us -> 16.1 us
  Pallas kernels: 9.52 us -> 8.66 us
    ppermute x5 -> x1, starting transfers between devices: 15.3 us -> 0.1 us  [gather(): a = join([a, lax.ppermute(a, axis, [(i, i ^ step) for i in range(count)])])]
    ppermute x6 -> x10, starting transfers between devices: 5.81 us -> 16 us  [the longest x8 11.1 us: swap(): lax.ppermute(a, axis, swaps(count, kind, ring))]
    ppermute x6 -> x10, waiting for transfers between devices: 0.02 us -> 3.65 us  [the longest x8 1.96 us: swap(): lax.ppermute(a, axis, swaps(count, kind, ring))]
    ppermute x5 -> x1, waiting for transfers between devices: 3.35 us -> 0.01 us  [gather(): a = join([a, lax.ppermute(a, axis, [(i, i ^ step) for i in range(count)])])]
    pallas_call x6 -> x7, Pallas kernels: 9.52 us -> 8.66 us  [run(): return list(call(*arrays))]
    unnamed x8 -> x10, local copies, waits for them, and re-layouts: 1.24 us -> 1.24 us
  transfers between devices with their start and end apart: 11 -> 11, of which waited for: 2 -> 3; matrix products, arithmetic and copies ran while one was open for 0% -> 0% of each run, Pallas kernels for 15% -> 17%
where the time goes in v3:
time: 29.9 us; the launch traced here: 29.8 us
  starting transfers between devices  16.1 us (54%)
  Pallas kernels  8.66 us (29%)
  waiting for transfers between devices  3.65 us (12%)
  local copies, waits for them, and re-layouts  1.24 us (4%)
    ppermute x8, starting transfers between devices, swap(): lax.ppermute(a, axis, swaps(count, kind, ring))  11.1 us
    pallas_call x7, Pallas kernels, run(): return list(call(*arrays))  8.66 us
    ppermute x1, starting transfers between devices, shards(): across = lax.ppermute(known, 'gz', [(i, i ^ 2) for i in range(s.nz)])  4.78 us
    ppermute x8, waiting for transfers between devices, swap(): lax.ppermute(a, axis, swaps(count, kind, ring))  1.96 us
    unnamed x10, local copies, waits for them, and re-layouts  1.24 us
    ppermute x1, waiting for transfers between devices, shards(): across = lax.ppermute(piece, 'gx', [(i, i ^ 2) for i in range(s.nx)])  1.22 us
  transfers between devices with their start and end apart: 11, of which 3 were waited for; matrix products, arithmetic and copies ran while one was open for 0% of the time, Pallas kernels for 17%

profile of v3, /device:TPU:0, one launch (start us, length us, event | category | flops | bytes accessed | tf_op | source)
XLA Modules:
  0.0 29.8 jit_solution(9761062661647943177)
XLA Ops:
  0.0 0.0 copy-start
  0.0 1.2 %copy-done = bf16[16,16,16,128]{3,2,1,0:T(8,128)(2,1)S(1)} copy-done((bf16[16,16,16,128]{3,2,1,0:T(8,128)(2,1)S(1)}, bf16[16,16,16,128]{3,2,1,0:T(8,128)(2,1)}, u32[]{:S(2)}) %copy-start) | copy-done | bytes 1048600
  1.2 0.0 copy-start.1
  1.2 0.0 copy-start.3
  1.2 0.0 copy-start.4
  1.2 1.2 %edges_kernel.1 = (bf16[320,128]{1,0:T(8,128)(2,1)S(1)}, bf16[320,128]{1,0:T(8,128)(2,1)S(1)}, bf16[32,128]{1,0:T(8,128)(2,1)S(1)}) custom-call(bf16[16,16,16,128]{3,2,1,0:T(8,128)(2,1)S(1)} %copy-done), custom_call_target="tpu_custom_call" | custom-call | bytes 1048576 | tf_op jit(solution)/shard_map/edges/edges_kernel/pallas_call | solution.py:425
  2.5 3.0 %collective-permute-start = (bf16[320,128]{1,0:T(8,128)(2,1)S(1)}, bf16[320,128]{1,0:T(8,128)(2,1)S(1)}, u32[]{:S(2)}, u32[]{:S(2)}) collective-permute-start(bf16[320,128]{1,0:T(8,128)(2,1)S(1)} %get-tuple-element.21), channel_id=1, source_target_pairs={{0,8},{8,0},{16,24},{24,16},{1,9},{9,1},{17,25},{25,17},{2,10},{10... | collective-permute-start | bytes 245768 | tf_op jit(solution)/shard_map/xedge/ppermute | solution.py:428
  5.5 1.5 %collective-permute-start.1 = (bf16[320,128]{1,0:T(8,128)(2,1)S(1)}, bf16[320,128]{1,0:T(8,128)(2,1)S(1)}, u32[]{:S(2)}, u32[]{:S(2)}) collective-permute-start(bf16[320,128]{1,0:T(8,128)(2,1)S(1)} %get-tuple-element.22), channel_id=1, source_target_pairs={{8,16},{16,8},{0,24},{24,0},{9,17},{17,9},{1,25},{25,1},{10,18},{1... | collective-permute-start | bytes 245768 | tf_op jit(solution)/shard_map/xedge/ppermute | solution.py:428
  6.9 0.0 collective-permute-start.5
  7.0 0.2 faces_kernel.1
  7.2 2.1 %collective-permute-start.3 = (bf16[16,80,128]{2,1,0:T(8,128)(2,1)S(1)}, bf16[16,80,128]{2,1,0:T(8,128)(2,1)S(1)}, u32[]{:S(2)}, u32[]{:S(2)}) collective-permute-start(bf16[16,80,128]{2,1,0:T(8,128)(2,1)S(1)} %get-tuple-element.28), channel_id=1, source_target_pairs={{0,1},{1,0},{2,3},{3,2},{4,5},{5,4},{6,7},{7,6},{8,9},{9,8},{10,11... | collective-permute-start | bytes 983048 | tf_op jit(solution)/shard_map/zface/ppermute | solution.py:428
  9.3 0.7 %collective-permute-start.4 = (bf16[16,80,128]{2,1,0:T(8,128)(2,1)S(1)}, bf16[16,80,128]{2,1,0:T(8,128)(2,1)S(1)}, u32[]{:S(2)}, u32[]{:S(2)}) collective-permute-start(bf16[16,80,128]{2,1,0:T(8,128)(2,1)S(1)} %get-tuple-element.29), channel_id=1, source_target_pairs={{1,2},{2,1},{5,6},{6,5},{9,10},{10,9},{13,14},{14,13},{17,18},{18,... | collective-permute-start | bytes 983048 | tf_op jit(solution)/shard_map/zface/ppermute | solution.py:428
  10.0 1.2 %collective-permute-done.5.refs_3_ = bf16[32,128]{1,0:T(8,128)(2,1)S(1)} collective-permute-done((bf16[32,128]{1,0:T(8,128)(2,1)S(1)}, bf16[32,128]{1,0:T(8,128)(2,1)S(1)}, u32[]{:S(2)}, u32[]{:S(2)}) %collective-permute-start.5) | collective-permute-done | bytes 8224 | tf_op jit(solution)/shard_map/across/ppermute | solution.py:445
  11.2 0.0 collective-permute-done.refs_3_.refs_0_
  11.2 0.0 collective-permute-done.1.refs_4_.refs_1_
  11.2 3.7 %collective-permute-start.7 = (bf16[192,128]{1,0:T(8,128)(2,1)S(1)}, bf16[192,128]{1,0:T(8,128)(2,1)S(1)}, u32[]{:S(2)}, u32[]{:S(2)}) collective-permute-start(bf16[192,128]{1,0:T(8,128)(2,1)S(1)} %get-tuple-element.32), channel_id=1, source_target_pairs={{1,2},{2,1},{0,3},{3,0},{5,6},{6,5},{4,7},{7,4},{9,10},{10,9},{8,1... | collective-permute-start | bytes 147464 | tf_op jit(solution)/shard_map/zcorner/ppermute | solution.py:428
  14.9 0.0 copy-done.1
  14.9 0.0 copy-done.3
  14.9 0.0 copy-done.4
  14.9 2.5 %own_kernel.1 = (bf16[384,256]{1,0:T(8,128)(2,1)S(1)}, bf16[512,2048]{1,0:T(8,128)(2,1)S(1)}, bf16[96,2048]{1,0:T(8,128)(2,1)S(1)}) custom-call(f32[3,9]{1,0:T(4,128)S(1)} %copy-done.3, f32[3,9]{1,0:T(4,128)S(1)} %copy-done.4, bf16[16,16,16,128]{3,2,1,0:T(8,128)(2,1)S(1)} %copy-done.1, bf16[320,128]{1,0:T(8,128)(2,1)S(1)} %collective-permute-done.refs_3_.refs_0_, ...), custom_call_target="tpu_custom_call" | custom-call | flops 805306368 | bytes 1048576 | tf_op jit(solution)/shard_map/own/own_kernel/pallas_call | solution.py:425
  17.4 0.0 copy-start.2
  17.4 0.1 collective-permute-start.2
  17.5 0.1 collective-permute-start.6
  17.6 1.9 %collective-permute-done.7.refs_4_ = bf16[192,128]{1,0:T(8,128)(2,1)S(1)} collective-permute-done((bf16[192,128]{1,0:T(8,128)(2,1)S(1)}, bf16[192,128]{1,0:T(8,128)(2,1)S(1)}, u32[]{:S(2)}, u32[]{:S(2)}) %collective-permute-start.7) | collective-permute-done | bytes 49184 | tf_op jit(solution)/shard_map/zcorner/ppermute | solution.py:428
  19.5 4.8 %collective-permute-start.9 = (bf16[32,128]{1,0:T(8,128)(2,1)S(1)}, bf16[32,128]{1,0:T(8,128)(2,1)S(1)}, u32[]{:S(2)}, u32[]{:S(2)}) collective-permute-start(bf16[32,128]{1,0:T(8,128)(2,1)S(1)} %get-tuple-element.36), channel_id=1, source_target_pairs={{0,2},{1,3},{2,0},{3,1},{4,6},{5,7},{6,4},{7,5},{8,10},{9,11},{10,... | collective-permute-start | bytes 24584 | tf_op jit(solution)/shard_map/zacross/ppermute | solution.py:455
  24.3 0.0 collective-permute-done.6.refs_3_
  24.3 0.0 collective-permute-done.3.refs_1_
  24.3 0.0 collective-permute-done.4.refs_2_
  24.3 1.1 %sides_kernel.1 = (bf16[144,2048]{1,0:T(8,128)(2,1)S(1)}, bf16[144,2048]{1,0:T(8,128)(2,1)S(1)}, bf16[64,2048]{1,0:T(8,128)(2,1)S(1)}) custom-call(bf16[384,256]{1,0:T(8,128)(2,1)S(1)} %get-tuple-element.27.refs_0_, bf16[16,80,128]{2,1,0:T(8,128)(2,1)S(1)} %collective-permute-done.3.refs_1_, bf16[16,80,128]{2,1,0:T(8,128)(2,1)S(1)} %collective-permute-done.4.refs_2_, ...), custom_call_target="tpu_custom_call" | custom-call | bytes 1048576 | tf_op jit(solution)/shard_map/sides/sides_kernel/pallas_call | solution.py:425
  25.4 0.1 collective-permute-start.8
  25.4 0.5 %collective-permute-done.9 = bf16[32,128]{1,0:T(8,128)(2,1)S(1)} collective-permute-done((bf16[32,128]{1,0:T(8,128)(2,1)S(1)}, bf16[32,128]{1,0:T(8,128)(2,1)S(1)}, u32[]{:S(2)}, u32[]{:S(2)}) %collective-permute-start.9) | collective-permute-done | bytes 8224 | tf_op jit(solution)/shard_map/zacross/ppermute | solution.py:455
  25.9 0.1 collective-permute-start.10
  26.0 1.3 %partial_kernel.1 = (f32[256,2048]{1,0:T(8,128)S(1)}, bf16[256,512]{1,0:T(8,128)(2,1)S(1)}) custom-call(f32[3,9]{1,0:T(4,128)S(1)} %copy-done.3, f32[3,9]{1,0:T(4,128)S(1)} %copy-done.4, bf16[512,2048]{1,0:T(8,128)(2,1)S(1)} %get-tuple-element.23.refs_2_), custom_call_target="tpu_custom_call" | custom-call | flops 536870912 | bytes 1048576 | tf_op jit(solution)/shard_map/partial/partial_kernel/pallas_call | solution.py:425
  27.4 0.0 collective-permute-done.10
  27.4 0.0 collective-permute-done.2.refs_2_
  27.4 0.0 collective-permute-done.8.refs_5_
  27.4 0.0 copy-done.2
  27.4 2.3 %final_kernel.1 = bf16[16,16,16,128]{3,2,1,0:T(8,128)(2,1)} custom-call(f32[256,2048]{1,0:T(8,128)S(1)} %get-tuple-element.24.refs_0_, bf16[256,512]{1,0:T(8,128)(2,1)S(1)} %get-tuple-element.25.refs_1_, bf16[96,2048]{1,0:T(8,128)(2,1)S(1)} %collective-permute-done.2.refs_2_, bf16[144,2048]{1,0:T(8,128)(2,1)S(1)} %get-tuple-element.33.refs_3_, ...), custom_call_target="tpu_custom_call" | custom-call | bytes 1048576 | tf_op jit(solution)/shard_map/final/final_kernel/pallas_call | solution.py:425
  (5 shorter events, 0.0 us)
Async XLA Ops:
  0.0 1.2 %copy-start = (bf16[16,16,16,128]{3,2,1,0:T(8,128)(2,1)S(1)}, bf16[16,16,16,128]{3,2,1,0:T(8,128)(2,1)}, u32[]{:S(2)}) copy-start(bf16[16,16,16,128]{3,2,1,0:T(8,128)(2,1)} %refs_0_.7) | copy-start | bytes 3145732
  1.2 13.7 %copy-start.1 = (bf16[16,16,16,128]{3,2,1,0:T(8,128)(2,1)S(1)}, bf16[16,16,16,128]{3,2,1,0:T(8,128)(2,1)}, u32[]{:S(2)}) copy-start(bf16[16,16,16,128]{3,2,1,0:T(8,128)(2,1)} %refs_0_.7) | copy-start | bytes 3145732
  1.2 13.7 %copy-start.3 = (f32[3,9]{1,0:T(4,128)S(1)}, f32[3,9]{1,0:T(4,128)}, u32[]{:S(2)}) copy-start(f32[3,9]{1,0:T(4,128)} %refs_0_.6) | copy-start | bytes 328
  1.2 13.7 %copy-start.4 = (f32[3,9]{1,0:T(4,128)S(1)}, f32[3,9]{1,0:T(4,128)}, u32[]{:S(2)}) copy-start(f32[3,9]{1,0:T(4,128)} %refs_1_.3) | copy-start | bytes 328
  2.5 8.7 %collective-permute-start = (bf16[320,128]{1,0:T(8,128)(2,1)S(1)}, bf16[320,128]{1,0:T(8,128)(2,1)S(1)}, u32[]{:S(2)}, u32[]{:S(2)}) collective-permute-start(bf16[320,128]{1,0:T(8,128)(2,1)S(1)} %get-tuple-element.21), channel_id=1, source_target_pairs={{0,8},{8,0},{16,24},{24,16},{1,9},{9,1},{17,25},{25,17},{2,10},{10... | collective-permute-start | bytes 245768 | tf_op jit(solution)/shard_map/xedge/ppermute | solution.py:428
  5.5 5.7 %collective-permute-start.1 = (bf16[320,128]{1,0:T(8,128)(2,1)S(1)}, bf16[320,128]{1,0:T(8,128)(2,1)S(1)}, u32[]{:S(2)}, u32[]{:S(2)}) collective-permute-start(bf16[320,128]{1,0:T(8,128)(2,1)S(1)} %get-tuple-element.22), channel_id=1, source_target_pairs={{8,16},{16,8},{0,24},{24,0},{9,17},{17,9},{1,25},{25,1},{10,18},{1... | collective-permute-start | bytes 245768 | tf_op jit(solution)/shard_map/xedge/ppermute | solution.py:428
  6.9 4.3 %collective-permute-start.5 = (bf16[32,128]{1,0:T(8,128)(2,1)S(1)}, bf16[32,128]{1,0:T(8,128)(2,1)S(1)}, u32[]{:S(2)}, u32[]{:S(2)}) collective-permute-start(bf16[32,128]{1,0:T(8,128)(2,1)S(1)} %get-tuple-element.30.refs_2_), channel_id=1, source_target_pairs={{0,16},{8,24},{16,0},{24,8},{1,17},{9,25},{17,1},{25,9},{2,18},{10... | collective-permute-start | bytes 24584 | tf_op jit(solution)/shard_map/across/ppermute | solution.py:445
  7.2 17.1 %collective-permute-start.3 = (bf16[16,80,128]{2,1,0:T(8,128)(2,1)S(1)}, bf16[16,80,128]{2,1,0:T(8,128)(2,1)S(1)}, u32[]{:S(2)}, u32[]{:S(2)}) collective-permute-start(bf16[16,80,128]{2,1,0:T(8,128)(2,1)S(1)} %get-tuple-element.28), channel_id=1, source_target_pairs={{0,1},{1,0},{2,3},{3,2},{4,5},{5,4},{6,7},{7,6},{8,9},{9,8},{10,11... | collective-permute-start | bytes 983048 | tf_op jit(solution)/shard_map/zface/ppermute | solution.py:428
  9.3 15.0 %collective-permute-start.4 = (bf16[16,80,128]{2,1,0:T(8,128)(2,1)S(1)}, bf16[16,80,128]{2,1,0:T(8,128)(2,1)S(1)}, u32[]{:S(2)}, u32[]{:S(2)}) collective-permute-start(bf16[16,80,128]{2,1,0:T(8,128)(2,1)S(1)} %get-tuple-element.29), channel_id=1, source_target_pairs={{1,2},{2,1},{5,6},{6,5},{9,10},{10,9},{13,14},{14,13},{17,18},{18,... | collective-permute-start | bytes 983048 | tf_op jit(solution)/shard_map/zface/ppermute | solution.py:428
  11.2 8.3 %collective-permute-start.7 = (bf16[192,128]{1,0:T(8,128)(2,1)S(1)}, bf16[192,128]{1,0:T(8,128)(2,1)S(1)}, u32[]{:S(2)}, u32[]{:S(2)}) collective-permute-start(bf16[192,128]{1,0:T(8,128)(2,1)S(1)} %get-tuple-element.32), channel_id=1, source_target_pairs={{1,2},{2,1},{0,3},{3,0},{5,6},{6,5},{4,7},{7,4},{9,10},{10,9},{8,1... | collective-permute-start | bytes 147464 | tf_op jit(solution)/shard_map/zcorner/ppermute | solution.py:428
  17.4 10.0 %copy-start.2 = (bf16[2,2,16,2048]{3,2,1,0:T(8,128)(2,1)S(1)}, bf16[2,2,16,2048]{3,2,1,0:T(8,128)(2,1)}, u32[]{:S(2)}) copy-start(bf16[2,2,16,2048]{3,2,1,0:T(8,128)(2,1)} %param.7) | copy-start | bytes 786436
  17.4 10.0 %collective-permute-start.2 = (bf16[96,2048]{1,0:T(8,128)(2,1)S(1)}, bf16[96,2048]{1,0:T(8,128)(2,1)S(1)}, u32[]{:S(2)}, u32[]{:S(2)}) collective-permute-start(bf16[96,2048]{1,0:T(8,128)(2,1)S(1)} %get-tuple-element.26), channel_id=1, source_target_pairs={{0,4},{4,0},{1,5},{5,1},{2,6},{6,2},{3,7},{7,3},{8,12},{12,8},{9,1... | collective-permute-start | bytes 1179656 | tf_op jit(solution)/shard_map/yown/ppermute | solution.py:428
  17.5 6.8 %collective-permute-start.6 = (bf16[192,128]{1,0:T(8,128)(2,1)S(1)}, bf16[192,128]{1,0:T(8,128)(2,1)S(1)}, u32[]{:S(2)}, u32[]{:S(2)}) collective-permute-start(bf16[192,128]{1,0:T(8,128)(2,1)S(1)} %get-tuple-element.31), channel_id=1, source_target_pairs={{0,1},{1,0},{2,3},{3,2},{4,5},{5,4},{6,7},{7,6},{8,9},{9,8},{10,11... | collective-permute-start | bytes 147464 | tf_op jit(solution)/shard_map/zcorner/ppermute | solution.py:428
  19.5 6.4 %collective-permute-start.9 = (bf16[32,128]{1,0:T(8,128)(2,1)S(1)}, bf16[32,128]{1,0:T(8,128)(2,1)S(1)}, u32[]{:S(2)}, u32[]{:S(2)}) collective-permute-start(bf16[32,128]{1,0:T(8,128)(2,1)S(1)} %get-tuple-element.36), channel_id=1, source_target_pairs={{0,2},{1,3},{2,0},{3,1},{4,6},{5,7},{6,4},{7,5},{8,10},{9,11},{10,... | collective-permute-start | bytes 24584 | tf_op jit(solution)/shard_map/zacross/ppermute | solution.py:455
  25.4 2.0 %collective-permute-start.8 = (bf16[64,2048]{1,0:T(8,128)(2,1)S(1)}, bf16[64,2048]{1,0:T(8,128)(2,1)S(1)}, u32[]{:S(2)}, u32[]{:S(2)}) collective-permute-start(bf16[64,2048]{1,0:T(8,128)(2,1)S(1)} %get-tuple-element.35), channel_id=1, source_target_pairs={{0,4},{4,0},{1,5},{5,1},{2,6},{6,2},{3,7},{7,3},{8,12},{12,8},{9,1... | collective-permute-start | bytes 786440 | tf_op jit(solution)/shard_map/yside/ppermute | solution.py:428
  25.9 1.4 %collective-permute-start.10 = (bf16[1,4,32,128]{3,2,1,0:T(8,128)(2,1)S(1)}, bf16[1,4,32,128]{3,2,1,0:T(8,128)(2,1)S(1)}, u32[]{:S(2)}, u32[]{:S(2)}) collective-permute-start(bf16[1,4,32,128]{3,2,1,0:T(8,128)(2,1)S(1)} %maximum_bitcast_fusion), channel_id=1, source_target_pairs={{0,4},{4,0},{1,5},{5,1},{2,6},{6,2},{3,7},{7,3},{8,12},{12,8},{9,1... | collective-permute-start | bytes 98312 | tf_op jit(solution)/shard_map/known/ppermute | solution.py:388

commit v4 on v3

--- a/solution.py
+++ b/solution.py
@@ -4,6 +4,7 @@
 from jax.experimental import pallas as pl
 from jax.experimental.pallas import tpu as pltpu
 from jax.sharding import PartitionSpec as P
+
 
 F32 = jnp.float32
 BF16 = jnp.bfloat16
@@ -74,6 +75,7 @@
         self.tile = self.ty * self.tx * self.nx
         self.ride = self.nx == 4 and self.nz == 4 and self.tile == self.V * E
         self.edge = self.rows + 2 * self.avg + (self.tz * self.V if self.ride else 0)
+        self.ypack = len(self.kz) * (self.zyf + self.zyc)
         self.chunks = 4 if self.V % 4 == 0 else 1
         self.corner = len(self.kx) * self.face + (self.tz * self.V if self.ride else 0)
 
@@ -84,24 +86,6 @@
 
 def vmem():
     return pl.BlockSpec(memory_space=pltpu.VMEM)
-
-
-def faces_kernel(s, field, *outs):
-    me = lax.axis_index("gz")
-    row = iota((s.avg, s.raw), 0)
-    col = iota((s.avg, s.raw), 1)
-    half = s.Y // 2
-    mean = one((col // s.Y // 2 == row // half) & (col % s.Y // 2 == row % half), 0.25)
-    for kind, out in zip(s.kz, outs):
-        up = upper(me, kind)
-        start = jnp.where(up, s.Z - R, 0)
-        further = jnp.where(up, s.Z - E, R)
-        for v in range(s.V):
-            out[v, : s.raw, :] = field[v, pl.ds(start, R)].reshape(s.raw, s.X)
-        data = wide([field[v, pl.ds(further, R)].reshape(s.raw, s.X) for v in range(s.V)])
-        means = dot(mean, data).astype(BF16)
-        for v in range(s.V):
-            out[v, s.raw :, :] = means[:, v * s.X : (v + 1) * s.X]
 
 
 def corners_kernel(s, *refs):
@@ -128,37 +112,56 @@
             out[n * s.face :, :] = total.astype(BF16)
 
 
-def edges_kernel(s, field, *refs):
+def front_kernel(s, field, *refs):
     gx = lax.axis_index("gx")
-    n = len(s.kx)
-    edges, piece = refs[:n], refs[n]
-    chunk = s.V // s.chunks
+    n, m = len(s.kx), len(s.kz)
+    faces, edges, (piece, held, sem) = refs[:m], refs[m : m + n], refs[m + n :]
+    copy = pltpu.make_async_copy(field, held, sem)
+    copy.start()
     half = s.Y // 2
     deep, tall, long = s.Z // s.tz, s.Y // s.ty, s.X // s.tx
-    row = iota((chunk * s.X, s.V * E), 0)
-    lane = iota((chunk * s.X, s.V * E), 1)
-    own_v, own_x = row // s.X, row % s.X
-    r, c = iota((8, s.rows), 0), iota((8, s.rows), 1)
-    pool = one(c // s.Y // deep * s.ty + c % s.Y // tall == r, 1.0 / (deep * tall))
+    x, lane = iota((s.X, s.V * E), 0), iota((s.X, s.V * E), 1)
+    picks = [one(x - jnp.where(upper(gx, kind), s.X - E, 0) == lane % E) for kind in s.kx]
+    group = iota((1, s.V * E), 1) // E
+    by_v = [
+        wide([jnp.where(group == lane_group(s, j, v), p, jnp.zeros_like(p)) for j, p in enumerate(picks)])
+        for v in range(s.V)
+    ]
     sub = iota((s.V, s.X), 0)
-    first = [jnp.where(upper(gx, kind), s.X - E, 0) for kind in s.kx]
-    packed = [jnp.zeros((s.rows, s.V * E), F32) for kind in s.kx]
+    copy.wait()
+    found = dot(
+        wide([held[v].reshape(s.rows, s.X) for v in range(s.V)]), jnp.concatenate(by_v, axis=0)
+    )
     by_vector = [jnp.zeros((s.V, s.X), F32) for _ in range(s.tz * s.ty)]
-    for i in range(s.chunks):
-        data = wide([field[v].reshape(s.rows, s.X) for v in range(i * chunk, (i + 1) * chunk)])
-        for j in range(n):
-            pick = one((own_v + i * chunk == lane // E) & (own_x - first[j] == lane % E))
-            packed[j] = packed[j] + dot(data, pick)
-        sums = dot(pool, data)
-        for p in range(s.tz * s.ty):
-            for v in range(chunk):
-                line = jnp.broadcast_to(sums[p : p + 1, v * s.X : (v + 1) * s.X], (s.V, s.X))
-                by_vector[p] = jnp.where(sub == v + i * chunk, line, by_vector[p])
+    for v in range(s.V):
+        for i in range(s.tz):
+            layers = held[v, i * deep].astype(F32)
+            for z in range(i * deep + 1, (i + 1) * deep):
+                layers = layers + held[v, z].astype(F32)
+            for j in range(s.ty):
+                line = jnp.sum(layers[j * tall : (j + 1) * tall], axis=0, keepdims=True)
+                line = jnp.broadcast_to(line * (1.0 / (deep * tall)), (s.V, s.X))
+                by_vector[i * s.ty + j] = jnp.where(sub == v, line, by_vector[i * s.ty + j])
+    gz = lax.axis_index("gz")
+    row = iota((s.avg, s.raw), 0)
+    col = iota((s.avg, s.raw), 1)
+    half = s.Y // 2
+    mean = one((col // s.Y // 2 == row // half) & (col % s.Y // 2 == row % half), 0.25)
+    for kind, out in zip(s.kz, faces):
+        up = upper(gz, kind)
+        start = jnp.where(up, s.Z - R, 0)
+        further = jnp.where(up, s.Z - E, R)
+        for v in range(s.V):
+            out[v, : s.raw, :] = held[v, pl.ds(start, R)].reshape(s.raw, s.X)
+        data = wide([held[v, pl.ds(further, R)].reshape(s.raw, s.X) for v in range(s.V)])
+        means = dot(mean, data).astype(BF16)
+        for v in range(s.V):
+            out[v, s.raw :, :] = means[:, v * s.X : (v + 1) * s.X]
     r, c = iota((2 * s.avg, s.rows), 0), iota((2 * s.avg, s.rows), 1)
     layer = r // half * 2 + jnp.where(r < s.avg, R, s.Z - E - R)
     mean = one((c // s.Y // 2 * 2 == layer) & (c % s.Y // 2 == r % half), 0.25)
     for j in range(n):
-        edge = packed[j].astype(BF16)
+        edge = found[:, j * s.V * E : (j + 1) * s.V * E].astype(BF16)
         edges[j][: s.rows, :] = edge
         edges[j][s.rows : s.rows + 2 * s.avg, :] = dot(mean, edge).astype(BF16)
     x, lane = iota((s.X, s.tile), 0), iota((s.X, s.tile), 1)
@@ -177,20 +180,24 @@
 
 def x_weights(s, fine, coarse):
     gx = lax.axis_index("gx")
-    blocks = []
-
-    def block(place, count):
+
+    def rows(place, count):
         col = iota((count, s.X), 1)
         a = lookup(place - col + R, fine, 2)
-        b = 0.5 * lookup((place + E) // 2 - R - col // 2 + R, coarse, 2)
-        blocks.append(wide([a, b]).astype(BF16))
-
-    block(iota((s.X, s.X), 0), s.X)
+        b = 0.5 * lookup((place + E) // 2 - col // 2, coarse, 2)
+        return wide([a, b])
+
+    half = s.V // 2
+    own = rows(iota((s.X, s.X), 0), s.X).astype(BF16)
+    sides = []
     for kind in s.kx:
-        c = iota((s.V * E, s.X), 0) % E
+        c = iota((E, s.X), 0)
         place = jnp.where(upper(gx, kind), s.X + c, c - E)
-        block(jnp.where(partner_missing(gx, s.nx, kind), -4 * s.X, place), s.V * E)
-    return jnp.concatenate(blocks, axis=0)
+        place = jnp.where(partner_missing(gx, s.nx, kind), -4 * s.X, place)
+        sides.append(jnp.concatenate([rows(place, E)] * half, axis=0).astype(BF16))
+    if len(sides) < 2:
+        sides += [jnp.zeros((half * E, 2 * s.X), BF16)] * (2 - len(sides))
+    return [jnp.concatenate([own] + order, axis=0) for order in (sides, sides[::-1])]
 
 
 def pick_y(s, up, fine):
@@ -218,19 +225,23 @@
 
 
 def xpass(s, weights, data, halos, v):
-    lane_v = iota((1, s.V * E), 1) // E
-    masked = [jnp.where(lane_v == v, h, jnp.zeros_like(h)) for h in halos]
-    return dot(wide([data] + masked), weights).astype(BF16)
-
-
-def own_kernel(s, *refs):
-    fine, coarse, field, *refs = refs
+    group = iota((1, s.V * E), 1) // E
+    mixed = jnp.zeros((data.shape[0], s.V * E), BF16)
+    for i, halo in enumerate(halos):
+        mixed = jnp.where(group == lane_group(s, i, v), halo, mixed)
+    return dot(wide([data, mixed]), weights[v // (s.V // 2)]).astype(BF16)
+
+
+def lane_group(s, place, v):
+    return (v + place * (s.V // 2)) % s.V
+
+
+def own_kernel(s, weights, field, *refs):
     n = len(s.kx)
-    halos, (weights, own, *packs) = [h[: s.rows, :] for h in refs[:n]], refs[n:]
-    weights[...] = x_weights(s, fine, coarse)
+    halos, (own, *packs) = [h[: s.rows, :] for h in refs[:n]], refs[n:]
     for v in range(s.V):
         at = slice(v * s.X, (v + 1) * s.X)
-        passed = xpass(s, weights[...], field[v].reshape(s.rows, s.X), halos, v)
+        passed = xpass(s, weights, field[v].reshape(s.rows, s.X), halos, v)
         own[: s.rows, at] = passed[:, : s.X]
         own[s.rows :, at] = passed[:, s.X :]
     gy = lax.axis_index("gy")
@@ -242,7 +253,8 @@
 
 def sides_kernel(s, weights, *refs):
     m = len(s.kz)
-    faces, corners, sides, packs = refs[:m], refs[m : 2 * m], refs[2 * m : 3 * m], refs[3 * m :]
+    faces, corners, refs = refs[:m], refs[m : 2 * m], refs[2 * m :]
+    sides, packs = refs[:m], refs[m:]
     halos = [
         jnp.concatenate([c[i * s.face : (i + 1) * s.face, :] for c in corners], axis=0)
         for i in range(len(s.kx))
@@ -250,7 +262,7 @@
     for v in range(s.V):
         at = slice(v * s.X, (v + 1) * s.X)
         data = jnp.concatenate([f[v] for f in faces], axis=0)
-        passed = xpass(s, weights[...], data, halos, v)
+        passed = xpass(s, weights, data, halos, v)
         for i, side in enumerate(sides):
             base = i * s.face
             side[: s.raw, at] = passed[base : base + s.raw, : s.X]
@@ -308,30 +320,45 @@
         second.append(block(coarse, z, y, 2, jnp.where(c < s.raw, 0.25, 1.0)))
     for kind in s.ky:
         up = upper(gy, kind)
+        fy, cy = jnp.where(up, s.Y, -R), jnp.where(up, half, -R)
         for zkind in s.kz:
             zup = upper(gz, zkind)
             c = iota((1, s.zyf), 1)
-            z, y = c // R + jnp.where(zup, s.Z, -R), c % R + jnp.where(up, s.Y, -R)
-            second.append(block(fine, zplace(zkind, z), y, 1))
+            z = zplace(zkind, c // R + jnp.where(zup, s.Z, -R))
+            second.append(block(fine, z, c % R + fy, 1))
             c = iota((1, s.zyc), 1)
             q = c // R
             near = q + jnp.where(zup, deep, -R // 2)
             far = q - R // 2 + jnp.where(zup, deep + R // 2, -R)
-            z, y = jnp.where(q < R // 2, near, far), c % R + jnp.where(up, half, -R)
-            second.append(block(coarse, zplace(zkind, z), y, 2))
+            z = zplace(zkind, jnp.where(q < R // 2, near, far))
+            second.append(block(coarse, z, c % R + cy, 2))
     r, c = iota((s.rows, s.top), 0), iota((s.rows, s.top), 1)
     z, y = r // s.Y // (s.Z // s.tz), r % s.Y // (s.Y // s.ty)
     second.append(one(c // s.tx == z * s.ty + y))
     return first, second
 
 
-def partial_kernel(s, fine, coarse, own, total, later, now):
+def top_product(s, kernel, parts, total):
+    for z, y, part in parts:
+        for i in range(s.tz):
+            q = pl.multiple_of(((z * s.tz + i) * s.ny + y) * s.tile, s.tile)
+            rows = part(slice(i * s.V, (i + 1) * s.V), i)
+            total = total + dot(kernel[:, pl.ds(q, s.tile)], rows, ((1,), (1,)))
+    return total
+
+
+def weights_kernel(s, fine, coarse, x, now, later):
+    for i, block in enumerate(x_weights(s, fine, coarse)):
+        x[i] = block
     first, second = yz_weights(s, fine, coarse)
     for ref, blocks in ((now, first), (later, second)):
         at = 0
         for block in blocks:
             ref[:, at : at + block.shape[1]] = block
             at += block.shape[1]
+
+
+def partial_kernel(s, now, own, total):
     step = min(s.lanes, 4 * s.X)
     for at in range(0, s.lanes, step):
         cols = slice(at, at + step)
@@ -344,28 +371,30 @@
     ends, refs = refs[:k], refs[k:]
     sides, refs = refs[:m], refs[m:]
     packs, refs = refs[:k], refs[k:]
-    gathered, kernel, out, held, sems = refs
+    known, kernel, out, held, sems = refs
     gy, gz = lax.axis_index("gy"), lax.axis_index("gz")
-    total = jnp.zeros((s.top, s.V), F32)
-    for z in range(s.nz):
-        for y in range(s.ny):
-            for i in range(s.tz):
-                part = gathered[slot(y, gy, s.ny), slot(z, gz, s.nz), i * s.V : (i + 1) * s.V, :]
-                q = ((z * s.tz + i) * s.ny + y) * s.tile
-                total = total + dot(kernel[:, q : q + s.tile], part, ((1,), (1,)))
+    parts = [
+        (slot(z, gz, s.nz), slot(y, gy, s.ny), lambda at, i, y=y, z=z: known[y, z, at, :])
+        for y in range(s.ny)
+        for z in range(s.nz)
+    ]
+    total = top_product(s, kernel, parts, jnp.zeros((s.top, s.V), F32))
     r, c = iota((s.top, s.X), 0), iota((s.top, s.X), 1)
     spread = c // (s.X // s.tx) == r % s.tx
     chunk = s.V // s.chunks
     copies = []
-    for v in range(s.V):
-        cols = slice(v * s.X, (v + 1) * s.X)
-        line = jnp.broadcast_to(total[:, v : v + 1], (s.top, s.X))
-        top = jnp.where(spread, line, 0.0).astype(BF16)
-        parts = [x[:, cols] for x in (*ends, *sides, *packs)] + [top]
-        result = dot(later[...], jnp.concatenate(parts, axis=0)) + partial[:, cols]
-        held[v] = result.astype(BF16).reshape(s.Z, s.Y, s.X)
-        if v % chunk == chunk - 1:
-            at = pl.ds(v + 1 - chunk, chunk)
+    pair = 2 if chunk % 2 == 0 else 1
+    for v in range(0, s.V, pair):
+        cols = slice(v * s.X, (v + pair) * s.X)
+        lines = [jnp.broadcast_to(total[:, v + i : v + i + 1], (s.top, s.X)) for i in range(pair)]
+        top = wide([jnp.where(spread, line, 0.0).astype(BF16) for line in lines])
+        parts = [x[:, cols] for x in (*ends, *sides)]
+        parts += [x[:, cols] for x in packs] + [top]
+        result = (dot(later[...], jnp.concatenate(parts, axis=0)) + partial[:, cols]).astype(BF16)
+        for i in range(pair):
+            held[v + i] = result[:, i * s.X : (i + 1) * s.X].reshape(s.Z, s.Y, s.X)
+        if (v + pair) % chunk == 0:
+            at = pl.ds(v + pair - chunk, chunk)
             copies.append(pltpu.make_async_copy(held.at[at], out.at[at], sems.at[v // chunk]))
             copies[-1].start()
     for copy in copies:
@@ -376,8 +405,8 @@
     return count & (count - 1) == 0
 
 
-def slot(index, me, count):
-    return index ^ me if doubling(count) else index
+def slot(place, me, count):
+    return place ^ me if doubling(count) else place
 
 
 def gather(a, axis, count, join):
@@ -414,7 +443,6 @@
             specs[i] = pl.BlockSpec(memory_space=pltpu.HBM)
         call = pl.pallas_call(
             bind(body, s),
-            name=body.__name__,
             out_shape=outs,
             in_specs=specs,
             out_specs=[pl.BlockSpec(memory_space=pltpu.HBM) if far_out else vmem()] * len(outs),
@@ -427,77 +455,74 @@
     def swap(arrays, axis, count, which, ring=False):
         return [lax.ppermute(a, axis, swaps(count, kind, ring)) for a, kind in zip(arrays, which)]
 
-    taps = [fine_taps, coarse_taps]
     buffers = [pltpu.VMEM(field.shape, BF16), pltpu.SemaphoreType.DMA((s.chunks,))]
     top = shape(s.tz * s.V, s.tile)
-    with jax.named_scope("faces"):
-        faces = run(faces_kernel, [field], [shape(s.V, s.face, s.X)] * m)
-    with jax.named_scope("zface"):
-        faces = swap(faces, "gz", s.nz, s.kz)
-    with jax.named_scope("edges"):
-        *edges, piece = run(edges_kernel, [field], [shape(s.edge, s.V * E)] * n + [top])
-    with jax.named_scope("xedge"):
-        halos = swap(edges, "gx", s.nx, s.kx, s.ride)
+    outs = [shape(s.V, s.face, s.X)] * m + [shape(s.edge, s.V * E)] * n + [top]
+    *faces, field = run(
+        front_kernel,
+        [pltpu.with_memory_space_constraint(field, pltpu.HBM)],
+        outs + [shape(*field.shape)],
+        scratch=[pltpu.SemaphoreType.DMA],
+        far=(0,),
+    )
+    faces, edges, piece = faces[:m], faces[m : m + n], faces[-1]
+    halos = swap(edges, "gx", s.nx, s.kx, s.ride)
+    faces = swap(faces, "gz", s.nz, s.kz)
     corner = [shape(s.corner, s.V * E)] * m
     stack = lambda parts: jnp.concatenate(parts, axis=0)
     if s.ride:
-        with jax.named_scope("across"):
-            across = lax.ppermute(piece, "gx", [(i, i ^ 2) for i in range(s.nx)])
-        with jax.named_scope("corners"):
-            *corners, known = run(corners_kernel, halos + [piece, across], corner + [top])
+        across = lax.ppermute(piece, "gx", [(i, i ^ 2) for i in range(s.nx)])
+        *corners, known = run(corners_kernel, halos + [piece, across], corner + [top])
     else:
-        with jax.named_scope("corners"):
-            corners = run(corners_kernel, halos, corner)
-    with jax.named_scope("zcorner"):
-        corners = swap(corners, "gz", s.nz, s.kz, s.ride)
+        corners = run(corners_kernel, halos, corner)
+    corners = swap(corners, "gz", s.nz, s.kz, s.ride)
     if s.ride:
-        with jax.named_scope("zacross"):
-            across = lax.ppermute(known, "gz", [(i, i ^ 2) for i in range(s.nz)])
+        across = lax.ppermute(known, "gz", [(i, i ^ 2) for i in range(s.nz)])
         near, far = [c[n * s.face :] for c in corners]
         known = jnp.stack([known, near, across, far])
     else:
         known = gather(gather(piece, "gx", s.nx, sum)[None], "gz", s.nz, stack)
-    with jax.named_scope("known"):
-        known = gather(known[None], "gy", s.ny, stack)
-    x_depth = s.X + n * s.V * E
-    with jax.named_scope("own"):
-        weights, own, *ends = run(
-            own_kernel,
-            taps + [field] + halos,
-            [shape(x_depth, 2 * s.X), shape(2 * s.rows, s.lanes)]
-            + [shape(s.yf + s.yc, s.lanes)] * k,
-            scalars=2,
-            flops=4 * s.rows * s.V * x_depth * s.X,
-        )
-    with jax.named_scope("yown"):
-        ends = swap(ends, "gy", s.ny, s.ky)
-    later = k * (s.yf + s.yc) + m * s.gz + k * m * (s.zyf + s.zyc) + s.top
-    with jax.named_scope("partial"):
-        partial, w_later = run(
-            partial_kernel,
-            taps + [own],
-            [jax.ShapeDtypeStruct((s.rows, s.lanes), F32), shape(s.rows, later)],
-            scalars=2,
-            scratch=[pltpu.VMEM((s.rows, 2 * s.rows), BF16)],
-            flops=4 * s.rows * s.rows * s.lanes,
-        )
-    with jax.named_scope("sides"):
-        rest = run(
-            sides_kernel,
-            [weights] + faces + corners,
-            [shape(s.gz, s.lanes)] * m + [shape(m * (s.zyf + s.zyc), s.lanes)] * k,
-        )
-    with jax.named_scope("yside"):
-        sides, packs = rest[:m], swap(rest[m:], "gy", s.ny, s.ky)
+    x_depth = s.X + s.V * E
+    later = k * (s.yf + s.yc) + m * s.gz + k * s.ypack + s.top
+    weights, w_now, w_later = run(
+        weights_kernel,
+        [pltpu.with_memory_space_constraint(a, pltpu.HBM) for a in (fine_taps, coarse_taps)],
+        [
+            shape(2, x_depth, 2 * s.X),
+            shape(s.rows, 2 * s.rows),
+            shape(s.rows, later),
+        ],
+        scalars=2,
+    )
+    own, *ends = run(
+        own_kernel,
+        [weights, field] + halos,
+        [shape(2 * s.rows, s.lanes)] + [shape(s.yf + s.yc, s.lanes)] * k,
+        flops=4 * s.rows * s.V * x_depth * s.X,
+    )
+    ends = swap(ends, "gy", s.ny, s.ky)
+    rest = run(
+        sides_kernel,
+        [weights] + faces + corners,
+        [shape(s.gz, s.lanes)] * m + [shape(s.ypack, s.lanes)] * k,
+    )
+    sides, packs = rest[:m], rest[m:]
+    packs = swap(packs, "gy", s.ny, s.ky)
+    partial = run(
+        partial_kernel,
+        [w_now, own],
+        [jax.ShapeDtypeStruct((s.rows, s.lanes), F32)],
+        flops=4 * s.rows * s.rows * s.lanes,
+    )[0]
+    known = gather(known[None], "gy", s.ny, stack)
     kernel_rows = top_kernel.reshape(s.top, top_kernel.shape[3])
-    with jax.named_scope("final"):
-        return run(
-            final_kernel,
-            [partial, w_later] + ends + sides + packs + [known, kernel_rows],
-            [shape(*field.shape)],
-            scratch=buffers,
-            far_out=True,
-        )[0]
+    return run(
+        final_kernel,
+        [partial, w_later] + ends + sides + packs + [known, kernel_rows],
+        [shape(*field.shape)],
+        scratch=buffers,
+        far_out=True,
+    )[0]
 
 
 def solution(mesh):

time: 29.9 us -> 29 us (0.970)
  local copies, waits for them, and re-layouts: 1.24 us -> 0.01 us
  Pallas kernels: 8.66 us -> 8.05 us
  starting transfers between devices: 16.1 us -> 16.6 us
  waiting for transfers between devices: 3.65 us -> 3.96 us
    unnamed x10 -> x2, local copies, waits for them, and re-layouts: 1.24 us -> 0.01 us
    ppermute x1, waiting for transfers between devices: 1.22 us -> 0.16 us  [shards(): across = lax.ppermute(piece, 'gx', [(i, i ^ 2) for i in range(s.nx)])]
    pallas_call x7, Pallas kernels: 8.66 us -> 8.05 us  [run(): return list(call(*arrays))]
    ppermute x8, starting transfers between devices: 11.1 us -> 11.7 us  [swap(): lax.ppermute(a, axis, swaps(count, kind, ring))]
    ppermute x8, waiting for transfers between devices: 1.96 us -> 2.54 us  [swap(): lax.ppermute(a, axis, swaps(count, kind, ring))]
    ppermute x1, waiting for transfers between devices: 0.01 us -> 0.47 us  [gather(): a = join([a, lax.ppermute(a, axis, [(i, i ^ step) for i in range(count)])])]
    ppermute x1, waiting for transfers between devices: 0.47 us -> 0.79 us  [shards(): across = lax.ppermute(known, 'gz', [(i, i ^ 2) for i in range(s.nz)])]
  transfers between devices with their start and end apart: 11 -> 11, of which waited for: 3 -> 4; matrix products, arithmetic and copies ran while one was open for 0% -> 0% of each run, Pallas kernels for 17% -> 13%
where the time goes in v4:
time: 29 us; the launch traced here: 28.8 us
  starting transfers between devices  16.6 us (57%)
  Pallas kernels  8.05 us (28%)
  waiting for transfers between devices  3.96 us (14%)
    ppermute x8, starting transfers between devices, swap(): lax.ppermute(a, axis, swaps(count, kind, ring))  11.7 us
    pallas_call x7, Pallas kernels, run(): return list(call(*arrays))  8.05 us
    ppermute x1, starting transfers between devices, shards(): across = lax.ppermute(known, 'gz', [(i, i ^ 2) for i in range(s.nz)])  4.77 us
    ppermute x8, waiting for transfers between devices, swap(): lax.ppermute(a, axis, swaps(count, kind, ring))  2.54 us
    ppermute x1, waiting for transfers between devices, shards(): across = lax.ppermute(known, 'gz', [(i, i ^ 2) for i in range(s.nz)])  0.79 us
  transfers between devices with their start and end apart: 11, of which 4 were waited for; matrix products, arithmetic and copies ran while one was open for 0% of the time, Pallas kernels for 13%

profile of v4, /device:TPU:0, one launch (start us, length us, event | category | flops | bytes accessed | tf_op | source)
XLA Modules:
  0.0 28.8 jit_solution(11958847390069260927)
XLA Ops:
  0.0 2.5 %shard_map.47 = (bf16[16,80,128]{2,1,0:T(8,128)(2,1)S(1)}, bf16[16,80,128]{2,1,0:T(8,128)(2,1)S(1)}, bf16[320,128]{1,0:T(8,128)(2,1)S(1)}, bf16[320,128]{1,0:T(8...) custom-call(bf16[16,16,16,128]{3,2,1,0:T(8,128)(2,1)} %refs_0_.3), custom_call_target="tpu_custom_call" | custom-call | bytes 1048576 | tf_op jit(solution)/shard_map/pallas_call | solution.py:453
  2.5 3.0 %collective-permute-start = (bf16[320,128]{1,0:T(8,128)(2,1)S(1)}, bf16[320,128]{1,0:T(8,128)(2,1)S(1)}, u32[]{:S(2)}, u32[]{:S(2)}) collective-permute-start(bf16[320,128]{1,0:T(8,128)(2,1)S(1)} %get-tuple-element.25), channel_id=1, source_target_pairs={{0,8},{8,0},{16,24},{24,16},{1,9},{9,1},{17,25},{25,17},{2,10},{10... | collective-permute-start | bytes 245768 | tf_op jit(solution)/shard_map/ppermute | solution.py:456
  5.5 1.5 %collective-permute-start.1 = (bf16[320,128]{1,0:T(8,128)(2,1)S(1)}, bf16[320,128]{1,0:T(8,128)(2,1)S(1)}, u32[]{:S(2)}, u32[]{:S(2)}) collective-permute-start(bf16[320,128]{1,0:T(8,128)(2,1)S(1)} %get-tuple-element.26), channel_id=1, source_target_pairs={{8,16},{16,8},{0,24},{24,0},{9,17},{17,9},{1,25},{25,1},{10,18},{1... | collective-permute-start | bytes 245768 | tf_op jit(solution)/shard_map/ppermute | solution.py:456
  7.0 0.1 collective-permute-start.5
  7.0 2.0 %collective-permute-start.3 = (bf16[16,80,128]{2,1,0:T(8,128)(2,1)S(1)}, bf16[16,80,128]{2,1,0:T(8,128)(2,1)S(1)}, u32[]{:S(2)}, u32[]{:S(2)}) collective-permute-start(bf16[16,80,128]{2,1,0:T(8,128)(2,1)S(1)} %get-tuple-element.30), channel_id=1, source_target_pairs={{0,1},{1,0},{2,3},{3,2},{4,5},{5,4},{6,7},{7,6},{8,9},{9,8},{10,11... | collective-permute-start | bytes 983048 | tf_op jit(solution)/shard_map/ppermute | solution.py:456
  9.1 0.7 %collective-permute-start.4 = (bf16[16,80,128]{2,1,0:T(8,128)(2,1)S(1)}, bf16[16,80,128]{2,1,0:T(8,128)(2,1)S(1)}, u32[]{:S(2)}, u32[]{:S(2)}) collective-permute-start(bf16[16,80,128]{2,1,0:T(8,128)(2,1)S(1)} %get-tuple-element.31), channel_id=1, source_target_pairs={{1,2},{2,1},{5,6},{6,5},{9,10},{10,9},{13,14},{14,13},{17,18},{18,... | collective-permute-start | bytes 983048 | tf_op jit(solution)/shard_map/ppermute | solution.py:456
  9.8 1.3 %shard_map.46 = (bf16[2,256,256]{2,1,0:T(8,128)(2,1)S(1)}, bf16[256,512]{1,0:T(8,128)(2,1)S(1)}, bf16[256,512]{1,0:T(8,128)(2,1)S(1)}) custom-call(f32[3,9]{1,0:T(4,128)} %refs_0_.2, f32[3,9]{1,0:T(4,128)} %refs_1_.1), custom_call_target="tpu_custom_call" | custom-call | bytes 1048576 | tf_op jit(solution)/shard_map/pallas_call | solution.py:453
  11.1 0.2 collective-permute-done.5.refs_3_
  11.3 0.0 collective-permute-done.refs_2_.refs_0_
  11.3 0.0 collective-permute-done.1.refs_3_.refs_1_
  11.3 3.7 %collective-permute-start.7 = (bf16[192,128]{1,0:T(8,128)(2,1)S(1)}, bf16[192,128]{1,0:T(8,128)(2,1)S(1)}, u32[]{:S(2)}, u32[]{:S(2)}) collective-permute-start(bf16[192,128]{1,0:T(8,128)(2,1)S(1)} %get-tuple-element.34), channel_id=1, source_target_pairs={{1,2},{2,1},{0,3},{3,0},{5,6},{6,5},{4,7},{7,4},{9,10},{10,9},{8,1... | collective-permute-start | bytes 147464 | tf_op jit(solution)/shard_map/ppermute | solution.py:456
  15.0 1.0 %shard_map.48 = (bf16[512,2048]{1,0:T(8,128)(2,1)S(1)}, bf16[96,2048]{1,0:T(8,128)(2,1)S(1)}) custom-call(bf16[2,256,256]{2,1,0:T(8,128)(2,1)S(1)} %get-tuple-element.23.refs_0_, bf16[16,16,16,128]{3,2,1,0:T(8,128)(2,1)S(1)} %get-tuple-element.24.refs_1_, bf16[320,128]{1,0:T(8,128)(2,1)S(1)} %collective-permute-done.refs_2_.refs_0_, ...), custom_call_target="tpu_custom_call" | custom-call | flops 536870912 | bytes 1048576 | tf_op jit(solution)/shard_map/pallas_call | solution.py:453
  16.0 0.1 collective-permute-start.2
  16.1 0.7 %collective-permute-start.6 = (bf16[192,128]{1,0:T(8,128)(2,1)S(1)}, bf16[192,128]{1,0:T(8,128)(2,1)S(1)}, u32[]{:S(2)}, u32[]{:S(2)}) collective-permute-start(bf16[192,128]{1,0:T(8,128)(2,1)S(1)} %get-tuple-element.33), channel_id=1, source_target_pairs={{0,1},{1,0},{2,3},{3,2},{4,5},{5,4},{6,7},{7,6},{8,9},{9,8},{10,11... | collective-permute-start | bytes 147464 | tf_op jit(solution)/shard_map/ppermute | solution.py:456
  16.8 2.5 %collective-permute-done.7.refs_4_ = bf16[192,128]{1,0:T(8,128)(2,1)S(1)} collective-permute-done((bf16[192,128]{1,0:T(8,128)(2,1)S(1)}, bf16[192,128]{1,0:T(8,128)(2,1)S(1)}, u32[]{:S(2)}, u32[]{:S(2)}) %collective-permute-start.7) | collective-permute-done | bytes 49184 | tf_op jit(solution)/shard_map/ppermute | solution.py:456
  19.3 4.8 %collective-permute-start.9 = (bf16[32,128]{1,0:T(8,128)(2,1)S(1)}, bf16[32,128]{1,0:T(8,128)(2,1)S(1)}, u32[]{:S(2)}, u32[]{:S(2)}) collective-permute-start(bf16[32,128]{1,0:T(8,128)(2,1)S(1)} %get-tuple-element.38), channel_id=1, source_target_pairs={{0,2},{1,3},{2,0},{3,1},{4,6},{5,7},{6,4},{7,5},{8,10},{9,11},{10,... | collective-permute-start | bytes 24584 | tf_op jit(solution)/shard_map/ppermute | solution.py:480
  24.1 0.0 collective-permute-done.6.refs_3_
  24.1 0.0 collective-permute-done.3.refs_1_
  24.1 0.0 collective-permute-done.4.refs_2_
  24.1 0.7 %shard_map.51 = (bf16[144,2048]{1,0:T(8,128)(2,1)S(1)}, bf16[144,2048]{1,0:T(8,128)(2,1)S(1)}, bf16[64,2048]{1,0:T(8,128)(2,1)S(1)}) custom-call(bf16[2,256,256]{2,1,0:T(8,128)(2,1)S(1)} %get-tuple-element.23.refs_0_, bf16[16,80,128]{2,1,0:T(8,128)(2,1)S(1)} %collective-permute-done.3.refs_1_, bf16[16,80,128]{2,1,0:T(8,128)(2,1)S(1)} %collective-permute-done.4.refs_2_, ...), custom_call_target="tpu_custom_call" | custom-call | bytes 1048576 | tf_op jit(solution)/shard_map/pallas_call | solution.py:453
  24.8 0.1 collective-permute-start.8
  24.9 0.8 %collective-permute-done.9 = bf16[32,128]{1,0:T(8,128)(2,1)S(1)} collective-permute-done((bf16[32,128]{1,0:T(8,128)(2,1)S(1)}, bf16[32,128]{1,0:T(8,128)(2,1)S(1)}, u32[]{:S(2)}, u32[]{:S(2)}) %collective-permute-start.9) | collective-permute-done | bytes 8224 | tf_op jit(solution)/shard_map/ppermute | solution.py:480
  25.7 0.1 collective-permute-start.10
  25.8 0.0 copy-start
  25.8 0.7 %shard_map.49.refs_0_ = f32[256,2048]{1,0:T(8,128)S(1)} custom-call(bf16[256,512]{1,0:T(8,128)(2,1)S(1)} %get-tuple-element.22.refs_0_, bf16[512,2048]{1,0:T(8,128)(2,1)S(1)} %get-tuple-element.27.refs_1_), custom_call_target="tpu_custom_call" | custom-call | flops 536870912 | bytes 1048576 | tf_op jit(solution)/shard_map/pallas_call | solution.py:453
  26.5 0.5 %collective-permute-done.10 = bf16[1,4,32,128]{3,2,1,0:T(8,128)(2,1)S(1)} collective-permute-done((bf16[1,4,32,128]{3,2,1,0:T(8,128)(2,1)S(1)}, bf16[1,4,32,128]{3,2,1,0:T(8,128)(2,1)S(1)}, u32[]{:S(2)}, u32[]{:S(2)}) %collective-permute-start.10) | collective-permute-done | bytes 32800 | tf_op jit(solution)/shard_map/ppermute | solution.py:417
  27.0 0.0 collective-permute-done.2.refs_2_
  27.0 0.0 collective-permute-done.8.refs_5_
  27.0 0.0 copy-done
  27.0 1.8 %shard_map.52 = bf16[16,16,16,128]{3,2,1,0:T(8,128)(2,1)} custom-call(f32[256,2048]{1,0:T(8,128)S(1)} %shard_map.49.refs_0_, bf16[256,512]{1,0:T(8,128)(2,1)S(1)} %get-tuple-element.28.refs_1_, bf16[96,2048]{1,0:T(8,128)(2,1)S(1)} %collective-permute-done.2.refs_2_, bf16[144,2048]{1,0:T(8,128)(2,1)S(1)} %get-tuple-element.35.refs_3_, ...), custom_call_target="tpu_custom_call" | custom-call | bytes 1048576 | tf_op jit(solution)/shard_map/pallas_call | solution.py:453
  (5 shorter events, 0.0 us)
Async XLA Ops:
  2.5 8.8 %collective-permute-start = (bf16[320,128]{1,0:T(8,128)(2,1)S(1)}, bf16[320,128]{1,0:T(8,128)(2,1)S(1)}, u32[]{:S(2)}, u32[]{:S(2)}) collective-permute-start(bf16[320,128]{1,0:T(8,128)(2,1)S(1)} %get-tuple-element.25), channel_id=1, source_target_pairs={{0,8},{8,0},{16,24},{24,16},{1,9},{9,1},{17,25},{25,17},{2,10},{10... | collective-permute-start | bytes 245768 | tf_op jit(solution)/shard_map/ppermute | solution.py:456
  5.5 5.8 %collective-permute-start.1 = (bf16[320,128]{1,0:T(8,128)(2,1)S(1)}, bf16[320,128]{1,0:T(8,128)(2,1)S(1)}, u32[]{:S(2)}, u32[]{:S(2)}) collective-permute-start(bf16[320,128]{1,0:T(8,128)(2,1)S(1)} %get-tuple-element.26), channel_id=1, source_target_pairs={{8,16},{16,8},{0,24},{24,0},{9,17},{17,9},{1,25},{25,1},{10,18},{1... | collective-permute-start | bytes 245768 | tf_op jit(solution)/shard_map/ppermute | solution.py:456
  7.0 4.3 %collective-permute-start.5 = (bf16[32,128]{1,0:T(8,128)(2,1)S(1)}, bf16[32,128]{1,0:T(8,128)(2,1)S(1)}, u32[]{:S(2)}, u32[]{:S(2)}) collective-permute-start(bf16[32,128]{1,0:T(8,128)(2,1)S(1)} %get-tuple-element.32.refs_2_), channel_id=1, source_target_pairs={{0,16},{8,24},{16,0},{24,8},{1,17},{9,25},{17,1},{25,9},{2,18},{10... | collective-permute-start | bytes 24584 | tf_op jit(solution)/shard_map/ppermute | solution.py:474
  7.0 17.0 %collective-permute-start.3 = (bf16[16,80,128]{2,1,0:T(8,128)(2,1)S(1)}, bf16[16,80,128]{2,1,0:T(8,128)(2,1)S(1)}, u32[]{:S(2)}, u32[]{:S(2)}) collective-permute-start(bf16[16,80,128]{2,1,0:T(8,128)(2,1)S(1)} %get-tuple-element.30), channel_id=1, source_target_pairs={{0,1},{1,0},{2,3},{3,2},{4,5},{5,4},{6,7},{7,6},{8,9},{9,8},{10,11... | collective-permute-start | bytes 983048 | tf_op jit(solution)/shard_map/ppermute | solution.py:456
  9.1 15.0 %collective-permute-start.4 = (bf16[16,80,128]{2,1,0:T(8,128)(2,1)S(1)}, bf16[16,80,128]{2,1,0:T(8,128)(2,1)S(1)}, u32[]{:S(2)}, u32[]{:S(2)}) collective-permute-start(bf16[16,80,128]{2,1,0:T(8,128)(2,1)S(1)} %get-tuple-element.31), channel_id=1, source_target_pairs={{1,2},{2,1},{5,6},{6,5},{9,10},{10,9},{13,14},{14,13},{17,18},{18,... | collective-permute-start | bytes 983048 | tf_op jit(solution)/shard_map/ppermute | solution.py:456
  11.3 8.0 %collective-permute-start.7 = (bf16[192,128]{1,0:T(8,128)(2,1)S(1)}, bf16[192,128]{1,0:T(8,128)(2,1)S(1)}, u32[]{:S(2)}, u32[]{:S(2)}) collective-permute-start(bf16[192,128]{1,0:T(8,128)(2,1)S(1)} %get-tuple-element.34), channel_id=1, source_target_pairs={{1,2},{2,1},{0,3},{3,0},{5,6},{6,5},{4,7},{7,4},{9,10},{10,9},{8,1... | collective-permute-start | bytes 147464 | tf_op jit(solution)/shard_map/ppermute | solution.py:456
  16.0 11.0 %collective-permute-start.2 = (bf16[96,2048]{1,0:T(8,128)(2,1)S(1)}, bf16[96,2048]{1,0:T(8,128)(2,1)S(1)}, u32[]{:S(2)}, u32[]{:S(2)}) collective-permute-start(bf16[96,2048]{1,0:T(8,128)(2,1)S(1)} %get-tuple-element.29), channel_id=1, source_target_pairs={{0,4},{4,0},{1,5},{5,1},{2,6},{6,2},{3,7},{7,3},{8,12},{12,8},{9,1... | collective-permute-start | bytes 1179656 | tf_op jit(solution)/shard_map/ppermute | solution.py:456
  16.1 8.0 %collective-permute-start.6 = (bf16[192,128]{1,0:T(8,128)(2,1)S(1)}, bf16[192,128]{1,0:T(8,128)(2,1)S(1)}, u32[]{:S(2)}, u32[]{:S(2)}) collective-permute-start(bf16[192,128]{1,0:T(8,128)(2,1)S(1)} %get-tuple-element.33), channel_id=1, source_target_pairs={{0,1},{1,0},{2,3},{3,2},{4,5},{5,4},{6,7},{7,6},{8,9},{9,8},{10,11... | collective-permute-start | bytes 147464 | tf_op jit(solution)/shard_map/ppermute | solution.py:456
  19.3 6.4 %collective-permute-start.9 = (bf16[32,128]{1,0:T(8,128)(2,1)S(1)}, bf16[32,128]{1,0:T(8,128)(2,1)S(1)}, u32[]{:S(2)}, u32[]{:S(2)}) collective-permute-start(bf16[32,128]{1,0:T(8,128)(2,1)S(1)} %get-tuple-element.38), channel_id=1, source_target_pairs={{0,2},{1,3},{2,0},{3,1},{4,6},{5,7},{6,4},{7,5},{8,10},{9,11},{10,... | collective-permute-start | bytes 24584 | tf_op jit(solution)/shard_map/ppermute | solution.py:480
  24.8 2.2 %collective-permute-start.8 = (bf16[64,2048]{1,0:T(8,128)(2,1)S(1)}, bf16[64,2048]{1,0:T(8,128)(2,1)S(1)}, u32[]{:S(2)}, u32[]{:S(2)}) collective-permute-start(bf16[64,2048]{1,0:T(8,128)(2,1)S(1)} %get-tuple-element.37), channel_id=1, source_target_pairs={{0,4},{4,0},{1,5},{5,1},{2,6},{6,2},{3,7},{7,3},{8,12},{12,8},{9,1... | collective-permute-start | bytes 786440 | tf_op jit(solution)/shard_map/ppermute | solution.py:456
  25.7 1.3 %collective-permute-start.10 = (bf16[1,4,32,128]{3,2,1,0:T(8,128)(2,1)S(1)}, bf16[1,4,32,128]{3,2,1,0:T(8,128)(2,1)S(1)}, u32[]{:S(2)}, u32[]{:S(2)}) collective-permute-start(bf16[1,4,32,128]{3,2,1,0:T(8,128)(2,1)S(1)} %maximum_bitcast_fusion), channel_id=1, source_target_pairs={{0,4},{4,0},{1,5},{5,1},{2,6},{6,2},{3,7},{7,3},{8,12},{12,8},{9,1... | collective-permute-start | bytes 98312 | tf_op jit(solution)/shard_map/ppermute | solution.py:417
  25.8 1.2 %copy-start = (bf16[2,2,16,2048]{3,2,1,0:T(8,128)(2,1)S(1)}, bf16[2,2,16,2048]{3,2,1,0:T(8,128)(2,1)}, u32[]{:S(2)}) copy-start(bf16[2,2,16,2048]{3,2,1,0:T(8,128)(2,1)} %param.7) | copy-start | bytes 786436

commit v5 on v4

--- a/solution.py
+++ b/solution.py
@@ -112,12 +112,22 @@
             out[n * s.face :, :] = total.astype(BF16)
 
 
-def front_kernel(s, field, *refs):
+def front_kernel(s, field, fine_far, coarse_far, *refs):
     gx = lax.axis_index("gx")
     n, m = len(s.kx), len(s.kz)
-    faces, edges, (piece, held, sem) = refs[:m], refs[m : m + n], refs[m + n :]
-    copy = pltpu.make_async_copy(field, held, sem)
-    copy.start()
+    faces, edges, refs = refs[:m], refs[m : m + n], refs[m + n :]
+    piece, weights, held, fine, coarse, found, sems = refs
+    taps = [
+        pltpu.make_async_copy(fine_far, fine, sems.at[s.chunks]),
+        pltpu.make_async_copy(coarse_far, coarse, sems.at[s.chunks + 1]),
+    ]
+    chunk = s.V // s.chunks
+    copies = []
+    for i in range(s.chunks):
+        at = pl.ds(i * chunk, chunk)
+        copies.append(pltpu.make_async_copy(field.at[at], held.at[at], sems.at[i]))
+    for each in taps + copies:
+        each.start()
     half = s.Y // 2
     deep, tall, long = s.Z // s.tz, s.Y // s.ty, s.X // s.tx
     x, lane = iota((s.X, s.V * E), 0), iota((s.X, s.V * E), 1)
@@ -128,35 +138,40 @@
         for v in range(s.V)
     ]
     sub = iota((s.V, s.X), 0)
-    copy.wait()
-    found = dot(
-        wide([held[v].reshape(s.rows, s.X) for v in range(s.V)]), jnp.concatenate(by_v, axis=0)
-    )
+    gz = lax.axis_index("gz")
+    row, col = iota((s.avg, s.raw), 0), iota((s.avg, s.raw), 1)
+    mean = one((col // s.Y // 2 == row // half) & (col % s.Y // 2 == row % half), 0.25)
+    for each in taps:
+        each.wait()
+    for i, block in enumerate(x_weights(s, fine, coarse)):
+        weights[i] = block
     by_vector = [jnp.zeros((s.V, s.X), F32) for _ in range(s.tz * s.ty)]
-    for v in range(s.V):
-        for i in range(s.tz):
-            layers = held[v, i * deep].astype(F32)
-            for z in range(i * deep + 1, (i + 1) * deep):
-                layers = layers + held[v, z].astype(F32)
-            for j in range(s.ty):
-                line = jnp.sum(layers[j * tall : (j + 1) * tall], axis=0, keepdims=True)
-                line = jnp.broadcast_to(line * (1.0 / (deep * tall)), (s.V, s.X))
-                by_vector[i * s.ty + j] = jnp.where(sub == v, line, by_vector[i * s.ty + j])
-    gz = lax.axis_index("gz")
-    row = iota((s.avg, s.raw), 0)
-    col = iota((s.avg, s.raw), 1)
-    half = s.Y // 2
-    mean = one((col // s.Y // 2 == row // half) & (col % s.Y // 2 == row % half), 0.25)
-    for kind, out in zip(s.kz, faces):
-        up = upper(gz, kind)
-        start = jnp.where(up, s.Z - R, 0)
-        further = jnp.where(up, s.Z - E, R)
-        for v in range(s.V):
-            out[v, : s.raw, :] = held[v, pl.ds(start, R)].reshape(s.raw, s.X)
-        data = wide([held[v, pl.ds(further, R)].reshape(s.raw, s.X) for v in range(s.V)])
-        means = dot(mean, data).astype(BF16)
-        for v in range(s.V):
-            out[v, s.raw :, :] = means[:, v * s.X : (v + 1) * s.X]
+    for part, copy in enumerate(copies):
+        vectors = range(part * chunk, (part + 1) * chunk)
+        copy.wait()
+        data = wide([held[v].reshape(s.rows, s.X) for v in vectors])
+        more = dot(data, jnp.concatenate([by_v[v] for v in vectors], axis=0))
+        found[...] = more if part == 0 else found[...] + more
+        for kind, out in zip(s.kz, faces):
+            up = upper(gz, kind)
+            start = jnp.where(up, s.Z - R, 0)
+            further = jnp.where(up, s.Z - E, R)
+            for v in vectors:
+                out[v, : s.raw, :] = held[v, pl.ds(start, R)].reshape(s.raw, s.X)
+            data = wide([held[v, pl.ds(further, R)].reshape(s.raw, s.X) for v in vectors])
+            means = dot(mean, data).astype(BF16)
+            for v in vectors:
+                at = v % chunk * s.X
+                out[v, s.raw :, :] = means[:, at : at + s.X]
+        for v in vectors:
+            for i in range(s.tz):
+                layers = held[v, i * deep].astype(F32)
+                for z in range(i * deep + 1, (i + 1) * deep):
+                    layers = layers + held[v, z].astype(F32)
+                for j in range(s.ty):
+                    line = jnp.sum(layers[j * tall : (j + 1) * tall], axis=0, keepdims=True)
+                    line = jnp.broadcast_to(line * (1.0 / (deep * tall)), (s.V, s.X))
+                    by_vector[i * s.ty + j] = jnp.where(sub == v, line, by_vector[i * s.ty + j])
     r, c = iota((2 * s.avg, s.rows), 0), iota((2 * s.avg, s.rows), 1)
     layer = r // half * 2 + jnp.where(r < s.avg, R, s.Z - E - R)
     mean = one((c // s.Y // 2 * 2 == layer) & (c % s.Y // 2 == r % half), 0.25)
@@ -347,9 +362,7 @@
     return total
 
 
-def weights_kernel(s, fine, coarse, x, now, later):
-    for i, block in enumerate(x_weights(s, fine, coarse)):
-        x[i] = block
+def weights_kernel(s, fine, coarse, now, later):
     first, second = yz_weights(s, fine, coarse)
     for ref, blocks in ((now, first), (later, second)):
         at = 0
@@ -365,20 +378,26 @@
         total[:, cols] = dot(now[...], own[:, cols])
 
 
+def top_own_kernel(s, known, kernel, total):
+    gy, gz = lax.axis_index("gy"), lax.axis_index("gz")
+    parts = [(slot(z, gz, s.nz), gy, lambda at, i, z=z: known[z, at, :]) for z in range(s.nz)]
+    total[...] = top_product(s, kernel, parts, jnp.zeros((s.top, s.V), F32))
+
+
 def final_kernel(s, *refs):
     m, k = len(s.kz), len(s.ky)
     partial, later, *refs = refs
     ends, refs = refs[:k], refs[k:]
     sides, refs = refs[:m], refs[m:]
     packs, refs = refs[:k], refs[k:]
-    known, kernel, out, held, sems = refs
+    started, known, kernel, out, held, sems = refs
     gy, gz = lax.axis_index("gy"), lax.axis_index("gz")
     parts = [
         (slot(z, gz, s.nz), slot(y, gy, s.ny), lambda at, i, y=y, z=z: known[y, z, at, :])
-        for y in range(s.ny)
+        for y in range(1 if doubling(s.ny) else 0, s.ny)
         for z in range(s.nz)
     ]
-    total = top_product(s, kernel, parts, jnp.zeros((s.top, s.V), F32))
+    total = top_product(s, kernel, parts, started[...])
     r, c = iota((s.top, s.X), 0), iota((s.top, s.X), 1)
     spread = c // (s.X // s.tx) == r % s.tx
     chunk = s.V // s.chunks
@@ -453,19 +472,30 @@
         return list(call(*arrays))
 
     def swap(arrays, axis, count, which, ring=False):
-        return [lax.ppermute(a, axis, swaps(count, kind, ring)) for a, kind in zip(arrays, which)]
-
+        moved = []
+        for a, kind in zip(arrays, which):
+            moved.append(lax.ppermute(a, axis, swaps(count, kind, ring)))
+        return moved
+
+    taps = [fine_taps, coarse_taps]
     buffers = [pltpu.VMEM(field.shape, BF16), pltpu.SemaphoreType.DMA((s.chunks,))]
     top = shape(s.tz * s.V, s.tile)
-    outs = [shape(s.V, s.face, s.X)] * m + [shape(s.edge, s.V * E)] * n + [top]
-    *faces, field = run(
+    x_depth = s.X + s.V * E
+    outs = [shape(s.V, s.face, s.X)] * m + [shape(s.edge, s.V * E)] * n
+    outs += [top, shape(2, x_depth, 2 * s.X), shape(*field.shape)]
+    far = [pltpu.with_memory_space_constraint(a, pltpu.HBM) for a in (field, *taps)]
+    *faces, piece, weights, field = run(
         front_kernel,
-        [pltpu.with_memory_space_constraint(field, pltpu.HBM)],
-        outs + [shape(*field.shape)],
-        scratch=[pltpu.SemaphoreType.DMA],
-        far=(0,),
+        far,
+        outs,
+        scratch=[pltpu.SMEM(a.shape, a.dtype) for a in taps]
+        + [
+            pltpu.VMEM((s.rows, max(n, 1) * s.V * E), F32),
+            pltpu.SemaphoreType.DMA((s.chunks + 2,)),
+        ],
+        far=(0, 1, 2),
     )
-    faces, edges, piece = faces[:m], faces[m : m + n], faces[-1]
+    faces, edges = faces[:m], faces[m:]
     halos = swap(edges, "gx", s.nx, s.kx, s.ride)
     faces = swap(faces, "gz", s.nz, s.kz)
     corner = [shape(s.corner, s.V * E)] * m
@@ -482,17 +512,13 @@
         known = jnp.stack([known, near, across, far])
     else:
         known = gather(gather(piece, "gx", s.nx, sum)[None], "gz", s.nz, stack)
-    x_depth = s.X + s.V * E
     later = k * (s.yf + s.yc) + m * s.gz + k * s.ypack + s.top
-    weights, w_now, w_later = run(
+    w_now, w_later = run(
         weights_kernel,
-        [pltpu.with_memory_space_constraint(a, pltpu.HBM) for a in (fine_taps, coarse_taps)],
-        [
-            shape(2, x_depth, 2 * s.X),
-            shape(s.rows, 2 * s.rows),
-            shape(s.rows, later),
-        ],
+        taps,
+        [shape(s.rows, 2 * s.rows), shape(s.rows, later)],
         scalars=2,
+        flops=1 << 28,
     )
     own, *ends = run(
         own_kernel,
@@ -514,11 +540,16 @@
         [jax.ShapeDtypeStruct((s.rows, s.lanes), F32)],
         flops=4 * s.rows * s.rows * s.lanes,
     )[0]
+    kernel_rows = top_kernel.reshape(s.top, top_kernel.shape[3])
+    started = jnp.zeros((s.top, s.V), F32)
+    if doubling(s.ny):
+        started = run(
+            top_own_kernel, [known, kernel_rows], [jax.ShapeDtypeStruct((s.top, s.V), F32)]
+        )[0]
     known = gather(known[None], "gy", s.ny, stack)
-    kernel_rows = top_kernel.reshape(s.top, top_kernel.shape[3])
     return run(
         final_kernel,
-        [partial, w_later] + ends + sides + packs + [known, kernel_rows],
+        [partial, w_later] + ends + sides + packs + [started, known, kernel_rows],
         [shape(*field.shape)],
         scratch=buffers,
         far_out=True,

time: 29 us -> 28.5 us (0.983)
  waiting for transfers between devices: 3.96 us -> 2 us
  local copies, waits for them, and re-layouts: 0.01 us -> 1.6 us
    ppermute x8, waiting for transfers between devices: 2.54 us -> 0.44 us  [swap(): moved.append(lax.ppermute(a, axis, swaps(count, kind, ring)))]
    unnamed x2 -> x6, local copies, waits for them, and re-layouts: 0.01 us -> 1.6 us
    ppermute x1, waiting for transfers between devices: 0.16 us -> 0.69 us  [shards(): across = lax.ppermute(piece, 'gx', [(i, i ^ 2) for i in range(s.nx)])]
    ppermute x1, starting transfers between devices: 0.05 us -> 0.57 us  [shards(): across = lax.ppermute(piece, 'gx', [(i, i ^ 2) for i in range(s.nx)])]
    ppermute x1, waiting for transfers between devices: 0.47 us -> 0.07 us  [gather(): a = join([a, lax.ppermute(a, axis, [(i, i ^ step) for i in range(count)])])]
    ppermute x8, starting transfers between devices: 11.7 us -> 11.4 us  [swap(): moved.append(lax.ppermute(a, axis, swaps(count, kind, ring)))]
    pallas_call x7 -> x8, Pallas kernels: 8.05 us -> 7.77 us  [run(): return list(call(*arrays))]
where the time goes in v5:
time: 28.5 us; the launch traced here: 28.3 us
  starting transfers between devices  16.8 us (59%)
  Pallas kernels  7.77 us (27%)
  waiting for transfers between devices  2 us (7%)
  local copies, waits for them, and re-layouts  1.6 us (6%)
    ppermute x8, starting transfers between devices, swap(): moved.append(lax.ppermute(a, axis, swaps(count, kind, ring)))  11.4 us
    pallas_call x8, Pallas kernels, run(): return list(call(*arrays))  7.77 us
    ppermute x1, starting transfers between devices, shards(): across = lax.ppermute(known, 'gz', [(i, i ^ 2) for i in range(s.nz)])  4.7 us
    unnamed x6, local copies, waits for them, and re-layouts  1.6 us
    ppermute x1, waiting for transfers between devices, shards(): across = lax.ppermute(known, 'gz', [(i, i ^ 2) for i in range(s.nz)])  0.8 us
    ppermute x1, waiting for transfers between devices, shards(): across = lax.ppermute(piece, 'gx', [(i, i ^ 2) for i in range(s.nx)])  0.69 us
    ppermute x1, starting transfers between devices, shards(): across = lax.ppermute(piece, 'gx', [(i, i ^ 2) for i in range(s.nx)])  0.57 us
  transfers between devices with their start and end apart: 11, of which 4 were waited for; matrix products, arithmetic and copies ran while one was open for 0% of the time, Pallas kernels for 13%

profile of v5, /device:TPU:0, one launch (start us, length us, event | category | flops | bytes accessed | tf_op | source)
XLA Modules:
  0.0 28.3 jit_solution(11892836157398889469)
XLA Ops:
  0.0 2.4 %shard_map.47 = (bf16[16,80,128]{2,1,0:T(8,128)(2,1)S(1)}, bf16[16,80,128]{2,1,0:T(8,128)(2,1)S(1)}, bf16[320,128]{1,0:T(8,128)(2,1)S(1)}, bf16[320,128]{1,0:T(8...) custom-call(bf16[16,16,16,128]{3,2,1,0:T(8,128)(2,1)} %refs_0_.3, ...), custom_call_target="tpu_custom_call" | custom-call | bytes 1048576 | tf_op jit(solution)/shard_map/pallas_call | solution.py:472
  2.4 3.0 %collective-permute-start = (bf16[320,128]{1,0:T(8,128)(2,1)S(1)}, bf16[320,128]{1,0:T(8,128)(2,1)S(1)}, u32[]{:S(2)}, u32[]{:S(2)}) collective-permute-start(bf16[320,128]{1,0:T(8,128)(2,1)S(1)} %get-tuple-element.25), channel_id=1, source_target_pairs={{0,8},{8,0},{16,24},{24,16},{1,9},{9,1},{17,25},{25,17},{2,10},{10... | collective-permute-start | bytes 245768 | tf_op jit(solution)/shard_map/ppermute | solution.py:477
  5.4 1.5 %collective-permute-start.1 = (bf16[320,128]{1,0:T(8,128)(2,1)S(1)}, bf16[320,128]{1,0:T(8,128)(2,1)S(1)}, u32[]{:S(2)}, u32[]{:S(2)}) collective-permute-start(bf16[320,128]{1,0:T(8,128)(2,1)S(1)} %get-tuple-element.26), channel_id=1, source_target_pairs={{8,16},{16,8},{0,24},{24,0},{9,17},{17,9},{1,25},{25,1},{10,18},{1... | collective-permute-start | bytes 245768 | tf_op jit(solution)/shard_map/ppermute | solution.py:477
  6.9 1.6 %collective-permute-start.3 = (bf16[16,80,128]{2,1,0:T(8,128)(2,1)S(1)}, bf16[16,80,128]{2,1,0:T(8,128)(2,1)S(1)}, u32[]{:S(2)}, u32[]{:S(2)}) collective-permute-start(bf16[16,80,128]{2,1,0:T(8,128)(2,1)S(1)} %get-tuple-element.30), channel_id=1, source_target_pairs={{0,1},{1,0},{2,3},{3,2},{4,5},{5,4},{6,7},{7,6},{8,9},{9,8},{10,11... | collective-permute-start | bytes 983048 | tf_op jit(solution)/shard_map/ppermute | solution.py:477
  8.5 0.7 %collective-permute-start.4 = (bf16[16,80,128]{2,1,0:T(8,128)(2,1)S(1)}, bf16[16,80,128]{2,1,0:T(8,128)(2,1)S(1)}, u32[]{:S(2)}, u32[]{:S(2)}) collective-permute-start(bf16[16,80,128]{2,1,0:T(8,128)(2,1)S(1)} %get-tuple-element.31), channel_id=1, source_target_pairs={{1,2},{2,1},{5,6},{6,5},{9,10},{10,9},{13,14},{14,13},{17,18},{18,... | collective-permute-start | bytes 983048 | tf_op jit(solution)/shard_map/ppermute | solution.py:477
  9.2 0.6 %collective-permute-start.5 = (bf16[32,128]{1,0:T(8,128)(2,1)S(1)}, bf16[32,128]{1,0:T(8,128)(2,1)S(1)}, u32[]{:S(2)}, u32[]{:S(2)}) collective-permute-start(bf16[32,128]{1,0:T(8,128)(2,1)S(1)} %get-tuple-element.32.refs_2_), channel_id=1, source_target_pairs={{0,16},{8,24},{16,0},{24,8},{1,17},{9,25},{17,1},{25,9},{2,18},{10... | collective-permute-start | bytes 24584 | tf_op jit(solution)/shard_map/ppermute | solution.py:504
  9.7 0.0 copy-start.1
  9.7 0.7 %copy-done.1 = f32[3,9]{1,0:T(4,128)S(1)} copy-done((f32[3,9]{1,0:T(4,128)S(1)}, f32[3,9]{1,0:T(4,128)}, u32[]{:S(2)}) %copy-start.1) | copy-done | bytes 132
  10.4 0.0 copy-start.2
  10.4 0.7 %copy-done.2 = f32[3,9]{1,0:T(4,128)S(1)} copy-done((f32[3,9]{1,0:T(4,128)S(1)}, f32[3,9]{1,0:T(4,128)}, u32[]{:S(2)}) %copy-start.2) | copy-done | bytes 132
  11.1 1.1 %shard_map.46 = (bf16[256,512]{1,0:T(8,128)(2,1)S(1)}, bf16[256,512]{1,0:T(8,128)(2,1)S(1)}) custom-call(f32[3,9]{1,0:T(4,128)S(1)} %copy-done.1, f32[3,9]{1,0:T(4,128)S(1)} %copy-done.2), custom_call_target="tpu_custom_call" | custom-call | flops 268435456 | bytes 1048576 | tf_op jit(solution)/shard_map/pallas_call | solution.py:472
  12.2 0.7 %collective-permute-done.5.refs_3_ = bf16[32,128]{1,0:T(8,128)(2,1)S(1)} collective-permute-done((bf16[32,128]{1,0:T(8,128)(2,1)S(1)}, bf16[32,128]{1,0:T(8,128)(2,1)S(1)}, u32[]{:S(2)}, u32[]{:S(2)}) %collective-permute-start.5) | collective-permute-done | bytes 8224 | tf_op jit(solution)/shard_map/ppermute | solution.py:504
  12.9 0.0 collective-permute-done.refs_2_.refs_0_
  12.9 0.0 collective-permute-done.1.refs_3_.refs_1_
  12.9 2.5 %collective-permute-start.7 = (bf16[192,128]{1,0:T(8,128)(2,1)S(1)}, bf16[192,128]{1,0:T(8,128)(2,1)S(1)}, u32[]{:S(2)}, u32[]{:S(2)}) collective-permute-start(bf16[192,128]{1,0:T(8,128)(2,1)S(1)} %get-tuple-element.34), channel_id=1, source_target_pairs={{1,2},{2,1},{0,3},{3,0},{5,6},{6,5},{4,7},{7,4},{9,10},{10,9},{8,1... | collective-permute-start | bytes 147464 | tf_op jit(solution)/shard_map/ppermute | solution.py:477
  15.4 1.0 %shard_map.48 = (bf16[512,2048]{1,0:T(8,128)(2,1)S(1)}, bf16[96,2048]{1,0:T(8,128)(2,1)S(1)}) custom-call(bf16[2,256,256]{2,1,0:T(8,128)(2,1)S(1)} %get-tuple-element.23.refs_0_, bf16[16,16,16,128]{3,2,1,0:T(8,128)(2,1)S(1)} %get-tuple-element.24.refs_1_, bf16[320,128]{1,0:T(8,128)(2,1)S(1)} %collective-permute-done.refs_2_.refs_0_, ...), custom_call_target="tpu_custom_call" | custom-call | flops 536870912 | bytes 1048576 | tf_op jit(solution)/shard_map/pallas_call | solution.py:472
  16.5 0.1 collective-permute-start.2
  16.6 2.0 %collective-permute-start.6 = (bf16[192,128]{1,0:T(8,128)(2,1)S(1)}, bf16[192,128]{1,0:T(8,128)(2,1)S(1)}, u32[]{:S(2)}, u32[]{:S(2)}) collective-permute-start(bf16[192,128]{1,0:T(8,128)(2,1)S(1)} %get-tuple-element.33), channel_id=1, source_target_pairs={{0,1},{1,0},{2,3},{3,2},{4,5},{5,4},{6,7},{7,6},{8,9},{9,8},{10,11... | collective-permute-start | bytes 147464 | tf_op jit(solution)/shard_map/ppermute | solution.py:477
  18.5 0.4 %collective-permute-done.7.refs_4_ = bf16[192,128]{1,0:T(8,128)(2,1)S(1)} collective-permute-done((bf16[192,128]{1,0:T(8,128)(2,1)S(1)}, bf16[192,128]{1,0:T(8,128)(2,1)S(1)}, u32[]{:S(2)}, u32[]{:S(2)}) %collective-permute-start.7) | collective-permute-done | bytes 49184 | tf_op jit(solution)/shard_map/ppermute | solution.py:477
  19.0 4.7 %collective-permute-start.9 = (bf16[32,128]{1,0:T(8,128)(2,1)S(1)}, bf16[32,128]{1,0:T(8,128)(2,1)S(1)}, u32[]{:S(2)}, u32[]{:S(2)}) collective-permute-start(bf16[32,128]{1,0:T(8,128)(2,1)S(1)} %get-tuple-element.38), channel_id=1, source_target_pairs={{0,2},{1,3},{2,0},{3,1},{4,6},{5,7},{6,4},{7,5},{8,10},{9,11},{10,... | collective-permute-start | bytes 24584 | tf_op jit(solution)/shard_map/ppermute | solution.py:510
  23.7 0.0 collective-permute-done.6.refs_3_
  23.7 0.0 collective-permute-done.3.refs_1_
  23.7 0.0 collective-permute-done.4.refs_2_
  23.7 0.7 %shard_map.51 = (bf16[144,2048]{1,0:T(8,128)(2,1)S(1)}, bf16[144,2048]{1,0:T(8,128)(2,1)S(1)}, bf16[64,2048]{1,0:T(8,128)(2,1)S(1)}) custom-call(bf16[2,256,256]{2,1,0:T(8,128)(2,1)S(1)} %get-tuple-element.23.refs_0_, bf16[16,80,128]{2,1,0:T(8,128)(2,1)S(1)} %collective-permute-done.3.refs_1_, bf16[16,80,128]{2,1,0:T(8,128)(2,1)S(1)} %collective-permute-done.4.refs_2_, ...), custom_call_target="tpu_custom_call" | custom-call | bytes 1048576 | tf_op jit(solution)/shard_map/pallas_call | solution.py:472
  24.4 0.1 collective-permute-start.8
  24.5 0.8 %collective-permute-done.9 = bf16[32,128]{1,0:T(8,128)(2,1)S(1)} collective-permute-done((bf16[32,128]{1,0:T(8,128)(2,1)S(1)}, bf16[32,128]{1,0:T(8,128)(2,1)S(1)}, u32[]{:S(2)}, u32[]{:S(2)}) %collective-permute-start.9) | collective-permute-done | bytes 8224 | tf_op jit(solution)/shard_map/ppermute | solution.py:510
  25.3 0.1 collective-permute-start.10
  25.4 0.0 copy-start
  25.4 0.7 %shard_map.49.refs_0_ = f32[256,2048]{1,0:T(8,128)S(1)} custom-call(bf16[256,512]{1,0:T(8,128)(2,1)S(1)} %get-tuple-element.22.refs_0_, bf16[512,2048]{1,0:T(8,128)(2,1)S(1)} %get-tuple-element.27.refs_1_), custom_call_target="tpu_custom_call" | custom-call | flops 536870912 | bytes 1048576 | tf_op jit(solution)/shard_map/pallas_call | solution.py:472
  26.1 0.2 copy-done
  26.3 0.2 shard_map.52.refs_6_
  26.5 0.1 collective-permute-done.10
  26.6 0.0 collective-permute-done.2.refs_2_
  26.6 0.0 collective-permute-done.8.refs_5_
  26.6 1.7 %shard_map.53 = bf16[16,16,16,128]{3,2,1,0:T(8,128)(2,1)} custom-call(f32[256,2048]{1,0:T(8,128)S(1)} %shard_map.49.refs_0_, bf16[256,512]{1,0:T(8,128)(2,1)S(1)} %get-tuple-element.28.refs_1_, bf16[96,2048]{1,0:T(8,128)(2,1)S(1)} %collective-permute-done.2.refs_2_, bf16[144,2048]{1,0:T(8,128)(2,1)S(1)} %get-tuple-element.35.refs_3_, ...), custom_call_target="tpu_custom_call" | custom-call | bytes 1048576 | tf_op jit(solution)/shard_map/pallas_call | solution.py:472
  (5 shorter events, 0.0 us)
Async XLA Ops:
  2.4 10.5 %collective-permute-start = (bf16[320,128]{1,0:T(8,128)(2,1)S(1)}, bf16[320,128]{1,0:T(8,128)(2,1)S(1)}, u32[]{:S(2)}, u32[]{:S(2)}) collective-permute-start(bf16[320,128]{1,0:T(8,128)(2,1)S(1)} %get-tuple-element.25), channel_id=1, source_target_pairs={{0,8},{8,0},{16,24},{24,16},{1,9},{9,1},{17,25},{25,17},{2,10},{10... | collective-permute-start | bytes 245768 | tf_op jit(solution)/shard_map/ppermute | solution.py:477
  5.4 7.5 %collective-permute-start.1 = (bf16[320,128]{1,0:T(8,128)(2,1)S(1)}, bf16[320,128]{1,0:T(8,128)(2,1)S(1)}, u32[]{:S(2)}, u32[]{:S(2)}) collective-permute-start(bf16[320,128]{1,0:T(8,128)(2,1)S(1)} %get-tuple-element.26), channel_id=1, source_target_pairs={{8,16},{16,8},{0,24},{24,0},{9,17},{17,9},{1,25},{25,1},{10,18},{1... | collective-permute-start | bytes 245768 | tf_op jit(solution)/shard_map/ppermute | solution.py:477
  6.9 16.8 %collective-permute-start.3 = (bf16[16,80,128]{2,1,0:T(8,128)(2,1)S(1)}, bf16[16,80,128]{2,1,0:T(8,128)(2,1)S(1)}, u32[]{:S(2)}, u32[]{:S(2)}) collective-permute-start(bf16[16,80,128]{2,1,0:T(8,128)(2,1)S(1)} %get-tuple-element.30), channel_id=1, source_target_pairs={{0,1},{1,0},{2,3},{3,2},{4,5},{5,4},{6,7},{7,6},{8,9},{9,8},{10,11... | collective-permute-start | bytes 983048 | tf_op jit(solution)/shard_map/ppermute | solution.py:477
  8.5 15.2 %collective-permute-start.4 = (bf16[16,80,128]{2,1,0:T(8,128)(2,1)S(1)}, bf16[16,80,128]{2,1,0:T(8,128)(2,1)S(1)}, u32[]{:S(2)}, u32[]{:S(2)}) collective-permute-start(bf16[16,80,128]{2,1,0:T(8,128)(2,1)S(1)} %get-tuple-element.31), channel_id=1, source_target_pairs={{1,2},{2,1},{5,6},{6,5},{9,10},{10,9},{13,14},{14,13},{17,18},{18,... | collective-permute-start | bytes 983048 | tf_op jit(solution)/shard_map/ppermute | solution.py:477
  9.2 3.7 %collective-permute-start.5 = (bf16[32,128]{1,0:T(8,128)(2,1)S(1)}, bf16[32,128]{1,0:T(8,128)(2,1)S(1)}, u32[]{:S(2)}, u32[]{:S(2)}) collective-permute-start(bf16[32,128]{1,0:T(8,128)(2,1)S(1)} %get-tuple-element.32.refs_2_), channel_id=1, source_target_pairs={{0,16},{8,24},{16,0},{24,8},{1,17},{9,25},{17,1},{25,9},{2,18},{10... | collective-permute-start | bytes 24584 | tf_op jit(solution)/shard_map/ppermute | solution.py:504
  9.7 0.7 %copy-start.1 = (f32[3,9]{1,0:T(4,128)S(1)}, f32[3,9]{1,0:T(4,128)}, u32[]{:S(2)}) copy-start(f32[3,9]{1,0:T(4,128)} %refs_1_.3) | copy-start | bytes 328
  10.4 0.7 %copy-start.2 = (f32[3,9]{1,0:T(4,128)S(1)}, f32[3,9]{1,0:T(4,128)}, u32[]{:S(2)}) copy-start(f32[3,9]{1,0:T(4,128)} %refs_2_.1) | copy-start | bytes 328
  12.9 6.1 %collective-permute-start.7 = (bf16[192,128]{1,0:T(8,128)(2,1)S(1)}, bf16[192,128]{1,0:T(8,128)(2,1)S(1)}, u32[]{:S(2)}, u32[]{:S(2)}) collective-permute-start(bf16[192,128]{1,0:T(8,128)(2,1)S(1)} %get-tuple-element.34), channel_id=1, source_target_pairs={{1,2},{2,1},{0,3},{3,0},{5,6},{6,5},{4,7},{7,4},{9,10},{10,9},{8,1... | collective-permute-start | bytes 147464 | tf_op jit(solution)/shard_map/ppermute | solution.py:477
  16.5 10.1 %collective-permute-start.2 = (bf16[96,2048]{1,0:T(8,128)(2,1)S(1)}, bf16[96,2048]{1,0:T(8,128)(2,1)S(1)}, u32[]{:S(2)}, u32[]{:S(2)}) collective-permute-start(bf16[96,2048]{1,0:T(8,128)(2,1)S(1)} %get-tuple-element.29), channel_id=1, source_target_pairs={{0,4},{4,0},{1,5},{5,1},{2,6},{6,2},{3,7},{7,3},{8,12},{12,8},{9,1... | collective-permute-start | bytes 1179656 | tf_op jit(solution)/shard_map/ppermute | solution.py:477
  16.6 7.1 %collective-permute-start.6 = (bf16[192,128]{1,0:T(8,128)(2,1)S(1)}, bf16[192,128]{1,0:T(8,128)(2,1)S(1)}, u32[]{:S(2)}, u32[]{:S(2)}) collective-permute-start(bf16[192,128]{1,0:T(8,128)(2,1)S(1)} %get-tuple-element.33), channel_id=1, source_target_pairs={{0,1},{1,0},{2,3},{3,2},{4,5},{5,4},{6,7},{7,6},{8,9},{9,8},{10,11... | collective-permute-start | bytes 147464 | tf_op jit(solution)/shard_map/ppermute | solution.py:477
  19.0 6.3 %collective-permute-start.9 = (bf16[32,128]{1,0:T(8,128)(2,1)S(1)}, bf16[32,128]{1,0:T(8,128)(2,1)S(1)}, u32[]{:S(2)}, u32[]{:S(2)}) collective-permute-start(bf16[32,128]{1,0:T(8,128)(2,1)S(1)} %get-tuple-element.38), channel_id=1, source_target_pairs={{0,2},{1,3},{2,0},{3,1},{4,6},{5,7},{6,4},{7,5},{8,10},{9,11},{10,... | collective-permute-start | bytes 24584 | tf_op jit(solution)/shard_map/ppermute | solution.py:510
  24.4 2.2 %collective-permute-start.8 = (bf16[64,2048]{1,0:T(8,128)(2,1)S(1)}, bf16[64,2048]{1,0:T(8,128)(2,1)S(1)}, u32[]{:S(2)}, u32[]{:S(2)}) collective-permute-start(bf16[64,2048]{1,0:T(8,128)(2,1)S(1)} %get-tuple-element.37), channel_id=1, source_target_pairs={{0,4},{4,0},{1,5},{5,1},{2,6},{6,2},{3,7},{7,3},{8,12},{12,8},{9,1... | collective-permute-start | bytes 786440 | tf_op jit(solution)/shard_map/ppermute | solution.py:477
  25.3 1.3 %collective-permute-start.10 = (bf16[1,4,32,128]{3,2,1,0:T(8,128)(2,1)S(1)}, bf16[1,4,32,128]{3,2,1,0:T(8,128)(2,1)S(1)}, u32[]{:S(2)}, u32[]{:S(2)}) collective-permute-start(bf16[1,4,32,128]{3,2,1,0:T(8,128)(2,1)S(1)} %get-tuple-element.39), channel_id=1, source_target_pairs={{0,4},{4,0},{1,5},{5,1},{2,6},{6,2},{3,7},{7,3},{8,12},{12,8},{9,1... | collective-permute-start | bytes 98312 | tf_op jit(solution)/shard_map/ppermute | solution.py:436
  25.4 1.0 %copy-start = (bf16[2,2,16,2048]{3,2,1,0:T(8,128)(2,1)S(1)}, bf16[2,2,16,2048]{3,2,1,0:T(8,128)(2,1)}, u32[]{:S(2)}) copy-start(bf16[2,2,16,2048]{3,2,1,0:T(8,128)(2,1)} %param.7) | copy-start | bytes 786436

commit v6 on v5

--- a/solution.py
+++ b/solution.py
@@ -72,6 +72,7 @@
         self.tz, self.ty, self.tx = top_shape
         self.top = self.tz * self.ty * self.tx
         self.gz = self.raw + self.face
+        self.sent = self.V * self.raw + self.V // 2 * self.avg
         self.tile = self.ty * self.tx * self.nx
         self.ride = self.nx == 4 and self.nz == 4 and self.tile == self.V * E
         self.edge = self.rows + 2 * self.avg + (self.tz * self.V if self.ride else 0)
@@ -141,11 +142,16 @@
     gz = lax.axis_index("gz")
     row, col = iota((s.avg, s.raw), 0), iota((s.avg, s.raw), 1)
     mean = one((col // s.Y // 2 == row // half) & (col % s.Y // 2 == row % half), 0.25)
+    r, c = iota((2 * s.X, s.X), 0), iota((2 * s.X, s.X), 1)
+    halve = one(r // 2 == c, 0.5)
     for each in taps:
         each.wait()
-    for i, block in enumerate(x_weights(s, fine, coarse)):
+    *blocks, pairs_block = x_weights(s, fine, coarse)
+    for i, block in enumerate(blocks):
         weights[i] = block
+    weights[2, : s.X, : s.X] = pairs_block
     by_vector = [jnp.zeros((s.V, s.X), F32) for _ in range(s.tz * s.ty)]
+    stacked = {kind: [] for kind in s.kz}
     for part, copy in enumerate(copies):
         vectors = range(part * chunk, (part + 1) * chunk)
         copy.wait()
@@ -157,12 +163,12 @@
             start = jnp.where(up, s.Z - R, 0)
             further = jnp.where(up, s.Z - E, R)
             for v in vectors:
-                out[v, : s.raw, :] = held[v, pl.ds(start, R)].reshape(s.raw, s.X)
+                at = v * s.raw
+                out[at : at + s.raw, :] = held[v, pl.ds(start, R)].reshape(s.raw, s.X)
             data = wide([held[v, pl.ds(further, R)].reshape(s.raw, s.X) for v in vectors])
             means = dot(mean, data).astype(BF16)
-            for v in vectors:
-                at = v % chunk * s.X
-                out[v, s.raw :, :] = means[:, at : at + s.X]
+            for i in range(0, chunk, 2):
+                stacked[kind].append(means[:, i * s.X : (i + 2) * s.X])
         for v in vectors:
             for i in range(s.tz):
                 layers = held[v, i * deep].astype(F32)
@@ -172,6 +178,11 @@
                     line = jnp.sum(layers[j * tall : (j + 1) * tall], axis=0, keepdims=True)
                     line = jnp.broadcast_to(line * (1.0 / (deep * tall)), (s.V, s.X))
                     by_vector[i * s.ty + j] = jnp.where(sub == v, line, by_vector[i * s.ty + j])
+    if faces:
+        means = dot(jnp.concatenate([x for kind in s.kz for x in stacked[kind]], axis=0), halve)
+        count = s.V // 2 * s.avg
+        for i, out in enumerate(faces):
+            out[s.V * s.raw :, :] = means[i * count : (i + 1) * count].astype(BF16)
     r, c = iota((2 * s.avg, s.rows), 0), iota((2 * s.avg, s.rows), 1)
     layer = r // half * 2 + jnp.where(r < s.avg, R, s.Z - E - R)
     mean = one((c // s.Y // 2 * 2 == layer) & (c % s.Y // 2 == r % half), 0.25)
@@ -212,7 +223,9 @@
         sides.append(jnp.concatenate([rows(place, E)] * half, axis=0).astype(BF16))
     if len(sides) < 2:
         sides += [jnp.zeros((half * E, 2 * s.X), BF16)] * (2 - len(sides))
-    return [jnp.concatenate([own] + order, axis=0) for order in (sides, sides[::-1])]
+    both = [jnp.concatenate([own] + order, axis=0) for order in (sides, sides[::-1])]
+    c, col = iota((s.X, s.X), 0) % (s.X // 2), iota((s.X, s.X), 1)
+    return both + [lookup(c - col // 2 + R, coarse, 2).astype(BF16)]
 
 
 def pick_y(s, up, fine):
@@ -239,11 +252,16 @@
     return jnp.where(near, 0.25, jnp.where(far, 1.0, 0.0)).astype(BF16)
 
 
-def xpass(s, weights, data, halos, v):
+def mix(s, halos, v):
     group = iota((1, s.V * E), 1) // E
-    mixed = jnp.zeros((data.shape[0], s.V * E), BF16)
+    mixed = jnp.zeros((halos[0].shape[0] if halos else 0, s.V * E), BF16)
     for i, halo in enumerate(halos):
         mixed = jnp.where(group == lane_group(s, i, v), halo, mixed)
+    return mixed
+
+
+def xpass(s, weights, data, halos, v):
+    mixed = mix(s, halos, v) if halos else jnp.zeros((data.shape[0], s.V * E), BF16)
     return dot(wide([data, mixed]), weights[v // (s.V // 2)]).astype(BF16)
 
 
@@ -270,18 +288,35 @@
     m = len(s.kz)
     faces, corners, refs = refs[:m], refs[m : 2 * m], refs[2 * m :]
     sides, packs = refs[:m], refs[m:]
-    halos = [
-        jnp.concatenate([c[i * s.face : (i + 1) * s.face, :] for c in corners], axis=0)
-        for i in range(len(s.kx))
-    ]
+    near, far = [], []
+    for i in range(len(s.kx)):
+        at = i * s.face
+        near.append(jnp.concatenate([c[at : at + s.raw, :] for c in corners], axis=0))
+        far.append(jnp.concatenate([c[at + s.raw : at + s.face, :] for c in corners], axis=0))
     for v in range(s.V):
         at = slice(v * s.X, (v + 1) * s.X)
-        data = jnp.concatenate([f[v] for f in faces], axis=0)
-        passed = xpass(s, weights, data, halos, v)
+        data = jnp.concatenate([f[v * s.raw : (v + 1) * s.raw, :] for f in faces], axis=0)
+        passed = xpass(s, weights, data, near, v)
         for i, side in enumerate(sides):
-            base = i * s.face
-            side[: s.raw, at] = passed[base : base + s.raw, : s.X]
-            side[s.raw :, at] = passed[base : base + s.face, s.X :]
+            rows = slice(i * s.raw, (i + 1) * s.raw)
+            side[: s.raw, at] = passed[rows, : s.X]
+            side[s.raw : 2 * s.raw, at] = passed[rows, s.X :]
+    right = iota((1, s.X), 1) // (s.X // 2)
+    half = s.V // 2
+    for h in range(2):
+        rows = []
+        for v in range(h * half, (h + 1) * half):
+            at = s.V * s.raw + v // 2 * s.avg
+            data = jnp.concatenate([f[at : at + s.avg, :] for f in faces], axis=0)
+            data = jnp.where(right == v % 2, data, jnp.zeros_like(data))
+            mixed = mix(s, far, v) if far else jnp.zeros_like(data)
+            rows.append(wide([data, mixed]))
+        w = jnp.concatenate([weights[2, : s.X, : s.X], weights[h, s.X :, s.X :]], axis=0)
+        passed = dot(jnp.concatenate(rows, axis=0), w).astype(BF16)
+        for v in range(h * half, (h + 1) * half):
+            for i, side in enumerate(sides):
+                at = ((v % half) * len(faces) + i) * s.avg
+                side[2 * s.raw :, v * s.X : (v + 1) * s.X] = passed[at : at + s.avg, :]
     gy = lax.axis_index("gy")
     for kind, pack in zip(s.ky, packs):
         up = upper(gy, kind)
@@ -481,8 +516,8 @@
     buffers = [pltpu.VMEM(field.shape, BF16), pltpu.SemaphoreType.DMA((s.chunks,))]
     top = shape(s.tz * s.V, s.tile)
     x_depth = s.X + s.V * E
-    outs = [shape(s.V, s.face, s.X)] * m + [shape(s.edge, s.V * E)] * n
-    outs += [top, shape(2, x_depth, 2 * s.X), shape(*field.shape)]
+    outs = [shape(s.sent, s.X)] * m + [shape(s.edge, s.V * E)] * n
+    outs += [top, shape(3, x_depth, 2 * s.X), shape(*field.shape)]
     far = [pltpu.with_memory_space_constraint(a, pltpu.HBM) for a in (field, *taps)]
     *faces, piece, weights, field = run(
         front_kernel,

time: 28.5 us -> 27.8 us (0.975)
  starting transfers between devices: 16.8 us -> 16.1 us
    ppermute x1, starting transfers between devices: 4.7 us -> 4 us  [shards(): across = lax.ppermute(known, 'gz', [(i, i ^ 2) for i in range(s.nz)])]
  transfers between devices with their start and end apart: 11 -> 11, of which waited for: 4 -> 4; matrix products, arithmetic and copies ran while one was open for 0% -> 0% of each run, Pallas kernels for 13% -> 14%
where the time goes in v6:
time: 27.8 us; the launch traced here: 27.6 us
  starting transfers between devices  16.1 us (58%)
  Pallas kernels  7.78 us (28%)
  waiting for transfers between devices  1.97 us (7%)
  local copies, waits for them, and re-layouts  1.6 us (6%)
    ppermute x8, starting transfers between devices, swap(): moved.append(lax.ppermute(a, axis, swaps(count, kind, ring)))  11.4 us
    pallas_call x8, Pallas kernels, run(): return list(call(*arrays))  7.78 us
    ppermute x1, starting transfers between devices, shards(): across = lax.ppermute(known, 'gz', [(i, i ^ 2) for i in range(s.nz)])  4 us
    unnamed x6, local copies, waits for them, and re-layouts  1.6 us
    ppermute x1, waiting for transfers between devices, shards(): across = lax.ppermute(known, 'gz', [(i, i ^ 2) for i in range(s.nz)])  0.78 us
    ppermute x1, waiting for transfers between devices, shards(): across = lax.ppermute(piece, 'gx', [(i, i ^ 2) for i in range(s.nx)])  0.69 us
    ppermute x1, starting transfers between devices, shards(): across = lax.ppermute(piece, 'gx', [(i, i ^ 2) for i in range(s.nx)])  0.57 us
  transfers between devices with their start and end apart: 11, of which 4 were waited for; matrix products, arithmetic and copies ran while one was open for 0% of the time, Pallas kernels for 14%

profile of v6, /device:TPU:0, one launch (start us, length us, event | category | flops | bytes accessed | tf_op | source)
XLA Modules:
  0.0 27.6 jit_solution(17662785852689661193)
XLA Ops:
  0.0 2.4 %shard_map.47 = (bf16[1152,128]{1,0:T(8,128)(2,1)S(1)}, bf16[1152,128]{1,0:T(8,128)(2,1)S(1)}, bf16[320,128]{1,0:T(8,128)(2,1)S(1)}, bf16[320,128]{1,0:T(8,128)(...) custom-call(bf16[16,16,16,128]{3,2,1,0:T(8,128)(2,1)} %refs_0_.3, ...), custom_call_target="tpu_custom_call" | custom-call | bytes 1048576 | tf_op jit(solution)/shard_map/pallas_call | solution.py:507
  2.4 3.0 %collective-permute-start = (bf16[320,128]{1,0:T(8,128)(2,1)S(1)}, bf16[320,128]{1,0:T(8,128)(2,1)S(1)}, u32[]{:S(2)}, u32[]{:S(2)}) collective-permute-start(bf16[320,128]{1,0:T(8,128)(2,1)S(1)} %get-tuple-element.25), channel_id=1, source_target_pairs={{0,8},{8,0},{16,24},{24,16},{1,9},{9,1},{17,25},{25,17},{2,10},{10... | collective-permute-start | bytes 245768 | tf_op jit(solution)/shard_map/ppermute | solution.py:512
  5.4 1.5 %collective-permute-start.1 = (bf16[320,128]{1,0:T(8,128)(2,1)S(1)}, bf16[320,128]{1,0:T(8,128)(2,1)S(1)}, u32[]{:S(2)}, u32[]{:S(2)}) collective-permute-start(bf16[320,128]{1,0:T(8,128)(2,1)S(1)} %get-tuple-element.26), channel_id=1, source_target_pairs={{8,16},{16,8},{0,24},{24,0},{9,17},{17,9},{1,25},{25,1},{10,18},{1... | collective-permute-start | bytes 245768 | tf_op jit(solution)/shard_map/ppermute | solution.py:512
  6.9 1.6 %collective-permute-start.3 = (bf16[1152,128]{1,0:T(8,128)(2,1)S(1)}, bf16[1152,128]{1,0:T(8,128)(2,1)S(1)}, u32[]{:S(2)}, u32[]{:S(2)}) collective-permute-start(bf16[1152,128]{1,0:T(8,128)(2,1)S(1)} %get-tuple-element.30), channel_id=1, source_target_pairs={{0,1},{1,0},{2,3},{3,2},{4,5},{5,4},{6,7},{7,6},{8,9},{9,8},{10,11... | collective-permute-start | bytes 884744 | tf_op jit(solution)/shard_map/ppermute | solution.py:512
  8.5 0.7 %collective-permute-start.4 = (bf16[1152,128]{1,0:T(8,128)(2,1)S(1)}, bf16[1152,128]{1,0:T(8,128)(2,1)S(1)}, u32[]{:S(2)}, u32[]{:S(2)}) collective-permute-start(bf16[1152,128]{1,0:T(8,128)(2,1)S(1)} %get-tuple-element.31), channel_id=1, source_target_pairs={{1,2},{2,1},{5,6},{6,5},{9,10},{10,9},{13,14},{14,13},{17,18},{18,... | collective-permute-start | bytes 884744 | tf_op jit(solution)/shard_map/ppermute | solution.py:512
  9.2 0.6 %collective-permute-start.5 = (bf16[32,128]{1,0:T(8,128)(2,1)S(1)}, bf16[32,128]{1,0:T(8,128)(2,1)S(1)}, u32[]{:S(2)}, u32[]{:S(2)}) collective-permute-start(bf16[32,128]{1,0:T(8,128)(2,1)S(1)} %get-tuple-element.32.refs_2_), channel_id=1, source_target_pairs={{0,16},{8,24},{16,0},{24,8},{1,17},{9,25},{17,1},{25,9},{2,18},{10... | collective-permute-start | bytes 24584 | tf_op jit(solution)/shard_map/ppermute | solution.py:539
  9.7 0.0 copy-start.1
  9.7 0.7 %copy-done.1 = f32[3,9]{1,0:T(4,128)S(1)} copy-done((f32[3,9]{1,0:T(4,128)S(1)}, f32[3,9]{1,0:T(4,128)}, u32[]{:S(2)}) %copy-start.1) | copy-done | bytes 132
  10.4 0.0 copy-start.2
  10.4 0.7 %copy-done.2 = f32[3,9]{1,0:T(4,128)S(1)} copy-done((f32[3,9]{1,0:T(4,128)S(1)}, f32[3,9]{1,0:T(4,128)}, u32[]{:S(2)}) %copy-start.2) | copy-done | bytes 132
  11.1 1.1 %shard_map.46 = (bf16[256,512]{1,0:T(8,128)(2,1)S(1)}, bf16[256,512]{1,0:T(8,128)(2,1)S(1)}) custom-call(f32[3,9]{1,0:T(4,128)S(1)} %copy-done.1, f32[3,9]{1,0:T(4,128)S(1)} %copy-done.2), custom_call_target="tpu_custom_call" | custom-call | flops 268435456 | bytes 1048576 | tf_op jit(solution)/shard_map/pallas_call | solution.py:507
  12.2 0.7 %collective-permute-done.5.refs_3_ = bf16[32,128]{1,0:T(8,128)(2,1)S(1)} collective-permute-done((bf16[32,128]{1,0:T(8,128)(2,1)S(1)}, bf16[32,128]{1,0:T(8,128)(2,1)S(1)}, u32[]{:S(2)}, u32[]{:S(2)}) %collective-permute-start.5) | collective-permute-done | bytes 8224 | tf_op jit(solution)/shard_map/ppermute | solution.py:539
  12.9 0.0 collective-permute-done.refs_2_.refs_0_
  12.9 0.0 collective-permute-done.1.refs_3_.refs_1_
  12.9 2.5 %collective-permute-start.7 = (bf16[192,128]{1,0:T(8,128)(2,1)S(1)}, bf16[192,128]{1,0:T(8,128)(2,1)S(1)}, u32[]{:S(2)}, u32[]{:S(2)}) collective-permute-start(bf16[192,128]{1,0:T(8,128)(2,1)S(1)} %get-tuple-element.34), channel_id=1, source_target_pairs={{1,2},{2,1},{0,3},{3,0},{5,6},{6,5},{4,7},{7,4},{9,10},{10,9},{8,1... | collective-permute-start | bytes 147464 | tf_op jit(solution)/shard_map/ppermute | solution.py:512
  15.4 1.0 %shard_map.48 = (bf16[512,2048]{1,0:T(8,128)(2,1)S(1)}, bf16[96,2048]{1,0:T(8,128)(2,1)S(1)}) custom-call(bf16[3,256,256]{2,1,0:T(8,128)(2,1)S(1)} %get-tuple-element.23.refs_0_, bf16[16,16,16,128]{3,2,1,0:T(8,128)(2,1)S(1)} %get-tuple-element.24.refs_1_, bf16[320,128]{1,0:T(8,128)(2,1)S(1)} %collective-permute-done.refs_2_.refs_0_, ...), custom_call_target="tpu_custom_call" | custom-call | flops 536870912 | bytes 1048576 | tf_op jit(solution)/shard_map/pallas_call | solution.py:507
  16.5 0.1 collective-permute-start.2
  16.6 2.0 %collective-permute-start.6 = (bf16[192,128]{1,0:T(8,128)(2,1)S(1)}, bf16[192,128]{1,0:T(8,128)(2,1)S(1)}, u32[]{:S(2)}, u32[]{:S(2)}) collective-permute-start(bf16[192,128]{1,0:T(8,128)(2,1)S(1)} %get-tuple-element.33), channel_id=1, source_target_pairs={{0,1},{1,0},{2,3},{3,2},{4,5},{5,4},{6,7},{7,6},{8,9},{9,8},{10,11... | collective-permute-start | bytes 147464 | tf_op jit(solution)/shard_map/ppermute | solution.py:512
  18.6 0.4 %collective-permute-done.7.refs_4_ = bf16[192,128]{1,0:T(8,128)(2,1)S(1)} collective-permute-done((bf16[192,128]{1,0:T(8,128)(2,1)S(1)}, bf16[192,128]{1,0:T(8,128)(2,1)S(1)}, u32[]{:S(2)}, u32[]{:S(2)}) %collective-permute-start.7) | collective-permute-done | bytes 49184 | tf_op jit(solution)/shard_map/ppermute | solution.py:512
  19.0 4.0 %collective-permute-start.9 = (bf16[32,128]{1,0:T(8,128)(2,1)S(1)}, bf16[32,128]{1,0:T(8,128)(2,1)S(1)}, u32[]{:S(2)}, u32[]{:S(2)}) collective-permute-start(bf16[32,128]{1,0:T(8,128)(2,1)S(1)} %get-tuple-element.38), channel_id=1, source_target_pairs={{0,2},{1,3},{2,0},{3,1},{4,6},{5,7},{6,4},{7,5},{8,10},{9,11},{10,... | collective-permute-start | bytes 24584 | tf_op jit(solution)/shard_map/ppermute | solution.py:545
  23.0 0.0 collective-permute-done.6.refs_3_
  23.0 0.0 collective-permute-done.3.refs_1_
  23.0 0.0 collective-permute-done.4.refs_2_
  23.0 0.7 %shard_map.51 = (bf16[144,2048]{1,0:T(8,128)(2,1)S(1)}, bf16[144,2048]{1,0:T(8,128)(2,1)S(1)}, bf16[64,2048]{1,0:T(8,128)(2,1)S(1)}) custom-call(bf16[3,256,256]{2,1,0:T(8,128)(2,1)S(1)} %get-tuple-element.23.refs_0_, bf16[1152,128]{1,0:T(8,128)(2,1)S(1)} %collective-permute-done.3.refs_1_, bf16[1152,128]{1,0:T(8,128)(2,1)S(1)} %collective-permute-done.4.refs_2_, ...), custom_call_target="tpu_custom_call" | custom-call | bytes 1048576 | tf_op jit(solution)/shard_map/pallas_call | solution.py:507
  23.7 0.1 collective-permute-start.8
  23.8 0.8 %collective-permute-done.9 = bf16[32,128]{1,0:T(8,128)(2,1)S(1)} collective-permute-done((bf16[32,128]{1,0:T(8,128)(2,1)S(1)}, bf16[32,128]{1,0:T(8,128)(2,1)S(1)}, u32[]{:S(2)}, u32[]{:S(2)}) %collective-permute-start.9) | collective-permute-done | bytes 8224 | tf_op jit(solution)/shard_map/ppermute | solution.py:545
  24.6 0.1 collective-permute-start.10
  24.7 0.0 copy-start
  24.7 0.7 %shard_map.49.refs_0_ = f32[256,2048]{1,0:T(8,128)S(1)} custom-call(bf16[256,512]{1,0:T(8,128)(2,1)S(1)} %get-tuple-element.22.refs_0_, bf16[512,2048]{1,0:T(8,128)(2,1)S(1)} %get-tuple-element.27.refs_1_), custom_call_target="tpu_custom_call" | custom-call | flops 536870912 | bytes 1048576 | tf_op jit(solution)/shard_map/pallas_call | solution.py:507
  25.4 0.2 copy-done
  25.6 0.2 shard_map.52.refs_6_
  25.8 0.1 collective-permute-done.10
  25.9 0.0 collective-permute-done.2.refs_2_
  25.9 0.0 collective-permute-done.8.refs_5_
  25.9 1.7 %shard_map.53 = bf16[16,16,16,128]{3,2,1,0:T(8,128)(2,1)} custom-call(f32[256,2048]{1,0:T(8,128)S(1)} %shard_map.49.refs_0_, bf16[256,512]{1,0:T(8,128)(2,1)S(1)} %get-tuple-element.28.refs_1_, bf16[96,2048]{1,0:T(8,128)(2,1)S(1)} %collective-permute-done.2.refs_2_, bf16[144,2048]{1,0:T(8,128)(2,1)S(1)} %get-tuple-element.35.refs_3_, ...), custom_call_target="tpu_custom_call" | custom-call | bytes 1048576 | tf_op jit(solution)/shard_map/pallas_call | solution.py:507
  (5 shorter events, 0.0 us)
Async XLA Ops:
  2.4 10.5 %collective-permute-start = (bf16[320,128]{1,0:T(8,128)(2,1)S(1)}, bf16[320,128]{1,0:T(8,128)(2,1)S(1)}, u32[]{:S(2)}, u32[]{:S(2)}) collective-permute-start(bf16[320,128]{1,0:T(8,128)(2,1)S(1)} %get-tuple-element.25), channel_id=1, source_target_pairs={{0,8},{8,0},{16,24},{24,16},{1,9},{9,1},{17,25},{25,17},{2,10},{10... | collective-permute-start | bytes 245768 | tf_op jit(solution)/shard_map/ppermute | solution.py:512
  5.4 7.5 %collective-permute-start.1 = (bf16[320,128]{1,0:T(8,128)(2,1)S(1)}, bf16[320,128]{1,0:T(8,128)(2,1)S(1)}, u32[]{:S(2)}, u32[]{:S(2)}) collective-permute-start(bf16[320,128]{1,0:T(8,128)(2,1)S(1)} %get-tuple-element.26), channel_id=1, source_target_pairs={{8,16},{16,8},{0,24},{24,0},{9,17},{17,9},{1,25},{25,1},{10,18},{1... | collective-permute-start | bytes 245768 | tf_op jit(solution)/shard_map/ppermute | solution.py:512
  6.9 16.1 %collective-permute-start.3 = (bf16[1152,128]{1,0:T(8,128)(2,1)S(1)}, bf16[1152,128]{1,0:T(8,128)(2,1)S(1)}, u32[]{:S(2)}, u32[]{:S(2)}) collective-permute-start(bf16[1152,128]{1,0:T(8,128)(2,1)S(1)} %get-tuple-element.30), channel_id=1, source_target_pairs={{0,1},{1,0},{2,3},{3,2},{4,5},{5,4},{6,7},{7,6},{8,9},{9,8},{10,11... | collective-permute-start | bytes 884744 | tf_op jit(solution)/shard_map/ppermute | solution.py:512
  8.5 14.5 %collective-permute-start.4 = (bf16[1152,128]{1,0:T(8,128)(2,1)S(1)}, bf16[1152,128]{1,0:T(8,128)(2,1)S(1)}, u32[]{:S(2)}, u32[]{:S(2)}) collective-permute-start(bf16[1152,128]{1,0:T(8,128)(2,1)S(1)} %get-tuple-element.31), channel_id=1, source_target_pairs={{1,2},{2,1},{5,6},{6,5},{9,10},{10,9},{13,14},{14,13},{17,18},{18,... | collective-permute-start | bytes 884744 | tf_op jit(solution)/shard_map/ppermute | solution.py:512
  9.2 3.7 %collective-permute-start.5 = (bf16[32,128]{1,0:T(8,128)(2,1)S(1)}, bf16[32,128]{1,0:T(8,128)(2,1)S(1)}, u32[]{:S(2)}, u32[]{:S(2)}) collective-permute-start(bf16[32,128]{1,0:T(8,128)(2,1)S(1)} %get-tuple-element.32.refs_2_), channel_id=1, source_target_pairs={{0,16},{8,24},{16,0},{24,8},{1,17},{9,25},{17,1},{25,9},{2,18},{10... | collective-permute-start | bytes 24584 | tf_op jit(solution)/shard_map/ppermute | solution.py:539
  9.7 0.7 %copy-start.1 = (f32[3,9]{1,0:T(4,128)S(1)}, f32[3,9]{1,0:T(4,128)}, u32[]{:S(2)}) copy-start(f32[3,9]{1,0:T(4,128)} %refs_1_.3) | copy-start | bytes 328
  10.4 0.7 %copy-start.2 = (f32[3,9]{1,0:T(4,128)S(1)}, f32[3,9]{1,0:T(4,128)}, u32[]{:S(2)}) copy-start(f32[3,9]{1,0:T(4,128)} %refs_2_.1) | copy-start | bytes 328
  12.9 6.1 %collective-permute-start.7 = (bf16[192,128]{1,0:T(8,128)(2,1)S(1)}, bf16[192,128]{1,0:T(8,128)(2,1)S(1)}, u32[]{:S(2)}, u32[]{:S(2)}) collective-permute-start(bf16[192,128]{1,0:T(8,128)(2,1)S(1)} %get-tuple-element.34), channel_id=1, source_target_pairs={{1,2},{2,1},{0,3},{3,0},{5,6},{6,5},{4,7},{7,4},{9,10},{10,9},{8,1... | collective-permute-start | bytes 147464 | tf_op jit(solution)/shard_map/ppermute | solution.py:512
  16.5 9.4 %collective-permute-start.2 = (bf16[96,2048]{1,0:T(8,128)(2,1)S(1)}, bf16[96,2048]{1,0:T(8,128)(2,1)S(1)}, u32[]{:S(2)}, u32[]{:S(2)}) collective-permute-start(bf16[96,2048]{1,0:T(8,128)(2,1)S(1)} %get-tuple-element.29), channel_id=1, source_target_pairs={{0,4},{4,0},{1,5},{5,1},{2,6},{6,2},{3,7},{7,3},{8,12},{12,8},{9,1... | collective-permute-start | bytes 1179656 | tf_op jit(solution)/shard_map/ppermute | solution.py:512
  16.6 6.4 %collective-permute-start.6 = (bf16[192,128]{1,0:T(8,128)(2,1)S(1)}, bf16[192,128]{1,0:T(8,128)(2,1)S(1)}, u32[]{:S(2)}, u32[]{:S(2)}) collective-permute-start(bf16[192,128]{1,0:T(8,128)(2,1)S(1)} %get-tuple-element.33), channel_id=1, source_target_pairs={{0,1},{1,0},{2,3},{3,2},{4,5},{5,4},{6,7},{7,6},{8,9},{9,8},{10,11... | collective-permute-start | bytes 147464 | tf_op jit(solution)/shard_map/ppermute | solution.py:512
  19.0 5.6 %collective-permute-start.9 = (bf16[32,128]{1,0:T(8,128)(2,1)S(1)}, bf16[32,128]{1,0:T(8,128)(2,1)S(1)}, u32[]{:S(2)}, u32[]{:S(2)}) collective-permute-start(bf16[32,128]{1,0:T(8,128)(2,1)S(1)} %get-tuple-element.38), channel_id=1, source_target_pairs={{0,2},{1,3},{2,0},{3,1},{4,6},{5,7},{6,4},{7,5},{8,10},{9,11},{10,... | collective-permute-start | bytes 24584 | tf_op jit(solution)/shard_map/ppermute | solution.py:545
  23.7 2.2 %collective-permute-start.8 = (bf16[64,2048]{1,0:T(8,128)(2,1)S(1)}, bf16[64,2048]{1,0:T(8,128)(2,1)S(1)}, u32[]{:S(2)}, u32[]{:S(2)}) collective-permute-start(bf16[64,2048]{1,0:T(8,128)(2,1)S(1)} %get-tuple-element.37), channel_id=1, source_target_pairs={{0,4},{4,0},{1,5},{5,1},{2,6},{6,2},{3,7},{7,3},{8,12},{12,8},{9,1... | collective-permute-start | bytes 786440 | tf_op jit(solution)/shard_map/ppermute | solution.py:512
  24.6 1.3 %collective-permute-start.10 = (bf16[1,4,32,128]{3,2,1,0:T(8,128)(2,1)S(1)}, bf16[1,4,32,128]{3,2,1,0:T(8,128)(2,1)S(1)}, u32[]{:S(2)}, u32[]{:S(2)}) collective-permute-start(bf16[1,4,32,128]{3,2,1,0:T(8,128)(2,1)S(1)} %get-tuple-element.39), channel_id=1, source_target_pairs={{0,4},{4,0},{1,5},{5,1},{2,6},{6,2},{3,7},{7,3},{8,12},{12,8},{9,1... | collective-permute-start | bytes 98312 | tf_op jit(solution)/shard_map/ppermute | solution.py:471
  24.7 1.0 %copy-start = (bf16[2,2,16,2048]{3,2,1,0:T(8,128)(2,1)S(1)}, bf16[2,2,16,2048]{3,2,1,0:T(8,128)(2,1)}, u32[]{:S(2)}) copy-start(bf16[2,2,16,2048]{3,2,1,0:T(8,128)(2,1)} %param.7) | copy-start | bytes 786436

commit v7 on v6

--- a/solution.py
+++ b/solution.py
@@ -51,6 +51,11 @@
 
 def one(condition, value=1.0):
     return jnp.where(condition, value, 0.0).astype(BF16)
+
+
+def split(a):
+    high = a.astype(BF16)
+    return high, (a - high.astype(F32)).astype(BF16)
 
 
 def wide(parts):
@@ -211,18 +216,18 @@
         col = iota((count, s.X), 1)
         a = lookup(place - col + R, fine, 2)
         b = 0.5 * lookup((place + E) // 2 - col // 2, coarse, 2)
-        return wide([a, b])
+        return wide([*split(a), b.astype(BF16)])
 
     half = s.V // 2
-    own = rows(iota((s.X, s.X), 0), s.X).astype(BF16)
+    own = rows(iota((s.X, s.X), 0), s.X)
     sides = []
     for kind in s.kx:
         c = iota((E, s.X), 0)
         place = jnp.where(upper(gx, kind), s.X + c, c - E)
         place = jnp.where(partner_missing(gx, s.nx, kind), -4 * s.X, place)
-        sides.append(jnp.concatenate([rows(place, E)] * half, axis=0).astype(BF16))
+        sides.append(jnp.concatenate([rows(place, E).astype(F32)] * half, axis=0).astype(BF16))
     if len(sides) < 2:
-        sides += [jnp.zeros((half * E, 2 * s.X), BF16)] * (2 - len(sides))
+        sides += [jnp.zeros((half * E, 3 * s.X), BF16)] * (2 - len(sides))
     both = [jnp.concatenate([own] + order, axis=0) for order in (sides, sides[::-1])]
     c, col = iota((s.X, s.X), 0) % (s.X // 2), iota((s.X, s.X), 1)
     return both + [lookup(c - col // 2 + R, coarse, 2).astype(BF16)]
@@ -262,7 +267,9 @@
 
 def xpass(s, weights, data, halos, v):
     mixed = mix(s, halos, v) if halos else jnp.zeros((data.shape[0], s.V * E), BF16)
-    return dot(wide([data, mixed]), weights[v // (s.V // 2)]).astype(BF16)
+    passed = dot(wide([data, mixed]), weights[v // (s.V // 2)])
+    fine = passed[:, : s.X] + passed[:, s.X : 2 * s.X]
+    return fine.astype(BF16), passed[:, 2 * s.X :].astype(BF16)
 
 
 def lane_group(s, place, v):
@@ -274,9 +281,9 @@
     halos, (own, *packs) = [h[: s.rows, :] for h in refs[:n]], refs[n:]
     for v in range(s.V):
         at = slice(v * s.X, (v + 1) * s.X)
-        passed = xpass(s, weights, field[v].reshape(s.rows, s.X), halos, v)
-        own[: s.rows, at] = passed[:, : s.X]
-        own[s.rows :, at] = passed[:, s.X :]
+        fine, coarse = xpass(s, weights, field[v].reshape(s.rows, s.X), halos, v)
+        own[: s.rows, at] = fine
+        own[s.rows :, at] = coarse
     gy = lax.axis_index("gy")
     for kind, pack in zip(s.ky, packs):
         up = upper(gy, kind)
@@ -296,11 +303,11 @@
     for v in range(s.V):
         at = slice(v * s.X, (v + 1) * s.X)
         data = jnp.concatenate([f[v * s.raw : (v + 1) * s.raw, :] for f in faces], axis=0)
-        passed = xpass(s, weights, data, near, v)
+        fine, coarse = xpass(s, weights, data, near, v)
         for i, side in enumerate(sides):
             rows = slice(i * s.raw, (i + 1) * s.raw)
-            side[: s.raw, at] = passed[rows, : s.X]
-            side[s.raw : 2 * s.raw, at] = passed[rows, s.X :]
+            side[: s.raw, at] = fine[rows, :]
+            side[s.raw : 2 * s.raw, at] = coarse[rows, :]
     right = iota((1, s.X), 1) // (s.X // 2)
     half = s.V // 2
     for h in range(2):
@@ -311,7 +318,7 @@
             data = jnp.where(right == v % 2, data, jnp.zeros_like(data))
             mixed = mix(s, far, v) if far else jnp.zeros_like(data)
             rows.append(wide([data, mixed]))
-        w = jnp.concatenate([weights[2, : s.X, : s.X], weights[h, s.X :, s.X :]], axis=0)
+        w = jnp.concatenate([weights[2, : s.X, : s.X], weights[h, s.X :, 2 * s.X :]], axis=0)
         passed = dot(jnp.concatenate(rows, axis=0), w).astype(BF16)
         for v in range(h * half, (h + 1) * half):
             for i, side in enumerate(sides):
@@ -339,13 +346,21 @@
         if scale is not None:
             b = b * scale
         both = a.reshape(s.Z, 1, count) * b.reshape(1, s.Y, count)
-        return both.reshape(s.rows, count).astype(BF16)
+        both = both.reshape(s.rows, count)
+        if div == 2:
+            return both.astype(BF16)
+        high, low = split(both)
+        lows.append(low)
+        return high
+
+    lows = []
 
     c = iota((1, s.rows), 1)
     first = [
         block(fine, c // s.Y, c % s.Y, 1),
         block(coarse, c // s.Y // 2, c % s.Y // 2, 2, 0.25),
     ]
+    first += [lows.pop()]
     second = []
 
     def zplace(kind, z):
@@ -385,7 +400,7 @@
     r, c = iota((s.rows, s.top), 0), iota((s.rows, s.top), 1)
     z, y = r // s.Y // (s.Z // s.tz), r % s.Y // (s.Y // s.ty)
     second.append(one(c // s.tx == z * s.ty + y))
-    return first, second
+    return first, second + lows
 
 
 def top_product(s, kernel, parts, total):
@@ -410,7 +425,8 @@
     step = min(s.lanes, 4 * s.X)
     for at in range(0, s.lanes, step):
         cols = slice(at, at + step)
-        total[:, cols] = dot(now[...], own[:, cols])
+        parts = [own[:, cols], own[: s.rows, cols]]
+        total[:, cols] = dot(now[...], jnp.concatenate(parts, axis=0))
 
 
 def top_own_kernel(s, known, kernel, total):
@@ -444,6 +460,9 @@
         top = wide([jnp.where(spread, line, 0.0).astype(BF16) for line in lines])
         parts = [x[:, cols] for x in (*ends, *sides)]
         parts += [x[:, cols] for x in packs] + [top]
+        parts += [x[: s.yf, cols] for x in ends] + [x[: s.raw, cols] for x in sides]
+        step = s.zyf + s.zyc
+        parts += [x[j * step : j * step + s.zyf, cols] for x in packs for j in range(m)]
         result = (dot(later[...], jnp.concatenate(parts, axis=0)) + partial[:, cols]).astype(BF16)
         for i in range(pair):
             held[v + i] = result[:, i * s.X : (i + 1) * s.X].reshape(s.Z, s.Y, s.X)
@@ -517,7 +536,7 @@
     top = shape(s.tz * s.V, s.tile)
     x_depth = s.X + s.V * E
     outs = [shape(s.sent, s.X)] * m + [shape(s.edge, s.V * E)] * n
-    outs += [top, shape(3, x_depth, 2 * s.X), shape(*field.shape)]
+    outs += [top, shape(3, x_depth, 3 * s.X), shape(*field.shape)]
     far = [pltpu.with_memory_space_constraint(a, pltpu.HBM) for a in (field, *taps)]
     *faces, piece, weights, field = run(
         front_kernel,
@@ -548,10 +567,11 @@
     else:
         known = gather(gather(piece, "gx", s.nx, sum)[None], "gz", s.nz, stack)
     later = k * (s.yf + s.yc) + m * s.gz + k * s.ypack + s.top
+    later += k * s.yf + m * s.raw + k * m * s.zyf
     w_now, w_later = run(
         weights_kernel,
         taps,
-        [shape(s.rows, 2 * s.rows), shape(s.rows, later)],
+        [shape(s.rows, 3 * s.rows), shape(s.rows, later)],
         scalars=2,
         flops=1 << 28,
     )

time: 27.8 us -> 28 us (level)
  Pallas kernels: 7.78 us -> 9.19 us
  waiting for transfers between devices: 1.97 us -> 1.11 us
    pallas_call x8, Pallas kernels: 7.78 us -> 9.19 us  [run(): return list(call(*arrays))]
    ppermute x8, waiting for transfers between devices: 0.43 us -> 0.02 us  [swap(): moved.append(lax.ppermute(a, axis, swaps(count, kind, ring)))]
  transfers between devices with their start and end apart: 11 -> 11, of which waited for: 4 -> 2; matrix products, arithmetic and copies ran while one was open for 0% -> 0% of each run, Pallas kernels for 14% -> 18%
where the time goes in v7:
time: 28 us; the launch traced here: 27.8 us
  starting transfers between devices  16 us (57%)
  Pallas kernels  9.19 us (33%)
  local copies, waits for them, and re-layouts  1.37 us (5%)
  waiting for transfers between devices  1.11 us (4%)
    ppermute x8, starting transfers between devices, swap(): moved.append(lax.ppermute(a, axis, swaps(count, kind, ring)))  11.4 us
    pallas_call x8, Pallas kernels, run(): return list(call(*arrays))  9.19 us
    ppermute x1, starting transfers between devices, shards(): across = lax.ppermute(known, 'gz', [(i, i ^ 2) for i in range(s.nz)])  3.94 us
    unnamed x6, local copies, waits for them, and re-layouts  1.37 us
    ppermute x1, starting transfers between devices, shards(): across = lax.ppermute(piece, 'gx', [(i, i ^ 2) for i in range(s.nx)])  0.57 us
  transfers between devices with their start and end apart: 11, of which 2 were waited for; matrix products, arithmetic and copies ran while one was open for 0% of the time, Pallas kernels for 18%

profile of v7, /device:TPU:0, one launch (start us, length us, event | category | flops | bytes accessed | tf_op | source)
XLA Modules:
  0.0 27.8 jit_solution(885679401423709743)
XLA Ops:
  0.0 2.4 %shard_map.47 = (bf16[1152,128]{1,0:T(8,128)(2,1)S(1)}, bf16[1152,128]{1,0:T(8,128)(2,1)S(1)}, bf16[320,128]{1,0:T(8,128)(2,1)S(1)}, bf16[320,128]{1,0:T(8,128)(...) custom-call(bf16[16,16,16,128]{3,2,1,0:T(8,128)(2,1)} %refs_0_.3, ...), custom_call_target="tpu_custom_call" | custom-call | bytes 1048576 | tf_op jit(solution)/shard_map/pallas_call | solution.py:526
  2.4 3.0 %collective-permute-start = (bf16[320,128]{1,0:T(8,128)(2,1)S(1)}, bf16[320,128]{1,0:T(8,128)(2,1)S(1)}, u32[]{:S(2)}, u32[]{:S(2)}) collective-permute-start(bf16[320,128]{1,0:T(8,128)(2,1)S(1)} %get-tuple-element.25), channel_id=1, source_target_pairs={{0,8},{8,0},{16,24},{24,16},{1,9},{9,1},{17,25},{25,17},{2,10},{10... | collective-permute-start | bytes 245768 | tf_op jit(solution)/shard_map/ppermute | solution.py:531
  5.4 1.5 %collective-permute-start.1 = (bf16[320,128]{1,0:T(8,128)(2,1)S(1)}, bf16[320,128]{1,0:T(8,128)(2,1)S(1)}, u32[]{:S(2)}, u32[]{:S(2)}) collective-permute-start(bf16[320,128]{1,0:T(8,128)(2,1)S(1)} %get-tuple-element.26), channel_id=1, source_target_pairs={{8,16},{16,8},{0,24},{24,0},{9,17},{17,9},{1,25},{25,1},{10,18},{1... | collective-permute-start | bytes 245768 | tf_op jit(solution)/shard_map/ppermute | solution.py:531
  6.9 1.6 %collective-permute-start.3 = (bf16[1152,128]{1,0:T(8,128)(2,1)S(1)}, bf16[1152,128]{1,0:T(8,128)(2,1)S(1)}, u32[]{:S(2)}, u32[]{:S(2)}) collective-permute-start(bf16[1152,128]{1,0:T(8,128)(2,1)S(1)} %get-tuple-element.30), channel_id=1, source_target_pairs={{0,1},{1,0},{2,3},{3,2},{4,5},{5,4},{6,7},{7,6},{8,9},{9,8},{10,11... | collective-permute-start | bytes 884744 | tf_op jit(solution)/shard_map/ppermute | solution.py:531
  8.5 0.7 %collective-permute-start.4 = (bf16[1152,128]{1,0:T(8,128)(2,1)S(1)}, bf16[1152,128]{1,0:T(8,128)(2,1)S(1)}, u32[]{:S(2)}, u32[]{:S(2)}) collective-permute-start(bf16[1152,128]{1,0:T(8,128)(2,1)S(1)} %get-tuple-element.31), channel_id=1, source_target_pairs={{1,2},{2,1},{5,6},{6,5},{9,10},{10,9},{13,14},{14,13},{17,18},{18,... | collective-permute-start | bytes 884744 | tf_op jit(solution)/shard_map/ppermute | solution.py:531
  9.2 0.6 %collective-permute-start.5 = (bf16[32,128]{1,0:T(8,128)(2,1)S(1)}, bf16[32,128]{1,0:T(8,128)(2,1)S(1)}, u32[]{:S(2)}, u32[]{:S(2)}) collective-permute-start(bf16[32,128]{1,0:T(8,128)(2,1)S(1)} %get-tuple-element.32.refs_2_), channel_id=1, source_target_pairs={{0,16},{8,24},{16,0},{24,8},{1,17},{9,25},{17,1},{25,9},{2,18},{10... | collective-permute-start | bytes 24584 | tf_op jit(solution)/shard_map/ppermute | solution.py:558
  9.7 0.0 copy-start.1
  9.7 0.7 %copy-done.1 = f32[3,9]{1,0:T(4,128)S(1)} copy-done((f32[3,9]{1,0:T(4,128)S(1)}, f32[3,9]{1,0:T(4,128)}, u32[]{:S(2)}) %copy-start.1) | copy-done | bytes 132
  10.4 0.0 copy-start.2
  10.4 0.7 %copy-done.2 = f32[3,9]{1,0:T(4,128)S(1)} copy-done((f32[3,9]{1,0:T(4,128)S(1)}, f32[3,9]{1,0:T(4,128)}, u32[]{:S(2)}) %copy-start.2) | copy-done | bytes 132
  11.1 1.2 %shard_map.46 = (bf16[256,768]{1,0:T(8,128)(2,1)S(1)}, bf16[256,736]{1,0:T(8,128)(2,1)S(1)}) custom-call(f32[3,9]{1,0:T(4,128)S(1)} %copy-done.1, f32[3,9]{1,0:T(4,128)S(1)} %copy-done.2), custom_call_target="tpu_custom_call" | custom-call | flops 268435456 | bytes 1048576 | tf_op jit(solution)/shard_map/pallas_call | solution.py:526
  12.3 0.5 %collective-permute-done.5.refs_3_ = bf16[32,128]{1,0:T(8,128)(2,1)S(1)} collective-permute-done((bf16[32,128]{1,0:T(8,128)(2,1)S(1)}, bf16[32,128]{1,0:T(8,128)(2,1)S(1)}, u32[]{:S(2)}, u32[]{:S(2)}) %collective-permute-start.5) | collective-permute-done | bytes 8224 | tf_op jit(solution)/shard_map/ppermute | solution.py:558
  12.9 0.0 collective-permute-done.refs_2_.refs_0_
  12.9 0.0 collective-permute-done.1.refs_3_.refs_1_
  12.9 2.5 %collective-permute-start.7 = (bf16[192,128]{1,0:T(8,128)(2,1)S(1)}, bf16[192,128]{1,0:T(8,128)(2,1)S(1)}, u32[]{:S(2)}, u32[]{:S(2)}) collective-permute-start(bf16[192,128]{1,0:T(8,128)(2,1)S(1)} %get-tuple-element.34), channel_id=1, source_target_pairs={{1,2},{2,1},{0,3},{3,0},{5,6},{6,5},{4,7},{7,4},{9,10},{10,9},{8,1... | collective-permute-start | bytes 147464 | tf_op jit(solution)/shard_map/ppermute | solution.py:531
  15.4 1.5 %shard_map.48 = (bf16[512,2048]{1,0:T(8,128)(2,1)S(1)}, bf16[96,2048]{1,0:T(8,128)(2,1)S(1)}) custom-call(bf16[3,256,384]{2,1,0:T(8,128)(2,1)S(1)} %get-tuple-element.23.refs_0_, bf16[16,16,16,128]{3,2,1,0:T(8,128)(2,1)S(1)} %get-tuple-element.24.refs_1_, bf16[320,128]{1,0:T(8,128)(2,1)S(1)} %collective-permute-done.refs_2_.refs_0_, ...), custom_call_target="tpu_custom_call" | custom-call | flops 536870912 | bytes 1048576 | tf_op jit(solution)/shard_map/pallas_call | solution.py:526
  17.0 0.1 collective-permute-start.2
  17.0 2.0 %collective-permute-start.6 = (bf16[192,128]{1,0:T(8,128)(2,1)S(1)}, bf16[192,128]{1,0:T(8,128)(2,1)S(1)}, u32[]{:S(2)}, u32[]{:S(2)}) collective-permute-start(bf16[192,128]{1,0:T(8,128)(2,1)S(1)} %get-tuple-element.33), channel_id=1, source_target_pairs={{0,1},{1,0},{2,3},{3,2},{4,5},{5,4},{6,7},{7,6},{8,9},{9,8},{10,11... | collective-permute-start | bytes 147464 | tf_op jit(solution)/shard_map/ppermute | solution.py:531
  19.0 0.0 collective-permute-done.7.refs_4_
  19.0 3.9 %collective-permute-start.9 = (bf16[32,128]{1,0:T(8,128)(2,1)S(1)}, bf16[32,128]{1,0:T(8,128)(2,1)S(1)}, u32[]{:S(2)}, u32[]{:S(2)}) collective-permute-start(bf16[32,128]{1,0:T(8,128)(2,1)S(1)} %get-tuple-element.38), channel_id=1, source_target_pairs={{0,2},{1,3},{2,0},{3,1},{4,6},{5,7},{6,4},{7,5},{8,10},{9,11},{10,... | collective-permute-start | bytes 24584 | tf_op jit(solution)/shard_map/ppermute | solution.py:564
  23.0 0.0 collective-permute-done.6.refs_3_
  23.0 0.0 collective-permute-done.3.refs_1_
  23.0 0.0 collective-permute-done.4.refs_2_
  23.0 1.0 %shard_map.51 = (bf16[144,2048]{1,0:T(8,128)(2,1)S(1)}, bf16[144,2048]{1,0:T(8,128)(2,1)S(1)}, bf16[64,2048]{1,0:T(8,128)(2,1)S(1)}) custom-call(bf16[3,256,384]{2,1,0:T(8,128)(2,1)S(1)} %get-tuple-element.23.refs_0_, bf16[1152,128]{1,0:T(8,128)(2,1)S(1)} %collective-permute-done.3.refs_1_, bf16[1152,128]{1,0:T(8,128)(2,1)S(1)} %collective-permute-done.4.refs_2_, ...), custom_call_target="tpu_custom_call" | custom-call | bytes 1048576 | tf_op jit(solution)/shard_map/pallas_call | solution.py:526
  24.0 0.1 collective-permute-start.8
  24.1 0.5 %collective-permute-done.9 = bf16[32,128]{1,0:T(8,128)(2,1)S(1)} collective-permute-done((bf16[32,128]{1,0:T(8,128)(2,1)S(1)}, bf16[32,128]{1,0:T(8,128)(2,1)S(1)}, u32[]{:S(2)}, u32[]{:S(2)}) %collective-permute-start.9) | collective-permute-done | bytes 8224 | tf_op jit(solution)/shard_map/ppermute | solution.py:564
  24.6 0.1 collective-permute-start.10
  24.7 0.0 copy-start
  24.7 1.0 %shard_map.49.refs_0_ = f32[256,2048]{1,0:T(8,128)S(1)} custom-call(bf16[256,768]{1,0:T(8,128)(2,1)S(1)} %get-tuple-element.22.refs_0_, bf16[512,2048]{1,0:T(8,128)(2,1)S(1)} %get-tuple-element.27.refs_1_), custom_call_target="tpu_custom_call" | custom-call | flops 536870912 | bytes 1048576 | tf_op jit(solution)/shard_map/pallas_call | solution.py:526
  25.7 0.0 copy-done
  25.7 0.2 shard_map.52.refs_6_
  25.9 0.0 collective-permute-done.10
  25.9 0.0 collective-permute-done.2.refs_2_
  25.9 0.0 collective-permute-done.8.refs_5_
  25.9 1.9 %shard_map.53 = bf16[16,16,16,128]{3,2,1,0:T(8,128)(2,1)} custom-call(f32[256,2048]{1,0:T(8,128)S(1)} %shard_map.49.refs_0_, bf16[256,736]{1,0:T(8,128)(2,1)S(1)} %get-tuple-element.28.refs_1_, bf16[96,2048]{1,0:T(8,128)(2,1)S(1)} %collective-permute-done.2.refs_2_, bf16[144,2048]{1,0:T(8,128)(2,1)S(1)} %get-tuple-element.35.refs_3_, ...), custom_call_target="tpu_custom_call" | custom-call | bytes 1048576 | tf_op jit(solution)/shard_map/pallas_call | solution.py:526
  (5 shorter events, 0.0 us)
Async XLA Ops:
  2.4 10.5 %collective-permute-start = (bf16[320,128]{1,0:T(8,128)(2,1)S(1)}, bf16[320,128]{1,0:T(8,128)(2,1)S(1)}, u32[]{:S(2)}, u32[]{:S(2)}) collective-permute-start(bf16[320,128]{1,0:T(8,128)(2,1)S(1)} %get-tuple-element.25), channel_id=1, source_target_pairs={{0,8},{8,0},{16,24},{24,16},{1,9},{9,1},{17,25},{25,17},{2,10},{10... | collective-permute-start | bytes 245768 | tf_op jit(solution)/shard_map/ppermute | solution.py:531
  5.4 7.5 %collective-permute-start.1 = (bf16[320,128]{1,0:T(8,128)(2,1)S(1)}, bf16[320,128]{1,0:T(8,128)(2,1)S(1)}, u32[]{:S(2)}, u32[]{:S(2)}) collective-permute-start(bf16[320,128]{1,0:T(8,128)(2,1)S(1)} %get-tuple-element.26), channel_id=1, source_target_pairs={{8,16},{16,8},{0,24},{24,0},{9,17},{17,9},{1,25},{25,1},{10,18},{1... | collective-permute-start | bytes 245768 | tf_op jit(solution)/shard_map/ppermute | solution.py:531
  6.9 16.1 %collective-permute-start.3 = (bf16[1152,128]{1,0:T(8,128)(2,1)S(1)}, bf16[1152,128]{1,0:T(8,128)(2,1)S(1)}, u32[]{:S(2)}, u32[]{:S(2)}) collective-permute-start(bf16[1152,128]{1,0:T(8,128)(2,1)S(1)} %get-tuple-element.30), channel_id=1, source_target_pairs={{0,1},{1,0},{2,3},{3,2},{4,5},{5,4},{6,7},{7,6},{8,9},{9,8},{10,11... | collective-permute-start | bytes 884744 | tf_op jit(solution)/shard_map/ppermute | solution.py:531
  8.5 14.5 %collective-permute-start.4 = (bf16[1152,128]{1,0:T(8,128)(2,1)S(1)}, bf16[1152,128]{1,0:T(8,128)(2,1)S(1)}, u32[]{:S(2)}, u32[]{:S(2)}) collective-permute-start(bf16[1152,128]{1,0:T(8,128)(2,1)S(1)} %get-tuple-element.31), channel_id=1, source_target_pairs={{1,2},{2,1},{5,6},{6,5},{9,10},{10,9},{13,14},{14,13},{17,18},{18,... | collective-permute-start | bytes 884744 | tf_op jit(solution)/shard_map/ppermute | solution.py:531
  9.2 3.7 %collective-permute-start.5 = (bf16[32,128]{1,0:T(8,128)(2,1)S(1)}, bf16[32,128]{1,0:T(8,128)(2,1)S(1)}, u32[]{:S(2)}, u32[]{:S(2)}) collective-permute-start(bf16[32,128]{1,0:T(8,128)(2,1)S(1)} %get-tuple-element.32.refs_2_), channel_id=1, source_target_pairs={{0,16},{8,24},{16,0},{24,8},{1,17},{9,25},{17,1},{25,9},{2,18},{10... | collective-permute-start | bytes 24584 | tf_op jit(solution)/shard_map/ppermute | solution.py:558
  9.7 0.7 %copy-start.1 = (f32[3,9]{1,0:T(4,128)S(1)}, f32[3,9]{1,0:T(4,128)}, u32[]{:S(2)}) copy-start(f32[3,9]{1,0:T(4,128)} %refs_1_.3) | copy-start | bytes 328
  10.4 0.7 %copy-start.2 = (f32[3,9]{1,0:T(4,128)S(1)}, f32[3,9]{1,0:T(4,128)}, u32[]{:S(2)}) copy-start(f32[3,9]{1,0:T(4,128)} %refs_2_.1) | copy-start | bytes 328
  12.9 6.1 %collective-permute-start.7 = (bf16[192,128]{1,0:T(8,128)(2,1)S(1)}, bf16[192,128]{1,0:T(8,128)(2,1)S(1)}, u32[]{:S(2)}, u32[]{:S(2)}) collective-permute-start(bf16[192,128]{1,0:T(8,128)(2,1)S(1)} %get-tuple-element.34), channel_id=1, source_target_pairs={{1,2},{2,1},{0,3},{3,0},{5,6},{6,5},{4,7},{7,4},{9,10},{10,9},{8,1... | collective-permute-start | bytes 147464 | tf_op jit(solution)/shard_map/ppermute | solution.py:531
  17.0 8.9 %collective-permute-start.2 = (bf16[96,2048]{1,0:T(8,128)(2,1)S(1)}, bf16[96,2048]{1,0:T(8,128)(2,1)S(1)}, u32[]{:S(2)}, u32[]{:S(2)}) collective-permute-start(bf16[96,2048]{1,0:T(8,128)(2,1)S(1)} %get-tuple-element.29), channel_id=1, source_target_pairs={{0,4},{4,0},{1,5},{5,1},{2,6},{6,2},{3,7},{7,3},{8,12},{12,8},{9,1... | collective-permute-start | bytes 1179656 | tf_op jit(solution)/shard_map/ppermute | solution.py:531
  17.0 5.9 %collective-permute-start.6 = (bf16[192,128]{1,0:T(8,128)(2,1)S(1)}, bf16[192,128]{1,0:T(8,128)(2,1)S(1)}, u32[]{:S(2)}, u32[]{:S(2)}) collective-permute-start(bf16[192,128]{1,0:T(8,128)(2,1)S(1)} %get-tuple-element.33), channel_id=1, source_target_pairs={{0,1},{1,0},{2,3},{3,2},{4,5},{5,4},{6,7},{7,6},{8,9},{9,8},{10,11... | collective-permute-start | bytes 147464 | tf_op jit(solution)/shard_map/ppermute | solution.py:531
  19.0 5.6 %collective-permute-start.9 = (bf16[32,128]{1,0:T(8,128)(2,1)S(1)}, bf16[32,128]{1,0:T(8,128)(2,1)S(1)}, u32[]{:S(2)}, u32[]{:S(2)}) collective-permute-start(bf16[32,128]{1,0:T(8,128)(2,1)S(1)} %get-tuple-element.38), channel_id=1, source_target_pairs={{0,2},{1,3},{2,0},{3,1},{4,6},{5,7},{6,4},{7,5},{8,10},{9,11},{10,... | collective-permute-start | bytes 24584 | tf_op jit(solution)/shard_map/ppermute | solution.py:564
  24.0 1.9 %collective-permute-start.8 = (bf16[64,2048]{1,0:T(8,128)(2,1)S(1)}, bf16[64,2048]{1,0:T(8,128)(2,1)S(1)}, u32[]{:S(2)}, u32[]{:S(2)}) collective-permute-start(bf16[64,2048]{1,0:T(8,128)(2,1)S(1)} %get-tuple-element.37), channel_id=1, source_target_pairs={{0,4},{4,0},{1,5},{5,1},{2,6},{6,2},{3,7},{7,3},{8,12},{12,8},{9,1... | collective-permute-start | bytes 786440 | tf_op jit(solution)/shard_map/ppermute | solution.py:531
  24.6 1.3 %collective-permute-start.10 = (bf16[1,4,32,128]{3,2,1,0:T(8,128)(2,1)S(1)}, bf16[1,4,32,128]{3,2,1,0:T(8,128)(2,1)S(1)}, u32[]{:S(2)}, u32[]{:S(2)}) collective-permute-start(bf16[1,4,32,128]{3,2,1,0:T(8,128)(2,1)S(1)} %get-tuple-element.39), channel_id=1, source_target_pairs={{0,4},{4,0},{1,5},{5,1},{2,6},{6,2},{3,7},{7,3},{8,12},{12,8},{9,1... | collective-permute-start | bytes 98312 | tf_op jit(solution)/shard_map/ppermute | solution.py:490
  24.7 1.0 %copy-start = (bf16[2,2,16,2048]{3,2,1,0:T(8,128)(2,1)S(1)}, bf16[2,2,16,2048]{3,2,1,0:T(8,128)(2,1)}, u32[]{:S(2)}) copy-start(bf16[2,2,16,2048]{3,2,1,0:T(8,128)(2,1)} %param.7) | copy-start | bytes 786436

commit v8 on v7

--- a/solution.py
+++ b/solution.py
@@ -82,6 +82,7 @@
         self.ride = self.nx == 4 and self.nz == 4 and self.tile == self.V * E
         self.edge = self.rows + 2 * self.avg + (self.tz * self.V if self.ride else 0)
         self.ypack = len(self.kz) * (self.zyf + self.zyc)
+        self.front = 2 if self.V % 4 == 0 else 1
         self.chunks = 4 if self.V % 4 == 0 else 1
         self.corner = len(self.kx) * self.face + (self.tz * self.V if self.ride else 0)
 
@@ -124,12 +125,12 @@
     faces, edges, refs = refs[:m], refs[m : m + n], refs[m + n :]
     piece, weights, held, fine, coarse, found, sems = refs
     taps = [
-        pltpu.make_async_copy(fine_far, fine, sems.at[s.chunks]),
-        pltpu.make_async_copy(coarse_far, coarse, sems.at[s.chunks + 1]),
+        pltpu.make_async_copy(fine_far, fine, sems.at[s.front]),
+        pltpu.make_async_copy(coarse_far, coarse, sems.at[s.front + 1]),
     ]
-    chunk = s.V // s.chunks
+    chunk = s.V // s.front
     copies = []
-    for i in range(s.chunks):
+    for i in range(s.front):
         at = pl.ds(i * chunk, chunk)
         copies.append(pltpu.make_async_copy(field.at[at], held.at[at], sems.at[i]))
     for each in taps + copies:
@@ -543,10 +544,7 @@
         far,
         outs,
         scratch=[pltpu.SMEM(a.shape, a.dtype) for a in taps]
-        + [
-            pltpu.VMEM((s.rows, max(n, 1) * s.V * E), F32),
-            pltpu.SemaphoreType.DMA((s.chunks + 2,)),
-        ],
+        + [pltpu.VMEM((s.rows, max(n, 1) * s.V * E), F32), pltpu.SemaphoreType.DMA((s.front + 2,))],
         far=(0, 1, 2),
     )
     faces, edges = faces[:m], faces[m:]

time: 28 us -> 28 us (level)
  no operation moved by 1% of the time
where the time goes in v8:
time: 28 us; the launch traced here: 27.8 us
  starting transfers between devices  16 us (57%)
  Pallas kernels  9.18 us (33%)
  local copies, waits for them, and re-layouts  1.37 us (5%)
  waiting for transfers between devices  1.11 us (4%)
    ppermute x8, starting transfers between devices, swap(): moved.append(lax.ppermute(a, axis, swaps(count, kind, ring)))  11.4 us
    pallas_call x8, Pallas kernels, run(): return list(call(*arrays))  9.18 us
    ppermute x1, starting transfers between devices, shards(): across = lax.ppermute(known, 'gz', [(i, i ^ 2) for i in range(s.nz)])  3.94 us
    unnamed x6, local copies, waits for them, and re-layouts  1.37 us
    ppermute x1, starting transfers between devices, shards(): across = lax.ppermute(piece, 'gx', [(i, i ^ 2) for i in range(s.nx)])  0.57 us
  transfers between devices with their start and end apart: 11, of which 2 were waited for; matrix products, arithmetic and copies ran while one was open for 0% of the time, Pallas kernels for 18%

profile of v8, /device:TPU:0, one launch (start us, length us, event | category | flops | bytes accessed | tf_op | source)
XLA Modules:
  0.0 27.8 jit_solution(13397948231215957304)
XLA Ops:
  0.0 2.4 %shard_map.47 = (bf16[1152,128]{1,0:T(8,128)(2,1)S(1)}, bf16[1152,128]{1,0:T(8,128)(2,1)S(1)}, bf16[320,128]{1,0:T(8,128)(2,1)S(1)}, bf16[320,128]{1,0:T(8,128)(...) custom-call(bf16[16,16,16,128]{3,2,1,0:T(8,128)(2,1)} %refs_0_.3, ...), custom_call_target="tpu_custom_call" | custom-call | bytes 1048576 | tf_op jit(solution)/shard_map/pallas_call | solution.py:527
  2.4 3.0 %collective-permute-start = (bf16[320,128]{1,0:T(8,128)(2,1)S(1)}, bf16[320,128]{1,0:T(8,128)(2,1)S(1)}, u32[]{:S(2)}, u32[]{:S(2)}) collective-permute-start(bf16[320,128]{1,0:T(8,128)(2,1)S(1)} %get-tuple-element.25), channel_id=1, source_target_pairs={{0,8},{8,0},{16,24},{24,16},{1,9},{9,1},{17,25},{25,17},{2,10},{10... | collective-permute-start | bytes 245768 | tf_op jit(solution)/shard_map/ppermute | solution.py:532
  5.4 1.5 %collective-permute-start.1 = (bf16[320,128]{1,0:T(8,128)(2,1)S(1)}, bf16[320,128]{1,0:T(8,128)(2,1)S(1)}, u32[]{:S(2)}, u32[]{:S(2)}) collective-permute-start(bf16[320,128]{1,0:T(8,128)(2,1)S(1)} %get-tuple-element.26), channel_id=1, source_target_pairs={{8,16},{16,8},{0,24},{24,0},{9,17},{17,9},{1,25},{25,1},{10,18},{1... | collective-permute-start | bytes 245768 | tf_op jit(solution)/shard_map/ppermute | solution.py:532
  6.9 1.6 %collective-permute-start.3 = (bf16[1152,128]{1,0:T(8,128)(2,1)S(1)}, bf16[1152,128]{1,0:T(8,128)(2,1)S(1)}, u32[]{:S(2)}, u32[]{:S(2)}) collective-permute-start(bf16[1152,128]{1,0:T(8,128)(2,1)S(1)} %get-tuple-element.30), channel_id=1, source_target_pairs={{0,1},{1,0},{2,3},{3,2},{4,5},{5,4},{6,7},{7,6},{8,9},{9,8},{10,11... | collective-permute-start | bytes 884744 | tf_op jit(solution)/shard_map/ppermute | solution.py:532
  8.5 0.7 %collective-permute-start.4 = (bf16[1152,128]{1,0:T(8,128)(2,1)S(1)}, bf16[1152,128]{1,0:T(8,128)(2,1)S(1)}, u32[]{:S(2)}, u32[]{:S(2)}) collective-permute-start(bf16[1152,128]{1,0:T(8,128)(2,1)S(1)} %get-tuple-element.31), channel_id=1, source_target_pairs={{1,2},{2,1},{5,6},{6,5},{9,10},{10,9},{13,14},{14,13},{17,18},{18,... | collective-permute-start | bytes 884744 | tf_op jit(solution)/shard_map/ppermute | solution.py:532
  9.1 0.6 %collective-permute-start.5 = (bf16[32,128]{1,0:T(8,128)(2,1)S(1)}, bf16[32,128]{1,0:T(8,128)(2,1)S(1)}, u32[]{:S(2)}, u32[]{:S(2)}) collective-permute-start(bf16[32,128]{1,0:T(8,128)(2,1)S(1)} %get-tuple-element.32.refs_2_), channel_id=1, source_target_pairs={{0,16},{8,24},{16,0},{24,8},{1,17},{9,25},{17,1},{25,9},{2,18},{10... | collective-permute-start | bytes 24584 | tf_op jit(solution)/shard_map/ppermute | solution.py:556
  9.7 0.0 copy-start.1
  9.7 0.7 %copy-done.1 = f32[3,9]{1,0:T(4,128)S(1)} copy-done((f32[3,9]{1,0:T(4,128)S(1)}, f32[3,9]{1,0:T(4,128)}, u32[]{:S(2)}) %copy-start.1) | copy-done | bytes 132
  10.4 0.0 copy-start.2
  10.4 0.7 %copy-done.2 = f32[3,9]{1,0:T(4,128)S(1)} copy-done((f32[3,9]{1,0:T(4,128)S(1)}, f32[3,9]{1,0:T(4,128)}, u32[]{:S(2)}) %copy-start.2) | copy-done | bytes 132
  11.1 1.2 %shard_map.46 = (bf16[256,768]{1,0:T(8,128)(2,1)S(1)}, bf16[256,736]{1,0:T(8,128)(2,1)S(1)}) custom-call(f32[3,9]{1,0:T(4,128)S(1)} %copy-done.1, f32[3,9]{1,0:T(4,128)S(1)} %copy-done.2), custom_call_target="tpu_custom_call" | custom-call | flops 268435456 | bytes 1048576 | tf_op jit(solution)/shard_map/pallas_call | solution.py:527
  12.3 0.5 %collective-permute-done.5.refs_3_ = bf16[32,128]{1,0:T(8,128)(2,1)S(1)} collective-permute-done((bf16[32,128]{1,0:T(8,128)(2,1)S(1)}, bf16[32,128]{1,0:T(8,128)(2,1)S(1)}, u32[]{:S(2)}, u32[]{:S(2)}) %collective-permute-start.5) | collective-permute-done | bytes 8224 | tf_op jit(solution)/shard_map/ppermute | solution.py:556
  12.9 0.0 collective-permute-done.refs_2_.refs_0_
  12.9 0.0 collective-permute-done.1.refs_3_.refs_1_
  12.9 2.5 %collective-permute-start.7 = (bf16[192,128]{1,0:T(8,128)(2,1)S(1)}, bf16[192,128]{1,0:T(8,128)(2,1)S(1)}, u32[]{:S(2)}, u32[]{:S(2)}) collective-permute-start(bf16[192,128]{1,0:T(8,128)(2,1)S(1)} %get-tuple-element.34), channel_id=1, source_target_pairs={{1,2},{2,1},{0,3},{3,0},{5,6},{6,5},{4,7},{7,4},{9,10},{10,9},{8,1... | collective-permute-start | bytes 147464 | tf_op jit(solution)/shard_map/ppermute | solution.py:532
  15.4 1.5 %shard_map.48 = (bf16[512,2048]{1,0:T(8,128)(2,1)S(1)}, bf16[96,2048]{1,0:T(8,128)(2,1)S(1)}) custom-call(bf16[3,256,384]{2,1,0:T(8,128)(2,1)S(1)} %get-tuple-element.23.refs_0_, bf16[16,16,16,128]{3,2,1,0:T(8,128)(2,1)S(1)} %get-tuple-element.24.refs_1_, bf16[320,128]{1,0:T(8,128)(2,1)S(1)} %collective-permute-done.refs_2_.refs_0_, ...), custom_call_target="tpu_custom_call" | custom-call | flops 536870912 | bytes 1048576 | tf_op jit(solution)/shard_map/pallas_call | solution.py:527
  16.9 0.1 collective-permute-start.2
  17.0 2.0 %collective-permute-start.6 = (bf16[192,128]{1,0:T(8,128)(2,1)S(1)}, bf16[192,128]{1,0:T(8,128)(2,1)S(1)}, u32[]{:S(2)}, u32[]{:S(2)}) collective-permute-start(bf16[192,128]{1,0:T(8,128)(2,1)S(1)} %get-tuple-element.33), channel_id=1, source_target_pairs={{0,1},{1,0},{2,3},{3,2},{4,5},{5,4},{6,7},{7,6},{8,9},{9,8},{10,11... | collective-permute-start | bytes 147464 | tf_op jit(solution)/shard_map/ppermute | solution.py:532
  19.0 0.0 collective-permute-done.7.refs_4_
  19.0 3.9 %collective-permute-start.9 = (bf16[32,128]{1,0:T(8,128)(2,1)S(1)}, bf16[32,128]{1,0:T(8,128)(2,1)S(1)}, u32[]{:S(2)}, u32[]{:S(2)}) collective-permute-start(bf16[32,128]{1,0:T(8,128)(2,1)S(1)} %get-tuple-element.38), channel_id=1, source_target_pairs={{0,2},{1,3},{2,0},{3,1},{4,6},{5,7},{6,4},{7,5},{8,10},{9,11},{10,... | collective-permute-start | bytes 24584 | tf_op jit(solution)/shard_map/ppermute | solution.py:562
  23.0 0.0 collective-permute-done.6.refs_3_
  23.0 0.0 collective-permute-done.3.refs_1_
  23.0 0.0 collective-permute-done.4.refs_2_
  23.0 1.0 %shard_map.51 = (bf16[144,2048]{1,0:T(8,128)(2,1)S(1)}, bf16[144,2048]{1,0:T(8,128)(2,1)S(1)}, bf16[64,2048]{1,0:T(8,128)(2,1)S(1)}) custom-call(bf16[3,256,384]{2,1,0:T(8,128)(2,1)S(1)} %get-tuple-element.23.refs_0_, bf16[1152,128]{1,0:T(8,128)(2,1)S(1)} %collective-permute-done.3.refs_1_, bf16[1152,128]{1,0:T(8,128)(2,1)S(1)} %collective-permute-done.4.refs_2_, ...), custom_call_target="tpu_custom_call" | custom-call | bytes 1048576 | tf_op jit(solution)/shard_map/pallas_call | solution.py:527
  24.0 0.1 collective-permute-start.8
  24.0 0.5 %collective-permute-done.9 = bf16[32,128]{1,0:T(8,128)(2,1)S(1)} collective-permute-done((bf16[32,128]{1,0:T(8,128)(2,1)S(1)}, bf16[32,128]{1,0:T(8,128)(2,1)S(1)}, u32[]{:S(2)}, u32[]{:S(2)}) %collective-permute-start.9) | collective-permute-done | bytes 8224 | tf_op jit(solution)/shard_map/ppermute | solution.py:562
  24.6 0.1 collective-permute-start.10
  24.7 0.0 copy-start
  24.7 1.0 %shard_map.49.refs_0_ = f32[256,2048]{1,0:T(8,128)S(1)} custom-call(bf16[256,768]{1,0:T(8,128)(2,1)S(1)} %get-tuple-element.22.refs_0_, bf16[512,2048]{1,0:T(8,128)(2,1)S(1)} %get-tuple-element.27.refs_1_), custom_call_target="tpu_custom_call" | custom-call | flops 536870912 | bytes 1048576 | tf_op jit(solution)/shard_map/pallas_call | solution.py:527
  25.7 0.0 copy-done
  25.7 0.2 shard_map.52.refs_6_
  25.9 0.0 collective-permute-done.10
  25.9 0.0 collective-permute-done.2.refs_2_
  25.9 0.0 collective-permute-done.8.refs_5_
  25.9 1.9 %shard_map.53 = bf16[16,16,16,128]{3,2,1,0:T(8,128)(2,1)} custom-call(f32[256,2048]{1,0:T(8,128)S(1)} %shard_map.49.refs_0_, bf16[256,736]{1,0:T(8,128)(2,1)S(1)} %get-tuple-element.28.refs_1_, bf16[96,2048]{1,0:T(8,128)(2,1)S(1)} %collective-permute-done.2.refs_2_, bf16[144,2048]{1,0:T(8,128)(2,1)S(1)} %get-tuple-element.35.refs_3_, ...), custom_call_target="tpu_custom_call" | custom-call | bytes 1048576 | tf_op jit(solution)/shard_map/pallas_call | solution.py:527
  (5 shorter events, 0.0 us)
Async XLA Ops:
  2.4 10.5 %collective-permute-start = (bf16[320,128]{1,0:T(8,128)(2,1)S(1)}, bf16[320,128]{1,0:T(8,128)(2,1)S(1)}, u32[]{:S(2)}, u32[]{:S(2)}) collective-permute-start(bf16[320,128]{1,0:T(8,128)(2,1)S(1)} %get-tuple-element.25), channel_id=1, source_target_pairs={{0,8},{8,0},{16,24},{24,16},{1,9},{9,1},{17,25},{25,17},{2,10},{10... | collective-permute-start | bytes 245768 | tf_op jit(solution)/shard_map/ppermute | solution.py:532
  5.4 7.5 %collective-permute-start.1 = (bf16[320,128]{1,0:T(8,128)(2,1)S(1)}, bf16[320,128]{1,0:T(8,128)(2,1)S(1)}, u32[]{:S(2)}, u32[]{:S(2)}) collective-permute-start(bf16[320,128]{1,0:T(8,128)(2,1)S(1)} %get-tuple-element.26), channel_id=1, source_target_pairs={{8,16},{16,8},{0,24},{24,0},{9,17},{17,9},{1,25},{25,1},{10,18},{1... | collective-permute-start | bytes 245768 | tf_op jit(solution)/shard_map/ppermute | solution.py:532
  6.9 16.1 %collective-permute-start.3 = (bf16[1152,128]{1,0:T(8,128)(2,1)S(1)}, bf16[1152,128]{1,0:T(8,128)(2,1)S(1)}, u32[]{:S(2)}, u32[]{:S(2)}) collective-permute-start(bf16[1152,128]{1,0:T(8,128)(2,1)S(1)} %get-tuple-element.30), channel_id=1, source_target_pairs={{0,1},{1,0},{2,3},{3,2},{4,5},{5,4},{6,7},{7,6},{8,9},{9,8},{10,11... | collective-permute-start | bytes 884744 | tf_op jit(solution)/shard_map/ppermute | solution.py:532
  8.5 14.5 %collective-permute-start.4 = (bf16[1152,128]{1,0:T(8,128)(2,1)S(1)}, bf16[1152,128]{1,0:T(8,128)(2,1)S(1)}, u32[]{:S(2)}, u32[]{:S(2)}) collective-permute-start(bf16[1152,128]{1,0:T(8,128)(2,1)S(1)} %get-tuple-element.31), channel_id=1, source_target_pairs={{1,2},{2,1},{5,6},{6,5},{9,10},{10,9},{13,14},{14,13},{17,18},{18,... | collective-permute-start | bytes 884744 | tf_op jit(solution)/shard_map/ppermute | solution.py:532
  9.1 3.7 %collective-permute-start.5 = (bf16[32,128]{1,0:T(8,128)(2,1)S(1)}, bf16[32,128]{1,0:T(8,128)(2,1)S(1)}, u32[]{:S(2)}, u32[]{:S(2)}) collective-permute-start(bf16[32,128]{1,0:T(8,128)(2,1)S(1)} %get-tuple-element.32.refs_2_), channel_id=1, source_target_pairs={{0,16},{8,24},{16,0},{24,8},{1,17},{9,25},{17,1},{25,9},{2,18},{10... | collective-permute-start | bytes 24584 | tf_op jit(solution)/shard_map/ppermute | solution.py:556
  9.7 0.7 %copy-start.1 = (f32[3,9]{1,0:T(4,128)S(1)}, f32[3,9]{1,0:T(4,128)}, u32[]{:S(2)}) copy-start(f32[3,9]{1,0:T(4,128)} %refs_1_.3) | copy-start | bytes 328
  10.4 0.7 %copy-start.2 = (f32[3,9]{1,0:T(4,128)S(1)}, f32[3,9]{1,0:T(4,128)}, u32[]{:S(2)}) copy-start(f32[3,9]{1,0:T(4,128)} %refs_2_.1) | copy-start | bytes 328
  12.9 6.1 %collective-permute-start.7 = (bf16[192,128]{1,0:T(8,128)(2,1)S(1)}, bf16[192,128]{1,0:T(8,128)(2,1)S(1)}, u32[]{:S(2)}, u32[]{:S(2)}) collective-permute-start(bf16[192,128]{1,0:T(8,128)(2,1)S(1)} %get-tuple-element.34), channel_id=1, source_target_pairs={{1,2},{2,1},{0,3},{3,0},{5,6},{6,5},{4,7},{7,4},{9,10},{10,9},{8,1... | collective-permute-start | bytes 147464 | tf_op jit(solution)/shard_map/ppermute | solution.py:532
  16.9 8.9 %collective-permute-start.2 = (bf16[96,2048]{1,0:T(8,128)(2,1)S(1)}, bf16[96,2048]{1,0:T(8,128)(2,1)S(1)}, u32[]{:S(2)}, u32[]{:S(2)}) collective-permute-start(bf16[96,2048]{1,0:T(8,128)(2,1)S(1)} %get-tuple-element.29), channel_id=1, source_target_pairs={{0,4},{4,0},{1,5},{5,1},{2,6},{6,2},{3,7},{7,3},{8,12},{12,8},{9,1... | collective-permute-start | bytes 1179656 | tf_op jit(solution)/shard_map/ppermute | solution.py:532
  17.0 5.9 %collective-permute-start.6 = (bf16[192,128]{1,0:T(8,128)(2,1)S(1)}, bf16[192,128]{1,0:T(8,128)(2,1)S(1)}, u32[]{:S(2)}, u32[]{:S(2)}) collective-permute-start(bf16[192,128]{1,0:T(8,128)(2,1)S(1)} %get-tuple-element.33), channel_id=1, source_target_pairs={{0,1},{1,0},{2,3},{3,2},{4,5},{5,4},{6,7},{7,6},{8,9},{9,8},{10,11... | collective-permute-start | bytes 147464 | tf_op jit(solution)/shard_map/ppermute | solution.py:532
  19.0 5.6 %collective-permute-start.9 = (bf16[32,128]{1,0:T(8,128)(2,1)S(1)}, bf16[32,128]{1,0:T(8,128)(2,1)S(1)}, u32[]{:S(2)}, u32[]{:S(2)}) collective-permute-start(bf16[32,128]{1,0:T(8,128)(2,1)S(1)} %get-tuple-element.38), channel_id=1, source_target_pairs={{0,2},{1,3},{2,0},{3,1},{4,6},{5,7},{6,4},{7,5},{8,10},{9,11},{10,... | collective-permute-start | bytes 24584 | tf_op jit(solution)/shard_map/ppermute | solution.py:562
  24.0 1.9 %collective-permute-start.8 = (bf16[64,2048]{1,0:T(8,128)(2,1)S(1)}, bf16[64,2048]{1,0:T(8,128)(2,1)S(1)}, u32[]{:S(2)}, u32[]{:S(2)}) collective-permute-start(bf16[64,2048]{1,0:T(8,128)(2,1)S(1)} %get-tuple-element.37), channel_id=1, source_target_pairs={{0,4},{4,0},{1,5},{5,1},{2,6},{6,2},{3,7},{7,3},{8,12},{12,8},{9,1... | collective-permute-start | bytes 786440 | tf_op jit(solution)/shard_map/ppermute | solution.py:532
  24.6 1.3 %collective-permute-start.10 = (bf16[1,4,32,128]{3,2,1,0:T(8,128)(2,1)S(1)}, bf16[1,4,32,128]{3,2,1,0:T(8,128)(2,1)S(1)}, u32[]{:S(2)}, u32[]{:S(2)}) collective-permute-start(bf16[1,4,32,128]{3,2,1,0:T(8,128)(2,1)S(1)} %get-tuple-element.39), channel_id=1, source_target_pairs={{0,4},{4,0},{1,5},{5,1},{2,6},{6,2},{3,7},{7,3},{8,12},{12,8},{9,1... | collective-permute-start | bytes 98312 | tf_op jit(solution)/shard_map/ppermute | solution.py:491
  24.7 1.0 %copy-start = (bf16[2,2,16,2048]{3,2,1,0:T(8,128)(2,1)S(1)}, bf16[2,2,16,2048]{3,2,1,0:T(8,128)(2,1)}, u32[]{:S(2)}) copy-start(bf16[2,2,16,2048]{3,2,1,0:T(8,128)(2,1)} %param.7) | copy-start | bytes 786436
